TPU v7x, 1024 devices: a whole 8x8x8 slice. The times are simulated.
1024 devices in a mesh: dp: 16 (over z_hi, y), audio: 64 (over z_lo, x, core).
Axes of the slice: x: 8, y: 8, z: 8 (z_hi: 2, z_lo: 4; z = z_hi * 4 + z_lo), core: 2. Of those that a mesh axis runs over, the one named last changes fastest.
Arguments:
- waveform: float32 [16, 112640], P('dp', 'audio'), may hold values from -6 to 6
- lengths: int32 [16], P('dp'), may hold values from 28160 to 112640, as said below
- conv0_weight: float32 [10, 512], replicated, may hold values from -2 to 2
- norm0_gain: float32 [512], replicated, may hold values from 0.5 to 1.5
- norm0_shift: float32 [512], replicated, may hold values from -1.8 to 1.8
- conv1_weight: bfloat16 [3, 512, 512], replicated, may hold values from -0.15625 to 0.15625
- norm1_gain: float32 [512], replicated, may hold values from 0.25 to 1.75
- norm1_shift: float32 [512], replicated, may hold values from -1.8 to 1.8
- cotangent: bfloat16 [16, 11264, 512], P('dp', 'audio'), may hold values from -0.013671875 to 0.013671875
Outputs:
- features: bfloat16 [16, 11264, 512], P('dp', 'audio')
- conv1_grad: float32 [786432], P(('dp', 'audio'))
- small_grads: float32 [14, 512], replicated
Inputs may be any that keep to these rules, and one draw needn't show every extreme that they name: `lengths`: window 0 is complete (112640 valid samples); each other window is complete or holds a valid prefix.
All inputs are finite; a program needn't handle non-finite values.
Results may differ from a plain program's by a relative error of at most 0.0055.
Values sent between devices are 32-bit elements; how exact they have to be, the bound alone decides.
No kernel may reach another device: no remote copies, remote signals or barrier semaphores. Data moves between devices by JAX's collectives and lax.ppermute only.
A program may use at most 32 MiB of HBM per device.

v0:
```python
import jax
import jax.numpy as jnp
from jax import lax
from jax.sharding import PartitionSpec as P


def shifted(block, axis, distance):
    devices = range(lax.axis_size(axis))
    route = [(i - distance, i) for i in devices if i - distance in devices]
    return lax.ppermute(block, axis, route)


def norm_gelu(pre_act, gain_vec, shift_vec):
    average = jnp.mean(pre_act, -1, keepdims=True)
    centred = pre_act - average
    variance = jnp.mean(centred * centred, -1, keepdims=True)
    return jax.nn.gelu(
        centred * lax.rsqrt(variance + 1e-05) * gain_vec + shift_vec, approximate=False
    )


def encoder_step(
    extended,
    valid_mask,
    cot_float,
    conv0_weight,
    norm0_gain,
    norm0_shift,
    conv1_weight,
    norm1_gain,
    norm1_shift,
):
    count_rows = extended.shape[0]
    chans = conv1_weight.shape[2]
    rows_first = extended.shape[1] // 5
    first_frames = rows_first - 1
    frames_dev = (extended.shape[1] - 10) // 10
    blocks = extended.reshape(count_rows, rows_first, 5)
    patches_first = jnp.concatenate([blocks[:, :first_frames], blocks[:, 1:]], 2).reshape(
        count_rows * first_frames, 10
    )
    pre_first = jnp.dot(
        patches_first,
        conv0_weight,
        precision=lax.Precision.HIGHEST,
        preferred_element_type=jnp.float32,
    ).reshape(count_rows, first_frames, chans)
    act_float, back_first = jax.vjp(norm_gelu, pre_first, norm0_gain, norm0_shift)
    act_first = act_float.astype(jnp.bfloat16)
    frame_pairs = act_first[:, : 2 * frames_dev].reshape(count_rows, frames_dev, 2 * chans)
    next_frame = act_first[:, 2::2]
    patches_second = jnp.concatenate([frame_pairs, next_frame], 2).reshape(
        count_rows * frames_dev, 3 * chans
    )
    kernel_mat = conv1_weight.reshape(3 * chans, chans)
    pre_second = jnp.dot(patches_second, kernel_mat, preferred_element_type=jnp.float32).reshape(
        count_rows, frames_dev, chans
    )

    def second_norm(pre_act, gain_vec, shift_vec):
        return norm_gelu(pre_act, gain_vec, shift_vec) * valid_mask[:, :, None]

    feat_float, back_second = jax.vjp(second_norm, pre_second, norm1_gain, norm1_shift)
    d_pre_second, d_gain_second, d_shift_second = back_second(cot_float)
    d_pre_second = d_pre_second.astype(jnp.bfloat16).reshape(count_rows * frames_dev, chans)
    grad_kernel = lax.dot_general(
        patches_second, d_pre_second, (((0,), (0,)), ((), ())), preferred_element_type=jnp.float32
    )
    d_patch = lax.dot_general(
        d_pre_second, kernel_mat, (((1,), (1,)), ((), ())), preferred_element_type=jnp.float32
    ).reshape(count_rows, frames_dev, 3, chans)
    leading = d_patch[:, :, :2].reshape(count_rows, 2 * frames_dev, chans)
    d_act_first = jnp.concatenate([leading, jnp.zeros((count_rows, 1, chans), leading.dtype)], 1)
    d_act_first = d_act_first.at[:, 2::2].add(d_patch[:, :, 2])
    d_pre_first, d_gain_first, d_shift_first = back_first(d_act_first)
    grad_first = lax.dot_general(
        patches_first,
        d_pre_first.reshape(count_rows * first_frames, chans),
        (((0,), (0,)), ((), ())),
        precision=lax.Precision.HIGHEST,
        preferred_element_type=jnp.float32,
    )
    small_terms = jnp.concatenate(
        [
            grad_first,
            d_gain_first[None],
            d_shift_first[None],
            d_gain_second[None],
            d_shift_second[None],
        ],
        0,
    )
    return (feat_float.astype(jnp.bfloat16), grad_kernel, small_terms)


def shards(
    waveform,
    lengths,
    conv0_weight,
    norm0_gain,
    norm0_shift,
    conv1_weight,
    norm1_gain,
    norm1_shift,
    cotangent,
):
    position = lax.axis_index("audio")
    samples_dev = waveform.shape[1]
    sample_pos = position * samples_dev + jnp.arange(samples_dev, dtype=jnp.int32)
    cleaned = waveform * (sample_pos[None, :] < lengths[:, None]).astype(jnp.float32)
    rim_samples = shifted(cleaned[:, :10], "audio", -1)
    extended = jnp.concatenate([cleaned, rim_samples], 1)
    frames_dev = samples_dev // 10
    frame_pos = position * frames_dev + jnp.arange(frames_dev, dtype=jnp.int32)
    valid_mask = (frame_pos[None, :] < (lengths // 10)[:, None]).astype(jnp.float32)
    features, grad_kernel, small_terms = encoder_step(
        extended,
        valid_mask,
        cotangent.astype(jnp.float32),
        conv0_weight,
        norm0_gain,
        norm0_shift,
        conv1_weight,
        norm1_gain,
        norm1_shift,
    )
    flat_grad = grad_kernel.reshape(-1)
    batch_share = lax.psum_scatter(flat_grad, "dp", scatter_dimension=0, tiled=True)
    conv1_grad = lax.psum_scatter(batch_share, "audio", scatter_dimension=0, tiled=True)
    small_grads = lax.psum(small_terms, ("dp", "audio"))
    return (features, conv1_grad, small_grads)


def solution(mesh):
    in_specs = (P("dp", "audio"), P("dp"), P(), P(), P(), P(), P(), P(), P("dp", "audio", None))
    out_specs = (P("dp", "audio", None), P(("dp", "audio")), P())
    return jax.shard_map(shards, mesh=mesh, in_specs=in_specs, out_specs=out_specs, check_vma=False)
```

profile of v0, /device:TPU:1, one launch (start us, length us, event | category | flops | bytes accessed | tf_op | source)
XLA Modules:
  0.0 760.4 jit_solution(8036835480453917845)
XLA Ops:
  8.0 0.7 compare_select_fusion
  8.7 16.1 %collective-permute-start = (f32[1,10]{1,0:T(1,128)S(1)}, f32[1,10]{1,0:T(1,128)S(1)}, u32[]{:S(2)}, u32[]{:S(2)}) collective-permute-start(f32[1,10]{1,0:T(1,128)S(1)} %slice.28), channel_id=1, source_target_pairs={{1,0},{2,1},{3,2},{4,3},{5,4},{6,5},{7,6},{8,7},{9,8},{10,9},{11,1... | collective-permute-start | bytes 128 | tf_op jit(solution)/shard_map/ppermute | solution.py:10
  24.8 0.8 collective-permute-done
  25.7 0.2 reshape.363
  26.2 1.6 fusion.47
  27.8 0.2 multiply_reduce_fusion
  28.1 2.7 fusion.11
  30.8 1.5 slice.25
  32.3 0.1 reshape.365
  32.5 1.6 fusion.48
  34.1 0.2 multiply_reduce_fusion.1
  34.3 1.9 fusion.15
  36.2 0.3 fusion.42
  36.5 0.6 convolution_bitcast_fusion
  37.1 2.5 copy.19
  39.7 1.3 dynamic-slice.2
  41.0 1.3 dynamic-slice
  43.6 0.7 convolution_bitcast_fusion.1
  44.3 1.0 copy-done.1
  45.3 0.7 copy.16
  46.1 1.0 pad_bitcast_fusion
  47.1 4.1 scatter_custom_fusion
  51.2 1.6 fusion.41
  52.9 0.2 fusion.4
  53.1 0.4 fusion.1
  53.6 0.7 fusion.2
  54.3 138.8 %psum.7 = f32[14,512]{1,0:T(8,128)} all-reduce(f32[14,512]{1,0:T(8,128)S(1)} %concatenate.19), channel_id=1, replica_groups=mesh['dp'=16,'audio'=64] {'dp','audio'}, use_global_device_ids=true, to_apply=%region_15.16 | all-reduce | flops 7168 | bytes 57344 | tf_op jit(solution)/shard_map/psum | solution.py:130
  193.1 63.1 %all-reduce.6.cloned.1.call-done = f32[786432]{0:T(1024)} async-done(((f32[786432]{0:T(1024)}), f32[786432]{0:T(1024)}) %all-reduce.6.cloned.1.call-update) | async-done | bytes 3145744
  256.3 1.6 dynamic-slice.1
  257.9 0.8 fusion.28
  258.8 493.5 %all-reduce.8.cloned.1.call-done = f32[49152]{0:T(1024)} async-done(((f32[49152]{0:T(1024)}), f32[49152]{0:T(1024)}) %all-reduce.8.cloned.1.call-update) | async-done | bytes 196624
  752.2 1.4 dynamic-slice.3
  (43 shorter events, 0.8 us)
Async XLA Ops:
  7.2 25.3 %copy-start = (bf16[3,512,512]{2,1,0:T(8,128)(2,1)S(1)}, bf16[3,512,512]{2,1,0:T(8,128)(2,1)}, u32[]{:S(2)}) copy-start(bf16[3,512,512]{2,1,0:T(8,128)(2,1)} %param.14) | copy-start | bytes 4718596
  7.2 20.9 %copy-start.6 = (f32[512]{0:T(512)S(1)}, f32[512]{0:T(512)}, u32[]{:S(2)}) copy-start(f32[512]{0:T(512)} %param.12) | copy-start | bytes 6148
  7.2 20.9 %copy-start.8 = (f32[512]{0:T(512)S(1)}, f32[512]{0:T(512)}, u32[]{:S(2)}) copy-start(f32[512]{0:T(512)} %param.13) | copy-start | bytes 6148
  7.2 249.1 %all-reduce.6.cloned.1.call-start = ((), (), s32[]{:S(2)}) async-start(), calls=%async_computation | async-start | bytes 6291456
  8.7 16.9 %collective-permute-start = (f32[1,10]{1,0:T(1,128)S(1)}, f32[1,10]{1,0:T(1,128)S(1)}, u32[]{:S(2)}, u32[]{:S(2)}) collective-permute-start(f32[1,10]{1,0:T(1,128)S(1)} %slice.28), channel_id=1, source_target_pairs={{1,0},{2,1},{3,2},{4,3},{5,4},{6,5},{7,6},{8,7},{9,8},{10,9},{11,1... | collective-permute-start | bytes 128 | tf_op jit(solution)/shard_map/ppermute | solution.py:10
  32.4 1.8 copy-start.5
  32.5 1.8 copy-start.7
  32.5 1.8 copy-start.9
  34.0 2.4 copy-start.4
  39.7 712.6 %all-reduce.8.cloned.1.call-start = ((), (), s32[]{:S(2)}) async-start(), calls=%async_computation.1 | async-start | bytes 393216
  44.3 1.0 copy-start.1
  46.1 5.1 copy-start.2
  53.1 204.8 %copy-start.3 = (f32[176,512]{1,0:T(8,128)S(1)}, f32[176,512]{1,0:T(8,128)}, u32[]{:S(2)}) copy-start(f32[176,512]{1,0:T(8,128)} %get-tuple-element.13) | copy-start | bytes 1081348
Sparse Core Ops, SparseCore 0:
  39.8 216.4 all-reduce.5
  259.8 492.4 all-reduce.7
where the time goes:
time: 762 us; the launch traced here: 760 us
  waiting for transfers between devices  557 us (73%)
  blocking collectives  139 us (18%)
  between operations  16.4 us (2%)
  starting transfers between devices  16.1 us (2%)
  other arithmetic  13.4 us (2%)
  local copies, waits for them, and re-layouts  13.1 us (2%)
    unnamed x4, waiting for transfers between devices  557 us
    psum x1, blocking collectives, shards(): small_grads = lax.psum(small_terms, ('dp', 'audio'))  139 us
    ppermute x1, starting transfers between devices, shifted(): return lax.ppermute(block, axis, route)  16.1 us
  transfers between devices with their start and end apart: 3, of which 3 were waited for; matrix products, arithmetic and copies ran while one was open for 2% of the time, Pallas kernels for 0%

commit v1 on v0

v1 whole, which is shorter than its diff:
```python
import functools

import jax
import jax.numpy as jnp
import numpy as np
from jax import lax
from jax.experimental import pallas as pl
from jax.experimental.pallas import tpu as pltpu
from jax.sharding import Mesh
from jax.sharding import PartitionSpec as P

SHAPE = (2, 8, 4, 8, 2)
AXES = ("zh", "y", "zl", "x", "core")
EPS = 1e-05
BF16, F32 = jnp.bfloat16, jnp.float32

LEVELS = (
    ((2, "y", 1), (0, "z", 1), (3, "y", 2), (1, "z", 2), (4, "y", 4), (5, "z", 4)),
    ((0, "z", 1), (2, "y", 1), (1, "z", 2), (3, "y", 2), (5, "z", 4), (4, "y", 4)),
)


def partners(step):
    route = []
    for i in range(int(np.prod(SHAPE))):
        zh, y, zl, x, core = (int(v) for v in np.unravel_index(i, SHAPE))
        at = {"z": zh * 4 + zl, "y": y, "x": x, "core": core}
        axis, distance = step(core)
        at[axis] ^= distance
        there = (at["z"] // 4, at["y"], at["z"] % 4, at["x"], at["core"])
        route.append((i, int(np.ravel_multi_index(there, SHAPE))))
    return route


def exchange(value, step):
    return lax.ppermute(value, AXES, partners(step))


def normal_cdf(v):
    return 0.5 + 0.5 * lax.erf(v * np.float32(0.5**0.5))


def normal_pdf(v):
    return jnp.exp(v * v * np.float32(-0.5)) * np.float32((2 * np.pi) ** -0.5)


def split_patches(x3_ref, rim_ref, odd_rows, even_last):
    value = x3_ref[...]
    row = lax.broadcasted_iota(jnp.int32, value.shape, 0)
    lane = lax.broadcasted_iota(jnp.int32, value.shape, 1)
    value = jnp.where(row == odd_rows - 1, value + rim_ref[0:1, :], value)
    value = jnp.where(row == even_last, value + rim_ref[1:2, :], value)
    high = value.astype(BF16).astype(F32)
    return jnp.where(lane < 20, high, value - high).astype(BF16)


def forward_kernel(
    frames,
    chunk,
    tab_ref,
    meta_ref,
    x3_ref,
    rim_ref,
    w3_ref,
    gain0_ref,
    shift0_ref,
    w1_ref,
    gain1_ref,
    shift1_ref,
    cot_ref,
    feat_ref,
    keep_ref,
    send_ref,
    d_ref,
    xhat_ref,
    slope_ref,
    rstd_ref,
    norm1_ref,
    pre0_ref,
    even_ref,
    patch_ref,
    pre1_ref,
    half_ref,
):
    chans = w1_ref.shape[1]
    rows = x3_ref.shape[0]
    xs = split_patches(x3_ref, rim_ref, frames, 2 * frames)
    w3 = w3_ref[...]
    w3 = w3 - jnp.mean(w3, -1, keepdims=True)
    high = w3.astype(BF16).astype(F32)
    tap = lax.broadcasted_iota(jnp.int32, w3.shape, 0)
    ws = jnp.where((tap >= 10) & (tap < 20), w3 - high, high).astype(BF16)
    pre0_ref[...] = jnp.dot(xs, ws, preferred_element_type=F32)
    gain0 = jnp.broadcast_to(gain0_ref[...], (chunk, chans))
    shift0 = jnp.broadcast_to(shift0_ref[...], (chunk, chans))
    for at in range(0, rows, chunk):
        centred = pre0_ref[at : at + chunk]
        rstd = lax.rsqrt(jnp.mean(centred * centred, -1, keepdims=True) + EPS)
        xhat = centred * rstd
        v = xhat * gain0 + shift0
        cdf = normal_cdf(v)
        xhat_ref[at : at + chunk] = xhat
        slope_ref[at : at + chunk] = cdf + v * normal_pdf(v)
        rstd_ref[at : at + chunk] = jnp.broadcast_to(rstd, (chunk, 128))
        act = v * cdf
        if at < frames:
            patch_ref[at : at + chunk, chans : 2 * chans] = act.astype(BF16)
        else:
            even_ref[at - frames : at - frames + chunk] = act
    for at in range(0, frames, chunk):
        patch_ref[at : at + chunk, :chans] = even_ref[at : at + chunk].astype(BF16)
        patch_ref[at : at + chunk, 2 * chans :] = even_ref[at + 1 : at + 1 + chunk].astype(BF16)
    pre1_ref[...] = jnp.dot(patch_ref[...], w1_ref[...], preferred_element_type=F32)
    gain1 = jnp.broadcast_to(gain1_ref[...], (chunk, chans))
    shift1 = jnp.broadcast_to(shift1_ref[...], (chunk, chans))
    sum_gain = jnp.zeros((chunk, chans), F32)
    sum_shift = jnp.zeros((chunk, chans), F32)
    half = chans // 2
    for at in range(0, frames, chunk):
        pre = pre1_ref[at : at + chunk]
        centred = pre - jnp.mean(pre, -1, keepdims=True)
        rstd = lax.rsqrt(jnp.mean(centred * centred, -1, keepdims=True) + EPS)
        xhat = centred * rstd
        v = xhat * gain1 + shift1
        cdf = normal_cdf(v)
        frame = at + lax.broadcasted_iota(jnp.int32, (chunk, chans), 0)
        valid = frame < meta_ref[0]
        feat_ref[at : at + chunk] = jnp.where(valid, v * cdf, 0.0).astype(BF16)
        dv = cot_ref[at : at + chunk].astype(F32) * (cdf + v * normal_pdf(v))
        dv = jnp.where(valid, dv, 0.0)
        sum_gain = sum_gain + dv * xhat
        sum_shift = sum_shift + dv
        dx = dv * gain1
        first = jnp.mean(dx, -1, keepdims=True)
        second = jnp.mean(dx * xhat, -1, keepdims=True)
        d = (rstd * (dx - first - xhat * second)).astype(BF16)
        d_ref[at : at + chunk] = d
        half_ref[0, at : at + chunk] = d[:, :half]
        half_ref[1, at : at + chunk] = d[:, half:]
    norm1_ref[0:1] = jnp.sum(sum_gain, 0, keepdims=True)
    norm1_ref[1:2] = jnp.sum(sum_shift, 0, keepdims=True)
    core = meta_ref[1]
    blocks, block_rows = keep_ref.shape[0], keep_ref.shape[1]
    step = 16
    for out_ref, side in ((send_ref, 1), (keep_ref, 0)):
        d_half = half_ref[core ^ side]
        for b in range(0, blocks, step):
            lanes = patch_ref[:, b * block_rows : (b + step) * block_rows]
            grad = lax.dot_general(lanes, d_half, (((0,), (0,)), ((), ())), preferred_element_type=F32)
            for i in range(step):
                out_ref[tab_ref[side, b + i]] = grad[i * block_rows : (i + 1) * block_rows]


def backward_kernel(
    frames,
    chunk,
    d_ref,
    w1_ref,
    xhat_ref,
    slope_ref,
    rstd_ref,
    gain0_ref,
    x3_ref,
    rim_ref,
    norm1_ref,
    small_ref,
    dact_ref,
    dhigh_ref,
    dlow_ref,
):
    chans = w1_ref.shape[1]
    rows = x3_ref.shape[0]

    def spread(tap):
        return lax.dot_general(
            d_ref[...],
            w1_ref[tap * chans : (tap + 1) * chans],
            (((1,), (1,)), ((), ())),
            preferred_element_type=F32,
        )

    dact_ref[:frames] = spread(1)
    dact_ref[frames : 2 * frames] = spread(0)
    dact_ref[2 * frames :] = jnp.zeros((rows - 2 * frames, chans), F32)
    dact_ref[frames + 1 : 2 * frames + 1] += spread(2)
    gain0 = jnp.broadcast_to(gain0_ref[...], (chunk, chans))
    sum_gain = jnp.zeros((chunk, chans), F32)
    sum_shift = jnp.zeros((chunk, chans), F32)
    for at in range(0, rows, chunk):
        xhat = xhat_ref[at : at + chunk]
        dv = dact_ref[at : at + chunk] * slope_ref[at : at + chunk]
        sum_gain = sum_gain + dv * xhat
        sum_shift = sum_shift + dv
        dx = dv * gain0
        first = jnp.mean(dx, -1, keepdims=True)
        second = jnp.mean(dx * xhat, -1, keepdims=True)
        d = rstd_ref[at : at + chunk, :1] * (dx - first - xhat * second)
        high = d.astype(BF16)
        dhigh_ref[at : at + chunk] = high
        dlow_ref[at : at + chunk] = (d - high.astype(F32)).astype(BF16)
    xs = split_patches(x3_ref, rim_ref, frames, 2 * frames)
    over_rows = (((0,), (0,)), ((), ()))
    by_high = lax.dot_general(xs, dhigh_ref[...], over_rows, preferred_element_type=F32)
    by_low = lax.dot_general(xs, dlow_ref[...], over_rows, preferred_element_type=F32)
    small_ref[...] = jnp.zeros_like(small_ref)
    small_ref[0:10] = by_high[0:10] + by_high[20:30] + by_low[0:10]
    small_ref[10:11] = jnp.sum(sum_gain, 0, keepdims=True)
    small_ref[11:12] = jnp.sum(sum_shift, 0, keepdims=True)
    small_ref[12:14] = norm1_ref[0:2]


VMEM = pl.BlockSpec(memory_space=pltpu.VMEM)
SMEM = pl.BlockSpec(memory_space=pltpu.SMEM)


def place_tables(block, core):
    v = lax.broadcasted_iota(jnp.int32, (1, 64), 1) ^ block
    tables = []
    for levels in LEVELS:
        place = jnp.zeros_like(v)
        for bit, _, _ in levels:
            place = place * 2 + ((v >> bit) & 1)
        tables.append(place)
    own = jnp.where(core == 0, tables[0], tables[1])
    other = jnp.where(core == 0, tables[1], tables[0])
    return jnp.concatenate([own, other], 0)


def shards(
    waveform,
    lengths,
    conv0_weight,
    norm0_gain,
    norm0_shift,
    conv1_weight,
    norm1_gain,
    norm1_shift,
    cotangent,
):
    zh, y, zl, x, core = (lax.axis_index(name) for name in AXES)
    position = (zl * 8 + x) * 2 + core
    samples_dev = waveform.shape[1]
    frames = samples_dev // 10
    chans = conv1_weight.shape[2]
    length = lengths[0]
    sample_pos = position * samples_dev + jnp.arange(samples_dev, dtype=jnp.int32)
    cleaned = jnp.where(sample_pos < length, waveform[0], 0.0)

    first = cleaned[:10]
    rim_odd = jnp.concatenate([jnp.zeros((5,), F32), first[:5]])
    rim = jnp.stack([jnp.tile(rim_odd, 3), jnp.tile(first, 3)])
    back = []
    for i in range(int(np.prod(SHAPE))):
        if i % 64:
            back.append((i, i - 1))
    rim = lax.ppermute(rim, AXES, back)

    odd = jnp.concatenate([cleaned[5:], jnp.zeros((5,), F32)]).reshape(frames, 10)
    even = cleaned.reshape(frames, 10)
    rows = 2 * frames + 16
    patches = jnp.concatenate([odd, even, jnp.zeros((16, 10), F32)], 0)
    x3 = jnp.concatenate([patches, patches, patches], 1)
    w3 = jnp.concatenate([conv0_weight, conv0_weight, conv0_weight], 0)

    block = ((zh * 8 + y) * 4) + zl
    tab = place_tables(block, core)
    meta = jnp.stack([length // 10 - position * frames, core]).astype(jnp.int32)
    w1 = conv1_weight.reshape(3 * chans, chans)
    half = chans // 2
    chunk = 16
    shape = jax.ShapeDtypeStruct
    features, keep, send, d, xhat, slope, rstd, norm1 = pl.pallas_call(
        functools.partial(forward_kernel, frames, chunk),
        out_shape=(
            shape((frames, chans), BF16),
            shape((64, 24, half), F32),
            shape((64, 24, half), F32),
            shape((frames, chans), BF16),
            shape((rows, chans), F32),
            shape((rows, chans), F32),
            shape((rows, 128), F32),
            shape((8, chans), F32),
        ),
        in_specs=[SMEM, SMEM] + [VMEM] * 9,
        out_specs=(VMEM,) * 8,
        scratch_shapes=[
            pltpu.VMEM((rows, chans), F32),
            pltpu.VMEM((rows - frames, chans), F32),
            pltpu.VMEM((frames, 3 * chans), BF16),
            pltpu.VMEM((frames, chans), F32),
            pltpu.VMEM((2, frames, half), BF16),
        ],
        compiler_params=pltpu.CompilerParams(vmem_limit_bytes=24 << 20),
        name="forward",
    )(
        tab,
        meta,
        x3,
        rim,
        w3,
        norm0_gain.reshape(1, chans),
        norm0_shift.reshape(1, chans),
        w1,
        norm1_gain.reshape(1, chans),
        norm1_shift.reshape(1, chans),
        cotangent[0],
    )
    received = lax.ppermute(send, "core", [(0, 1), (1, 0)])
    small = pl.pallas_call(
        functools.partial(backward_kernel, frames, chunk),
        out_shape=shape((16, chans), F32),
        in_specs=[VMEM] * 9,
        out_specs=VMEM,
        scratch_shapes=[
            pltpu.VMEM((rows, chans), F32),
            pltpu.VMEM((rows, chans), BF16),
            pltpu.VMEM((rows, chans), BF16),
        ],
        compiler_params=pltpu.CompilerParams(vmem_limit_bytes=16 << 20),
        name="backward",
    )(d, w1, xhat, slope, rstd, norm0_gain.reshape(1, chans), x3, rim, norm1)

    terms = [keep, received]
    count = 64
    for level in range(6):
        count //= 2
        step = lambda c, level=level: LEVELS[c][level][1:]
        out = sum(t[count : 2 * count] for t in terms)
        terms = [t[:count] for t in terms] + [exchange(out, step)]
        small = small + exchange(small, step)
    mine = sum(t[0] for t in terms).reshape(8, 3 * half)
    for distance in (1, 2, 4):
        bit = (x // distance) & 1
        pairs = mine.reshape(-1, 2, 3 * half)
        out = jnp.where(bit == 0, pairs[:, 1], pairs[:, 0])
        kept = jnp.where(bit == 0, pairs[:, 0], pairs[:, 1])
        step = lambda c, distance=distance: ("x", distance)
        mine = kept + exchange(out, step)
        small = small + exchange(small, step)

    mine = mine.reshape(3, half)
    out = jnp.where(core == 0, mine[2], mine[0])
    message = jnp.concatenate([small[:14].reshape(-1), out])
    other = lax.ppermute(message, "core", [(0, 1), (1, 0)])
    small_grads = small[:14] + other[: 14 * chans].reshape(14, chans)
    got = other[14 * chans :]
    conv1_grad = jnp.where(
        core == 0,
        jnp.concatenate([mine[0], got, mine[1]]),
        jnp.concatenate([mine[1], got, mine[2]]),
    )
    return (features[None], conv1_grad, small_grads)


def solution(mesh):
    torus = Mesh(mesh.devices.reshape(SHAPE), AXES)
    dp, audio = ("zh", "y"), ("zl", "x", "core")
    in_specs = (P(dp, audio), P(dp), P(), P(), P(), P(), P(), P(), P(dp, audio, None))
    out_specs = (P(dp, audio, None), P(dp + audio), P())
    return jax.shard_map(shards, mesh=torus, in_specs=in_specs, out_specs=out_specs, check_vma=False)
```

time: 762 us -> 154 us (0.20)
  waiting for transfers between devices: 557 us -> 47.8 us
  blocking collectives: 139 us -> 0 us
  starting transfers between devices: 16.1 us -> 87.4 us
  between operations: 16.4 us -> 1.94 us
  other arithmetic: 13.4 us -> 4.95 us
    unnamed x4 -> x0, waiting for transfers between devices: 557 us -> none
    psum x1 -> x0, blocking collectives: 139 us -> none  [shards(): small_grads = lax.psum(small_terms, ('dp', 'audio'))]
    ppermute x1 -> x21, starting transfers between devices: 16.1 us -> 87.4 us  [the longest x18 56.7 us: exchange(): return lax.ppermute(value, AXES, partners(step))]
    ppermute x1 -> x21, waiting for transfers between devices: 0.76 us -> 47.8 us  [the longest x18 43.6 us: exchange(): return lax.ppermute(value, AXES, partners(step))]
  transfers between devices with their start and end apart: 3 -> 21, of which waited for: 3 -> 10; matrix products, arithmetic and copies ran while one was open for 2% -> 2% of each run, Pallas kernels for 0% -> 1%
where the time goes in v1:
time: 154 us; the launch traced here: 153 us
  starting transfers between devices  87.4 us (57%)
  waiting for transfers between devices  47.8 us (31%)
  local copies, waits for them, and re-layouts  6 us (4%)
  other arithmetic  4.95 us (3%)
  Pallas kernels  4.45 us (3%)
  between operations  1.94 us (1%)
    ppermute x18, starting transfers between devices, exchange(): return lax.ppermute(value, AXES, partners(step))  56.7 us
    ppermute x18, waiting for transfers between devices, exchange(): return lax.ppermute(value, AXES, partners(step))  43.6 us
    ppermute x1, starting transfers between devices, shards(): rim = lax.ppermute(rim, AXES, back)  16.1 us
    ppermute x1, starting transfers between devices, shards(): other = lax.ppermute(message, 'core', [(0, 1), (1, 0)])  12.8 us
    unnamed x20, local copies, waits for them, and re-layouts  5.07 us
    ppermute x1, waiting for transfers between devices, shards(): received = lax.ppermute(send, 'core', [(0, 1), (1, 0)])  3.38 us
    pallas_call x1, Pallas kernels, shards(): pl.pallas_call(functools.partial(forward_kernel, frames, chunk), out_shap...  3.35 us
  transfers between devices with their start and end apart: 21, of which 10 were waited for; matrix products, arithmetic and copies ran while one was open for 2% of the time, Pallas kernels for 1%

profile of v1, /device:TPU:1, one launch (start us, length us, event | category | flops | bytes accessed | tf_op | source)
XLA Modules:
  0.0 152.6 jit_solution(4359500429934514784)
XLA Ops:
  2.3 16.1 %collective-permute-start = (f32[2,30]{1,0:T(2,128)S(1)}, f32[2,30]{1,0:T(2,128)S(1)}, u32[]{:S(2)}, u32[]{:S(2)}) collective-permute-start(f32[2,30]{1,0:T(2,128)S(1)} %pad_maximum_fusion.4), channel_id=1, source_target_pairs={{1,0},{2,1},{3,2},{4,3},{5,4},{6,5},{7,6},{8,7},{9,8},{10,9},{11,1... | collective-permute-start | bytes 728 | tf_op jit(solution)/shard_map/ppermute | solution.py:256
  20.2 1.4 copy-done
  25.3 3.3 %forward.1 = (bf16[176,512]{1,0:T(8,128)(2,1)}, f32[64,24,256]{2,1,0:T(8,128)S(1)}, f32[64,24,256]{2,1,0:T(8,128)S(1)}, bf16[176,512]{1,0:T(8,128)(2,1)S(1)}, f3...) custom-call(s32[2,64]{1,0:T(2,128)S(1)} %pad_add_fusion.tab_ref, ...), custom_call_target="tpu_custom_call" | custom-call | tf_op jit(solution)/shard_map/forward/pallas_call | solution.py:272
  28.6 1.9 %collective-permute-start.1 = (f32[64,24,256]{2,1,0:T(8,128)S(1)}, f32[64,24,256]{2,1,0:T(8,128)S(1)}, u32[]{:S(2)}, u32[]{:S(2)}) collective-permute-start(f32[64,24,256]{2,1,0:T(8,128)S(1)} %get-tuple-element.13), channel_id=1, source_target_pairs={{0,1},{1,0},{2,3},{3,2},{4,5},{5,4},{6,7},{7,6},{8,9},{9,8},{10,11... | collective-permute-start | bytes 4718600 | tf_op jit(solution)/shard_map/ppermute | solution.py:308
  30.5 3.4 %collective-permute-done.1 = f32[64,24,256]{2,1,0:T(8,128)S(1)} collective-permute-done((f32[64,24,256]{2,1,0:T(8,128)S(1)}, f32[64,24,256]{2,1,0:T(8,128)S(1)}, u32[]{:S(2)}, u32[]{:S(2)}) %collective-permute-start.1) | collective-permute-done | bytes 1572896 | tf_op jit(solution)/shard_map/ppermute | solution.py:308
  34.0 1.9 %collective-permute-start.2 = (f32[32,24,256]{2,1,0:T(8,128)S(1)}, f32[32,24,256]{2,1,0:T(8,128)S(1)}, u32[]{:S(2)}, u32[]{:S(2)}) collective-permute-start(f32[32,24,256]{2,1,0:T(8,128)S(1)} %slice_add_fusion), channel_id=1, source_target_pairs={{0,64},{1,17},{2,66},{3,19},{4,68},{5,21},{6,70},{7,23},{8,72},{9,... | collective-permute-start | bytes 2359304 | tf_op jit(solution)/shard_map/ppermute | solution.py:36
  36.0 11.1 %collective-permute-done.2 = f32[32,24,256]{2,1,0:T(8,128)S(1)} collective-permute-done((f32[32,24,256]{2,1,0:T(8,128)S(1)}, f32[32,24,256]{2,1,0:T(8,128)S(1)}, u32[]{:S(2)}, u32[]{:S(2)}) %collective-permute-start.2) | collective-permute-done | bytes 786464 | tf_op jit(solution)/shard_map/ppermute | solution.py:36
  47.1 1.9 %collective-permute-start.3 = (f32[16,24,256]{2,1,0:T(8,128)S(1)}, f32[16,24,256]{2,1,0:T(8,128)S(1)}, u32[]{:S(2)}, u32[]{:S(2)}) collective-permute-start(f32[16,24,256]{2,1,0:T(8,128)S(1)} %slice_add_fusion.1), channel_id=1, source_target_pairs={{0,16},{1,65},{2,18},{3,67},{4,20},{5,69},{6,22},{7,71},{8,24},{9,... | collective-permute-start | bytes 1179656 | tf_op jit(solution)/shard_map/ppermute | solution.py:36
  49.1 6.9 %collective-permute-done.3 = f32[16,24,256]{2,1,0:T(8,128)S(1)} collective-permute-done((f32[16,24,256]{2,1,0:T(8,128)S(1)}, f32[16,24,256]{2,1,0:T(8,128)S(1)}, u32[]{:S(2)}, u32[]{:S(2)}) %collective-permute-start.3) | collective-permute-done | bytes 393248 | tf_op jit(solution)/shard_map/ppermute | solution.py:36
  56.0 1.9 %collective-permute-start.4 = (f32[8,24,256]{2,1,0:T(8,128)S(1)}, f32[8,24,256]{2,1,0:T(8,128)S(1)}, u32[]{:S(2)}, u32[]{:S(2)}) collective-permute-start(f32[8,24,256]{2,1,0:T(8,128)S(1)} %slice_add_fusion.3), channel_id=1, source_target_pairs={{0,128},{1,33},{2,130},{3,35},{4,132},{5,37},{6,134},{7,39},{8,136... | collective-permute-start | bytes 589832 | tf_op jit(solution)/shard_map/ppermute | solution.py:36
  59.1 1.9 %collective-permute-start.11 = (f32[16,512]{1,0:T(8,128)S(1)}, f32[16,512]{1,0:T(8,128)S(1)}, u32[]{:S(2)}, u32[]{:S(2)}) collective-permute-start(f32[16,512]{1,0:T(8,128)S(1)} %backward.1), channel_id=1, source_target_pairs={{0,64},{1,17},{2,66},{3,19},{4,68},{5,21},{6,70},{7,23},{8,72},{9,... | collective-permute-start | bytes 98312 | tf_op jit(solution)/shard_map/ppermute | solution.py:36
  61.0 4.1 %collective-permute-done.4 = f32[8,24,256]{2,1,0:T(8,128)S(1)} collective-permute-done((f32[8,24,256]{2,1,0:T(8,128)S(1)}, f32[8,24,256]{2,1,0:T(8,128)S(1)}, u32[]{:S(2)}, u32[]{:S(2)}) %collective-permute-start.4) | collective-permute-done | bytes 196640 | tf_op jit(solution)/shard_map/ppermute | solution.py:36
  65.2 1.9 %collective-permute-start.5 = (f32[4,24,256]{2,1,0:T(8,128)S(1)}, f32[4,24,256]{2,1,0:T(8,128)S(1)}, u32[]{:S(2)}, u32[]{:S(2)}) collective-permute-start(f32[4,24,256]{2,1,0:T(8,128)S(1)} %slice_add_fusion.6), channel_id=1, source_target_pairs={{0,32},{1,129},{2,34},{3,131},{4,36},{5,133},{6,38},{7,135},{8,40}... | collective-permute-start | bytes 294920 | tf_op jit(solution)/shard_map/ppermute | solution.py:36
  67.1 1.9 %collective-permute-start.12 = (f32[16,512]{1,0:T(8,128)S(1)}, f32[16,512]{1,0:T(8,128)S(1)}, u32[]{:S(2)}, u32[]{:S(2)}) collective-permute-start(f32[16,512]{1,0:T(8,128)S(1)} %add.368), channel_id=1, source_target_pairs={{0,16},{1,65},{2,18},{3,67},{4,20},{5,69},{6,22},{7,71},{8,24},{9,... | collective-permute-start | bytes 98312 | tf_op jit(solution)/shard_map/ppermute | solution.py:36
  69.1 3.5 %collective-permute-done.12 = f32[16,512]{1,0:T(8,128)S(1)} collective-permute-done((f32[16,512]{1,0:T(8,128)S(1)}, f32[16,512]{1,0:T(8,128)S(1)}, u32[]{:S(2)}, u32[]{:S(2)}) %collective-permute-start.12) | collective-permute-done | bytes 32800 | tf_op jit(solution)/shard_map/ppermute | solution.py:36
  72.6 1.9 %collective-permute-start.13 = (f32[16,512]{1,0:T(8,128)S(1)}, f32[16,512]{1,0:T(8,128)S(1)}, u32[]{:S(2)}, u32[]{:S(2)}) collective-permute-start(f32[16,512]{1,0:T(8,128)S(1)} %add.369), channel_id=1, source_target_pairs={{0,128},{1,33},{2,130},{3,35},{4,132},{5,37},{6,134},{7,39},{8,136... | collective-permute-start | bytes 98312 | tf_op jit(solution)/shard_map/ppermute | solution.py:36
  74.5 3.6 %collective-permute-done.13 = f32[16,512]{1,0:T(8,128)S(1)} collective-permute-done((f32[16,512]{1,0:T(8,128)S(1)}, f32[16,512]{1,0:T(8,128)S(1)}, u32[]{:S(2)}, u32[]{:S(2)}) %collective-permute-start.13) | collective-permute-done | bytes 32800 | tf_op jit(solution)/shard_map/ppermute | solution.py:36
  78.1 3.8 %collective-permute-start.14 = (f32[16,512]{1,0:T(8,128)S(1)}, f32[16,512]{1,0:T(8,128)S(1)}, u32[]{:S(2)}, u32[]{:S(2)}) collective-permute-start(f32[16,512]{1,0:T(8,128)S(1)} %add.370), channel_id=1, source_target_pairs={{0,32},{1,129},{2,34},{3,131},{4,36},{5,133},{6,38},{7,135},{8,40}... | collective-permute-start | bytes 98312 | tf_op jit(solution)/shard_map/ppermute | solution.py:36
  82.0 5.6 %collective-permute-start.6 = (f32[2,24,256]{2,1,0:T(8,128)S(1)}, f32[2,24,256]{2,1,0:T(8,128)S(1)}, u32[]{:S(2)}, u32[]{:S(2)}) collective-permute-start(f32[2,24,256]{2,1,0:T(8,128)S(1)} %slice_add_fusion.10), channel_id=1, source_target_pairs={{0,256},{1,513},{2,258},{3,515},{4,260},{5,517},{6,262},{7,519},{8... | collective-permute-start | bytes 147464 | tf_op jit(solution)/shard_map/ppermute | solution.py:36
  87.6 3.6 %collective-permute-start.15 = (f32[16,512]{1,0:T(8,128)S(1)}, f32[16,512]{1,0:T(8,128)S(1)}, u32[]{:S(2)}, u32[]{:S(2)}) collective-permute-start(f32[16,512]{1,0:T(8,128)S(1)} %add.371), channel_id=1, source_target_pairs={{0,256},{1,513},{2,258},{3,515},{4,260},{5,517},{6,262},{7,519},{8... | collective-permute-start | bytes 98312 | tf_op jit(solution)/shard_map/ppermute | solution.py:36
  91.2 5.2 %collective-permute-done.15 = f32[16,512]{1,0:T(8,128)S(1)} collective-permute-done((f32[16,512]{1,0:T(8,128)S(1)}, f32[16,512]{1,0:T(8,128)S(1)}, u32[]{:S(2)}, u32[]{:S(2)}) %collective-permute-start.15) | collective-permute-done | bytes 32800 | tf_op jit(solution)/shard_map/ppermute | solution.py:36
  96.4 7.2 %collective-permute-start.16 = (f32[16,512]{1,0:T(8,128)S(1)}, f32[16,512]{1,0:T(8,128)S(1)}, u32[]{:S(2)}, u32[]{:S(2)}) collective-permute-start(f32[16,512]{1,0:T(8,128)S(1)} %add.372), channel_id=1, source_target_pairs={{0,512},{1,257},{2,514},{3,259},{4,516},{5,261},{6,518},{7,263},{8... | collective-permute-start | bytes 98312 | tf_op jit(solution)/shard_map/ppermute | solution.py:36
  104.3 2.0 %collective-permute-start.7 = (f32[1,24,256]{2,1,0:T(8,128)}, f32[1,24,256]{2,1,0:T(8,128)}, u32[]{:S(2)}, u32[]{:S(2)}) collective-permute-start(f32[1,24,256]{2,1,0:T(8,128)} %slice_add_fusion.16), channel_id=1, source_target_pairs={{0,512},{1,257},{2,514},{3,259},{4,516},{5,261},{6,518},{7,263},{8... | collective-permute-start | bytes 73736 | tf_op jit(solution)/shard_map/ppermute | solution.py:36
  106.3 2.5 %collective-permute-start.17 = (f32[16,512]{1,0:T(8,128)S(1)}, f32[16,512]{1,0:T(8,128)S(1)}, u32[]{:S(2)}, u32[]{:S(2)}) collective-permute-start(f32[16,512]{1,0:T(8,128)S(1)} %add.373), channel_id=1, source_target_pairs={{0,2},{1,3},{2,0},{3,1},{4,6},{5,7},{6,4},{7,5},{8,10},{9,11},{10,... | collective-permute-start | bytes 98312 | tf_op jit(solution)/shard_map/ppermute | solution.py:36
  108.8 4.6 %collective-permute-done.7 = f32[1,24,256]{2,1,0:T(8,128)} collective-permute-done((f32[1,24,256]{2,1,0:T(8,128)}, f32[1,24,256]{2,1,0:T(8,128)}, u32[]{:S(2)}, u32[]{:S(2)}) %collective-permute-start.7) | collective-permute-done | bytes 24608 | tf_op jit(solution)/shard_map/ppermute | solution.py:36
  114.2 2.3 %collective-permute-start.8 = (f32[4,768]{1,0:T(4,128)S(1)}, f32[4,768]{1,0:T(4,128)S(1)}, u32[]{:S(2)}, u32[]{:S(2)}) collective-permute-start(f32[4,768]{1,0:T(4,128)S(1)} %bitcast.50), channel_id=1, source_target_pairs={{0,2},{1,3},{2,0},{3,1},{4,6},{5,7},{6,4},{7,5},{8,10},{9,11},{10,... | collective-permute-start | bytes 36872 | tf_op jit(solution)/shard_map/ppermute | solution.py:36
  116.6 5.3 %collective-permute-start.18 = (f32[16,512]{1,0:T(8,128)S(1)}, f32[16,512]{1,0:T(8,128)S(1)}, u32[]{:S(2)}, u32[]{:S(2)}) collective-permute-start(f32[16,512]{1,0:T(8,128)S(1)} %add.374), channel_id=1, source_target_pairs={{0,4},{1,5},{2,6},{3,7},{4,0},{5,1},{6,2},{7,3},{8,12},{9,13},{10,... | collective-permute-start | bytes 98312 | tf_op jit(solution)/shard_map/ppermute | solution.py:36
  121.9 1.9 %collective-permute-start.9 = (f32[2,768]{1,0:T(2,128)S(1)}, f32[2,768]{1,0:T(2,128)S(1)}, u32[]{:S(2)}, u32[]{:S(2)}) collective-permute-start(f32[2,768]{1,0:T(2,128)S(1)} %bitcast.55), channel_id=1, source_target_pairs={{0,4},{1,5},{2,6},{3,7},{4,0},{5,1},{6,2},{7,3},{8,12},{9,13},{10,... | collective-permute-start | bytes 18440 | tf_op jit(solution)/shard_map/ppermute | solution.py:36
  123.9 5.5 %collective-permute-start.19 = (f32[16,512]{1,0:T(8,128)S(1)}, f32[16,512]{1,0:T(8,128)S(1)}, u32[]{:S(2)}, u32[]{:S(2)}) collective-permute-start(f32[16,512]{1,0:T(8,128)S(1)} %add.375), channel_id=1, source_target_pairs={{0,8},{1,9},{2,10},{3,11},{4,12},{5,13},{6,14},{7,15},{8,0},{9,1},... | collective-permute-start | bytes 98312 | tf_op jit(solution)/shard_map/ppermute | solution.py:36
  129.4 3.7 %collective-permute-start.10 = (f32[1,768]{1,0:T(1,128)S(1)}, f32[1,768]{1,0:T(1,128)S(1)}, u32[]{:S(2)}, u32[]{:S(2)}) collective-permute-start(f32[1,768]{1,0:T(1,128)S(1)} %fusion.13), channel_id=1, source_target_pairs={{0,8},{1,9},{2,10},{3,11},{4,12},{5,13},{6,14},{7,15},{8,0},{9,1},... | collective-permute-start | bytes 9224 | tf_op jit(solution)/shard_map/ppermute | solution.py:36
  133.2 4.5 %collective-permute-done.10 = f32[1,768]{1,0:T(1,128)S(1)} collective-permute-done((f32[1,768]{1,0:T(1,128)S(1)}, f32[1,768]{1,0:T(1,128)S(1)}, u32[]{:S(2)}, u32[]{:S(2)}) %collective-permute-start.10) | collective-permute-done | bytes 3104 | tf_op jit(solution)/shard_map/ppermute | solution.py:36
  137.7 12.8 %collective-permute-start.20 = (f32[7424]{0:T(1024)S(1)}, f32[7424]{0:T(1024)S(1)}, u32[]{:S(2)}, u32[]{:S(2)}) collective-permute-start(f32[7424]{0:T(1024)S(1)} %pad_maximum_fusion.1), channel_id=1, source_target_pairs={{0,1},{1,0},{2,3},{3,2},{4,5},{5,4},{6,7},{7,6},{8,9},{9,8},{10,11... | collective-permute-start | bytes 89096 | tf_op jit(solution)/shard_map/ppermute | solution.py:344
  (89 shorter events, 11.5 us)
Async XLA Ops:
  2.3 17.9 %collective-permute-start = (f32[2,30]{1,0:T(2,128)S(1)}, f32[2,30]{1,0:T(2,128)S(1)}, u32[]{:S(2)}, u32[]{:S(2)}) collective-permute-start(f32[2,30]{1,0:T(2,128)S(1)} %pad_maximum_fusion.4), channel_id=1, source_target_pairs={{1,0},{2,1},{3,2},{4,3},{5,4},{6,5},{7,6},{8,7},{9,8},{10,9},{11,1... | collective-permute-start | bytes 728 | tf_op jit(solution)/shard_map/ppermute | solution.py:256
  20.2 1.4 copy-start
  21.6 0.9 copy-start.1
  22.6 0.7 copy-start.2
  23.2 0.7 copy-start.3
  23.9 0.7 copy-start.4
  24.6 0.7 copy-start.5
  28.6 5.3 %collective-permute-start.1 = (f32[64,24,256]{2,1,0:T(8,128)S(1)}, f32[64,24,256]{2,1,0:T(8,128)S(1)}, u32[]{:S(2)}, u32[]{:S(2)}) collective-permute-start(f32[64,24,256]{2,1,0:T(8,128)S(1)} %get-tuple-element.13), channel_id=1, source_target_pairs={{0,1},{1,0},{2,3},{3,2},{4,5},{5,4},{6,7},{7,6},{8,9},{9,8},{10,11... | collective-permute-start | bytes 4718600 | tf_op jit(solution)/shard_map/ppermute | solution.py:308
  34.0 13.0 %collective-permute-start.2 = (f32[32,24,256]{2,1,0:T(8,128)S(1)}, f32[32,24,256]{2,1,0:T(8,128)S(1)}, u32[]{:S(2)}, u32[]{:S(2)}) collective-permute-start(f32[32,24,256]{2,1,0:T(8,128)S(1)} %slice_add_fusion), channel_id=1, source_target_pairs={{0,64},{1,17},{2,66},{3,19},{4,68},{5,21},{6,70},{7,23},{8,72},{9,... | collective-permute-start | bytes 2359304 | tf_op jit(solution)/shard_map/ppermute | solution.py:36
  47.1 56.6 %copy-start.6 = (f32[32,24,256]{2,1,0:T(8,128)}, f32[32,24,256]{2,1,0:T(8,128)S(1)}, u32[]{:S(2)}) copy-start(f32[32,24,256]{2,1,0:T(8,128)S(1)} %collective-permute-done.2) | copy-start | bytes 2359300
  47.1 8.8 %collective-permute-start.3 = (f32[16,24,256]{2,1,0:T(8,128)S(1)}, f32[16,24,256]{2,1,0:T(8,128)S(1)}, u32[]{:S(2)}, u32[]{:S(2)}) collective-permute-start(f32[16,24,256]{2,1,0:T(8,128)S(1)} %slice_add_fusion.1), channel_id=1, source_target_pairs={{0,16},{1,65},{2,18},{3,67},{4,20},{5,69},{6,22},{7,71},{8,24},{9,... | collective-permute-start | bytes 1179656 | tf_op jit(solution)/shard_map/ppermute | solution.py:36
  56.0 47.7 %copy-start.7 = (f32[16,24,256]{2,1,0:T(8,128)}, f32[16,24,256]{2,1,0:T(8,128)S(1)}, u32[]{:S(2)}) copy-start(f32[16,24,256]{2,1,0:T(8,128)S(1)} %collective-permute-done.3) | copy-start | bytes 1179652
  56.0 9.1 %collective-permute-start.4 = (f32[8,24,256]{2,1,0:T(8,128)S(1)}, f32[8,24,256]{2,1,0:T(8,128)S(1)}, u32[]{:S(2)}, u32[]{:S(2)}) collective-permute-start(f32[8,24,256]{2,1,0:T(8,128)S(1)} %slice_add_fusion.3), channel_id=1, source_target_pairs={{0,128},{1,33},{2,130},{3,35},{4,132},{5,37},{6,134},{7,39},{8,136... | collective-permute-start | bytes 589832 | tf_op jit(solution)/shard_map/ppermute | solution.py:36
  59.1 8.0 %collective-permute-start.11 = (f32[16,512]{1,0:T(8,128)S(1)}, f32[16,512]{1,0:T(8,128)S(1)}, u32[]{:S(2)}, u32[]{:S(2)}) collective-permute-start(f32[16,512]{1,0:T(8,128)S(1)} %backward.1), channel_id=1, source_target_pairs={{0,64},{1,17},{2,66},{3,19},{4,68},{5,21},{6,70},{7,23},{8,72},{9,... | collective-permute-start | bytes 98312 | tf_op jit(solution)/shard_map/ppermute | solution.py:36
  65.2 16.7 %collective-permute-start.5 = (f32[4,24,256]{2,1,0:T(8,128)S(1)}, f32[4,24,256]{2,1,0:T(8,128)S(1)}, u32[]{:S(2)}, u32[]{:S(2)}) collective-permute-start(f32[4,24,256]{2,1,0:T(8,128)S(1)} %slice_add_fusion.6), channel_id=1, source_target_pairs={{0,32},{1,129},{2,34},{3,131},{4,36},{5,133},{6,38},{7,135},{8,40}... | collective-permute-start | bytes 294920 | tf_op jit(solution)/shard_map/ppermute | solution.py:36
  67.1 5.4 %collective-permute-start.12 = (f32[16,512]{1,0:T(8,128)S(1)}, f32[16,512]{1,0:T(8,128)S(1)}, u32[]{:S(2)}, u32[]{:S(2)}) collective-permute-start(f32[16,512]{1,0:T(8,128)S(1)} %add.368), channel_id=1, source_target_pairs={{0,16},{1,65},{2,18},{3,67},{4,20},{5,69},{6,22},{7,71},{8,24},{9,... | collective-permute-start | bytes 98312 | tf_op jit(solution)/shard_map/ppermute | solution.py:36
  72.6 5.5 %collective-permute-start.13 = (f32[16,512]{1,0:T(8,128)S(1)}, f32[16,512]{1,0:T(8,128)S(1)}, u32[]{:S(2)}, u32[]{:S(2)}) collective-permute-start(f32[16,512]{1,0:T(8,128)S(1)} %add.369), channel_id=1, source_target_pairs={{0,128},{1,33},{2,130},{3,35},{4,132},{5,37},{6,134},{7,39},{8,136... | collective-permute-start | bytes 98312 | tf_op jit(solution)/shard_map/ppermute | solution.py:36
  78.1 9.4 %collective-permute-start.14 = (f32[16,512]{1,0:T(8,128)S(1)}, f32[16,512]{1,0:T(8,128)S(1)}, u32[]{:S(2)}, u32[]{:S(2)}) collective-permute-start(f32[16,512]{1,0:T(8,128)S(1)} %add.370), channel_id=1, source_target_pairs={{0,32},{1,129},{2,34},{3,131},{4,36},{5,133},{6,38},{7,135},{8,40}... | collective-permute-start | bytes 98312 | tf_op jit(solution)/shard_map/ppermute | solution.py:36
  82.0 21.7 %collective-permute-start.6 = (f32[2,24,256]{2,1,0:T(8,128)S(1)}, f32[2,24,256]{2,1,0:T(8,128)S(1)}, u32[]{:S(2)}, u32[]{:S(2)}) collective-permute-start(f32[2,24,256]{2,1,0:T(8,128)S(1)} %slice_add_fusion.10), channel_id=1, source_target_pairs={{0,256},{1,513},{2,258},{3,515},{4,260},{5,517},{6,262},{7,519},{8... | collective-permute-start | bytes 147464 | tf_op jit(solution)/shard_map/ppermute | solution.py:36
  87.6 8.9 %collective-permute-start.15 = (f32[16,512]{1,0:T(8,128)S(1)}, f32[16,512]{1,0:T(8,128)S(1)}, u32[]{:S(2)}, u32[]{:S(2)}) collective-permute-start(f32[16,512]{1,0:T(8,128)S(1)} %add.371), channel_id=1, source_target_pairs={{0,256},{1,513},{2,258},{3,515},{4,260},{5,517},{6,262},{7,519},{8... | collective-permute-start | bytes 98312 | tf_op jit(solution)/shard_map/ppermute | solution.py:36
  96.4 9.9 %collective-permute-start.16 = (f32[16,512]{1,0:T(8,128)S(1)}, f32[16,512]{1,0:T(8,128)S(1)}, u32[]{:S(2)}, u32[]{:S(2)}) collective-permute-start(f32[16,512]{1,0:T(8,128)S(1)} %add.372), channel_id=1, source_target_pairs={{0,512},{1,257},{2,514},{3,259},{4,516},{5,261},{6,518},{7,263},{8... | collective-permute-start | bytes 98312 | tf_op jit(solution)/shard_map/ppermute | solution.py:36
  103.6 0.6 copy-start.8
  104.3 9.0 %collective-permute-start.7 = (f32[1,24,256]{2,1,0:T(8,128)}, f32[1,24,256]{2,1,0:T(8,128)}, u32[]{:S(2)}, u32[]{:S(2)}) collective-permute-start(f32[1,24,256]{2,1,0:T(8,128)} %slice_add_fusion.16), channel_id=1, source_target_pairs={{0,512},{1,257},{2,514},{3,259},{4,516},{5,261},{6,518},{7,263},{8... | collective-permute-start | bytes 73736 | tf_op jit(solution)/shard_map/ppermute | solution.py:36
  106.3 10.2 %collective-permute-start.17 = (f32[16,512]{1,0:T(8,128)S(1)}, f32[16,512]{1,0:T(8,128)S(1)}, u32[]{:S(2)}, u32[]{:S(2)}) collective-permute-start(f32[16,512]{1,0:T(8,128)S(1)} %add.373), channel_id=1, source_target_pairs={{0,2},{1,3},{2,0},{3,1},{4,6},{5,7},{6,4},{7,5},{8,10},{9,11},{10,... | collective-permute-start | bytes 98312 | tf_op jit(solution)/shard_map/ppermute | solution.py:36
  114.2 7.6 %collective-permute-start.8 = (f32[4,768]{1,0:T(4,128)S(1)}, f32[4,768]{1,0:T(4,128)S(1)}, u32[]{:S(2)}, u32[]{:S(2)}) collective-permute-start(f32[4,768]{1,0:T(4,128)S(1)} %bitcast.50), channel_id=1, source_target_pairs={{0,2},{1,3},{2,0},{3,1},{4,6},{5,7},{6,4},{7,5},{8,10},{9,11},{10,... | collective-permute-start | bytes 36872 | tf_op jit(solution)/shard_map/ppermute | solution.py:36
  116.6 7.3 %collective-permute-start.18 = (f32[16,512]{1,0:T(8,128)S(1)}, f32[16,512]{1,0:T(8,128)S(1)}, u32[]{:S(2)}, u32[]{:S(2)}) collective-permute-start(f32[16,512]{1,0:T(8,128)S(1)} %add.374), channel_id=1, source_target_pairs={{0,4},{1,5},{2,6},{3,7},{4,0},{5,1},{6,2},{7,3},{8,12},{9,13},{10,... | collective-permute-start | bytes 98312 | tf_op jit(solution)/shard_map/ppermute | solution.py:36
  121.9 7.5 %collective-permute-start.9 = (f32[2,768]{1,0:T(2,128)S(1)}, f32[2,768]{1,0:T(2,128)S(1)}, u32[]{:S(2)}, u32[]{:S(2)}) collective-permute-start(f32[2,768]{1,0:T(2,128)S(1)} %bitcast.55), channel_id=1, source_target_pairs={{0,4},{1,5},{2,6},{3,7},{4,0},{5,1},{6,2},{7,3},{8,12},{9,13},{10,... | collective-permute-start | bytes 18440 | tf_op jit(solution)/shard_map/ppermute | solution.py:36
  123.9 9.3 %collective-permute-start.19 = (f32[16,512]{1,0:T(8,128)S(1)}, f32[16,512]{1,0:T(8,128)S(1)}, u32[]{:S(2)}, u32[]{:S(2)}) collective-permute-start(f32[16,512]{1,0:T(8,128)S(1)} %add.375), channel_id=1, source_target_pairs={{0,8},{1,9},{2,10},{3,11},{4,12},{5,13},{6,14},{7,15},{8,0},{9,1},... | collective-permute-start | bytes 98312 | tf_op jit(solution)/shard_map/ppermute | solution.py:36
  129.4 8.2 %collective-permute-start.10 = (f32[1,768]{1,0:T(1,128)S(1)}, f32[1,768]{1,0:T(1,128)S(1)}, u32[]{:S(2)}, u32[]{:S(2)}) collective-permute-start(f32[1,768]{1,0:T(1,128)S(1)} %fusion.13), channel_id=1, source_target_pairs={{0,8},{1,9},{2,10},{3,11},{4,12},{5,13},{6,14},{7,15},{8,0},{9,1},... | collective-permute-start | bytes 9224 | tf_op jit(solution)/shard_map/ppermute | solution.py:36
  137.7 13.6 %collective-permute-start.20 = (f32[7424]{0:T(1024)S(1)}, f32[7424]{0:T(1024)S(1)}, u32[]{:S(2)}, u32[]{:S(2)}) collective-permute-start(f32[7424]{0:T(1024)S(1)} %pad_maximum_fusion.1), channel_id=1, source_target_pairs={{0,1},{1,0},{2,3},{3,2},{4,5},{5,4},{6,7},{7,6},{8,9},{9,8},{10,11... | collective-permute-start | bytes 89096 | tf_op jit(solution)/shard_map/ppermute | solution.py:344

commit v2 on v1

v2 whole, which is shorter than its diff:
```python
import functools

import jax
import jax.numpy as jnp
import numpy as np
from jax import lax
from jax.experimental import pallas as pl
from jax.experimental.pallas import tpu as pltpu
from jax.sharding import Mesh
from jax.sharding import PartitionSpec as P

SHAPE = (2, 4, 2, 2, 2, 4, 2, 2)
AXES = ("zh", "yh", "y0", "z1", "z0", "xh", "x0", "core")
CUBE = ("y0", "z0", "x0")
CUBES = ("zh", "yh", "z1", "xh")
GROUP = 384
EPS = 1e-05
BF16, F32 = jnp.bfloat16, jnp.float32


def row_order():
    at = np.arange(GROUP).reshape(2, 2, 2, 2, 2, 2, 2, 3)
    return at.transpose(1, 3, 6, 0, 2, 4, 5, 7).reshape(1, GROUP).astype(np.int32)


def normal_cdf(v):
    return 0.5 + 0.5 * lax.erf(v * np.float32(0.5**0.5))


def normal_pdf(v):
    return jnp.exp(v * v * np.float32(-0.5)) * np.float32((2 * np.pi) ** -0.5)


def split_patches(x3_ref, rim_ref, odd_rows, even_last):
    value = x3_ref[...]
    row = lax.broadcasted_iota(jnp.int32, value.shape, 0)
    lane = lax.broadcasted_iota(jnp.int32, value.shape, 1)
    value = jnp.where(row == odd_rows - 1, value + rim_ref[0:1, :], value)
    value = jnp.where(row == even_last, value + rim_ref[1:2, :], value)
    high = value.astype(BF16).astype(F32)
    return jnp.where(lane < 20, high, value - high).astype(BF16)


def step_kernel(
    frames,
    chunk,
    meta_ref,
    order_ref,
    x3_ref,
    rim_ref,
    w3_ref,
    gain0_ref,
    shift0_ref,
    w1_ref,
    gain1_ref,
    shift1_ref,
    cot_ref,
    feat_ref,
    keep_ref,
    send_ref,
    pre0_ref,
    xhat_ref,
    slope_ref,
    rstd_ref,
    even_ref,
    patch_ref,
    pre1_ref,
    d_ref,
    dact_ref,
    dhigh_ref,
    dlow_ref,
    small_ref,
    grad_ref,
):
    chans = w1_ref.shape[1]
    half = chans // 2
    rows = x3_ref.shape[0]
    xs = split_patches(x3_ref, rim_ref, frames, 2 * frames)
    w3 = w3_ref[...]
    w3 = w3 - jnp.mean(w3, -1, keepdims=True)
    high = w3.astype(BF16).astype(F32)
    tap = lax.broadcasted_iota(jnp.int32, w3.shape, 0)
    ws = jnp.where((tap >= 10) & (tap < 20), w3 - high, high).astype(BF16)
    pre0_ref[...] = jnp.dot(xs, ws, preferred_element_type=F32)
    gain0 = jnp.broadcast_to(gain0_ref[...], (chunk, chans))
    shift0 = jnp.broadcast_to(shift0_ref[...], (chunk, chans))
    for at in range(0, rows, chunk):
        centred = pre0_ref[at : at + chunk]
        rstd = lax.rsqrt(jnp.mean(centred * centred, -1, keepdims=True) + EPS)
        xhat = centred * rstd
        v = xhat * gain0 + shift0
        cdf = normal_cdf(v)
        xhat_ref[at : at + chunk] = xhat
        slope_ref[at : at + chunk] = cdf + v * normal_pdf(v)
        rstd_ref[at : at + chunk] = jnp.broadcast_to(rstd, (chunk, 128))
        act = v * cdf
        if at < frames:
            patch_ref[at : at + chunk, chans : 2 * chans] = act.astype(BF16)
        else:
            even_ref[at - frames : at - frames + chunk] = act
    for at in range(0, frames, chunk):
        patch_ref[at : at + chunk, :chans] = even_ref[at : at + chunk].astype(BF16)
        patch_ref[at : at + chunk, 2 * chans :] = even_ref[at + 1 : at + 1 + chunk].astype(BF16)
    pre1_ref[...] = jnp.dot(patch_ref[...], w1_ref[...], preferred_element_type=F32)
    gain1 = jnp.broadcast_to(gain1_ref[...], (chunk, chans))
    shift1 = jnp.broadcast_to(shift1_ref[...], (chunk, chans))
    sum_gain = jnp.zeros((chunk, chans), F32)
    sum_shift = jnp.zeros((chunk, chans), F32)
    for at in range(0, frames, chunk):
        pre = pre1_ref[at : at + chunk]
        centred = pre - jnp.mean(pre, -1, keepdims=True)
        rstd = lax.rsqrt(jnp.mean(centred * centred, -1, keepdims=True) + EPS)
        xhat = centred * rstd
        v = xhat * gain1 + shift1
        cdf = normal_cdf(v)
        frame = at + lax.broadcasted_iota(jnp.int32, (chunk, chans), 0)
        valid = frame < meta_ref[0]
        feat_ref[at : at + chunk] = jnp.where(valid, v * cdf, 0.0).astype(BF16)
        dv = cot_ref[at : at + chunk].astype(F32) * (cdf + v * normal_pdf(v))
        dv = jnp.where(valid, dv, 0.0)
        sum_gain = sum_gain + dv * xhat
        sum_shift = sum_shift + dv
        dx = dv * gain1
        first = jnp.mean(dx, -1, keepdims=True)
        second = jnp.mean(dx * xhat, -1, keepdims=True)
        d_ref[at : at + chunk] = (rstd * (dx - first - xhat * second)).astype(BF16)
    small_ref[12:13] = jnp.sum(sum_gain, 0, keepdims=True)
    small_ref[13:14] = jnp.sum(sum_shift, 0, keepdims=True)
    small_ref[14:16] = jnp.zeros((2, chans), F32)

    source = lax.broadcasted_iota(jnp.int32, (GROUP, GROUP), 0)
    place = (source == order_ref[...]).astype(F32).astype(BF16)
    over_rows = (((0,), (0,)), ((), ()))
    part = GROUP // 8
    for group in range(3 * chans // GROUP):
        lanes = jnp.dot(patch_ref[:, group * GROUP : (group + 1) * GROUP], place, preferred_element_type=F32).astype(BF16)
        grad = lax.dot_general(lanes, d_ref[...], over_rows, preferred_element_type=F32)
        for cube in range(8):
            for side in range(2):
                grad_ref[side, cube, group * part : (group + 1) * part] = grad[
                    cube * part : (cube + 1) * part, side * half : (side + 1) * half
                ]

    def spread(tap):
        return lax.dot_general(
            d_ref[...],
            w1_ref[tap * chans : (tap + 1) * chans],
            (((1,), (1,)), ((), ())),
            preferred_element_type=F32,
        )

    dact_ref[:frames] = spread(1)
    dact_ref[frames : 2 * frames] = spread(0)
    dact_ref[2 * frames :] = jnp.zeros((rows - 2 * frames, chans), F32)
    dact_ref[frames + 1 : 2 * frames + 1] += spread(2)
    sum_gain = jnp.zeros((chunk, chans), F32)
    sum_shift = jnp.zeros((chunk, chans), F32)
    for at in range(0, rows, chunk):
        xhat = xhat_ref[at : at + chunk]
        dv = dact_ref[at : at + chunk] * slope_ref[at : at + chunk]
        sum_gain = sum_gain + dv * xhat
        sum_shift = sum_shift + dv
        dx = dv * gain0
        first = jnp.mean(dx, -1, keepdims=True)
        second = jnp.mean(dx * xhat, -1, keepdims=True)
        d = rstd_ref[at : at + chunk, :1] * (dx - first - xhat * second)
        high = d.astype(BF16)
        dhigh_ref[at : at + chunk] = high
        dlow_ref[at : at + chunk] = (d - high.astype(F32)).astype(BF16)
    by_high = lax.dot_general(xs, dhigh_ref[...], over_rows, preferred_element_type=F32)
    by_low = lax.dot_general(xs, dlow_ref[...], over_rows, preferred_element_type=F32)
    small_ref[0:10] = by_high[0:10] + by_high[20:30] + by_low[0:10]
    small_ref[10:11] = jnp.sum(sum_gain, 0, keepdims=True)
    small_ref[11:12] = jnp.sum(sum_shift, 0, keepdims=True)
    last = grad_ref.shape[2]
    for side in range(2):
        for cube in range(8):
            row = small_ref[8 * side + cube : 8 * side + cube + 1]
            grad_ref[side, cube, last - 8 : last - 7] = row[:, :half]
            grad_ref[side, cube, last - 7 : last - 6] = row[:, half:]
            grad_ref[side, cube, last - 6 :] = jnp.zeros((6, half), F32)
    core = meta_ref[1]
    keep_ref[...] = grad_ref[core]
    send_ref[...] = grad_ref[1 - core]


VMEM = pl.BlockSpec(memory_space=pltpu.VMEM)
SMEM = pl.BlockSpec(memory_space=pltpu.SMEM)


def shards(
    waveform,
    lengths,
    conv0_weight,
    norm0_gain,
    norm0_shift,
    conv1_weight,
    norm1_gain,
    norm1_shift,
    cotangent,
):
    position = lax.axis_index(("z1", "z0", "xh", "x0", "core"))
    core = lax.axis_index("core")
    samples_dev = waveform.shape[1]
    frames = samples_dev // 10
    chans = conv1_weight.shape[2]
    length = lengths[0]
    sample_pos = position * samples_dev + jnp.arange(samples_dev, dtype=jnp.int32)
    cleaned = jnp.where(sample_pos < length, waveform[0], 0.0)

    first = cleaned[:10]
    rim_odd = jnp.concatenate([jnp.zeros((5,), F32), first[:5]])
    rim = jnp.stack([jnp.tile(rim_odd, 3), jnp.tile(first, 3)])
    back = []
    for i in range(int(np.prod(SHAPE))):
        if i % 64:
            back.append((i, i - 1))
    rim = lax.ppermute(rim, AXES, back)

    odd = jnp.concatenate([cleaned[5:], jnp.zeros((5,), F32)]).reshape(frames, 10)
    even = cleaned.reshape(frames, 10)
    rows = 2 * frames + 16
    patches = jnp.concatenate([odd, even, jnp.zeros((16, 10), F32)], 0)
    x3 = jnp.concatenate([patches, patches, patches], 1)
    w3 = jnp.concatenate([conv0_weight, conv0_weight, conv0_weight], 0)

    meta = jnp.stack([length // 10 - position * frames, core]).astype(jnp.int32)
    half = chans // 2
    chunk = 16
    shape = jax.ShapeDtypeStruct
    features, keep, send = pl.pallas_call(
        functools.partial(step_kernel, frames, chunk),
        out_shape=(
            shape((frames, chans), BF16),
            shape((8, 200, half), F32),
            shape((8, 200, half), F32),
        ),
        in_specs=[SMEM] + [VMEM] * 10,
        out_specs=(VMEM,) * 3,
        scratch_shapes=[
            pltpu.VMEM((rows, chans), F32),
            pltpu.VMEM((rows, chans), F32),
            pltpu.VMEM((rows, chans), F32),
            pltpu.VMEM((rows, 128), F32),
            pltpu.VMEM((rows - frames, chans), F32),
            pltpu.VMEM((frames, 3 * chans), BF16),
            pltpu.VMEM((frames, chans), F32),
            pltpu.VMEM((frames, chans), BF16),
            pltpu.VMEM((rows, chans), F32),
            pltpu.VMEM((rows, chans), BF16),
            pltpu.VMEM((rows, chans), BF16),
            pltpu.VMEM((16, chans), F32),
            pltpu.VMEM((2, 8, 200, half), F32),
        ],
        compiler_params=pltpu.CompilerParams(vmem_limit_bytes=32 << 20),
        name="step",
    )(
        meta,
        row_order(),
        x3,
        rim,
        w3,
        norm0_gain.reshape(1, chans),
        norm0_shift.reshape(1, chans),
        conv1_weight.reshape(3 * chans, chans),
        norm1_gain.reshape(1, chans),
        norm1_shift.reshape(1, chans),
        cotangent[0],
    )
    mine = keep + lax.ppermute(send, "core", [(0, 1), (1, 0)])
    mine = jnp.sum(lax.all_to_all(mine, CUBE, 0, 0, tiled=True), 0)
    line = mine[192:194].reshape(1, chans)
    message = jnp.concatenate([mine[:192].reshape(64, 3 * half), jnp.broadcast_to(line, (64, chans))], 1)
    mine = jnp.sum(lax.all_to_all(message, CUBES, 0, 0, tiled=True), 0)
    part, line = mine[: 3 * half].reshape(3, half), mine[3 * half :]
    out = jnp.where(core == 0, part[2], part[0])
    message = jnp.broadcast_to(jnp.concatenate([line, out])[None], (16, chans + half))
    gathered = lax.all_to_all(message, ("core",) + CUBE, 0, 0, tiled=True)
    small_grads = gathered[:14, :chans]
    peer = (1 - core) * 8 + lax.axis_index(CUBE)
    got = lax.dynamic_slice(gathered, (peer, chans), (1, half))[0]
    conv1_grad = jnp.where(
        core == 0,
        jnp.concatenate([part[0], got, part[1]]),
        jnp.concatenate([part[1], got, part[2]]),
    )
    return (features[None], conv1_grad, small_grads)


def solution(mesh):
    torus = Mesh(mesh.devices.reshape(SHAPE), AXES)
    dp, audio = AXES[:3], AXES[3:]
    in_specs = (P(dp, audio), P(dp), P(), P(), P(), P(), P(), P(), P(dp, audio, None))
    out_specs = (P(dp, audio, None), P(dp + audio), P())
    return jax.shard_map(shards, mesh=torus, in_specs=in_specs, out_specs=out_specs, check_vma=False)
```

time: 154 us -> 110 us (0.71)
  starting transfers between devices: 87.4 us -> 40.2 us
  blocking collectives: 0 us -> 24.1 us
  waiting for transfers between devices: 47.8 us -> 26 us
  local copies, waits for them, and re-layouts: 6 us -> 8.92 us
  other arithmetic: 4.95 us -> 3.02 us
    ppermute x20 -> x1, starting transfers between devices: 71.4 us -> 1.91 us  [shards(): mine = keep + lax.ppermute(send, 'core', [(0, 1), (1, 0)])]
    ppermute x20 -> x1, waiting for transfers between devices: 47.8 us -> 3.47 us  [shards(): mine = keep + lax.ppermute(send, 'core', [(0, 1), (1, 0)])]
    all_to_all x0 -> x1, blocking collectives: none -> 24.1 us  [shards(): mine = jnp.sum(lax.all_to_all(mine, CUBE, 0, 0, tiled=True), 0)]
    all_to_all x0 -> x2, waiting for transfers between devices: none -> 22.5 us  [the longest x1 17.6 us: shards(): mine = jnp.sum(lax.all_to_all(message, CUBES, 0, 0, tiled=True), 0)]
    all_to_all x0 -> x2, starting transfers between devices: none -> 22.2 us  [the longest x1 15.2 us: shards(): mine = jnp.sum(lax.all_to_all(message, CUBES, 0, 0, tiled=True), 0)]
    add x19 -> x1, other arithmetic: 2.42 us -> 0.21 us  [shards(): mine = keep + lax.ppermute(send, 'core', [(0, 1), (1, 0)])]
    pallas_call x2 -> x1, Pallas kernels: 4.45 us -> 5.35 us  [shards(): pl.pallas_call(functools.partial(step_kernel, frames, chunk), out_shape=(...]
    unnamed x20 -> x17, local copies, waits for them, and re-layouts: 5.07 us -> 5.74 us
  transfers between devices with their start and end apart: 21 -> 4, of which waited for: 10 -> 3; matrix products, arithmetic and copies ran while one was open for 2% -> 2% of each run, Pallas kernels for 1% -> 0%
where the time goes in v2:
time: 110 us; the launch traced here: 109 us
  starting transfers between devices  40.2 us (37%)
  waiting for transfers between devices  26 us (24%)
  blocking collectives  24.1 us (22%)
  local copies, waits for them, and re-layouts  8.92 us (8%)
  Pallas kernels  5.35 us (5%)
  other arithmetic  3.02 us (3%)
  between operations  1.52 us (1%)
    all_to_all x1, blocking collectives, shards(): mine = jnp.sum(lax.all_to_all(mine, CUBE, 0, 0, tiled=True), 0)  24.1 us
    all_to_all x1, waiting for transfers between devices, shards(): mine = jnp.sum(lax.all_to_all(message, CUBES, 0, 0, tiled=True), 0)  17.6 us
    ppermute x1, starting transfers between devices, shards(): rim = lax.ppermute(rim, AXES, back)  16.1 us
    all_to_all x1, starting transfers between devices, shards(): mine = jnp.sum(lax.all_to_all(message, CUBES, 0, 0, tiled=True), 0)  15.2 us
    all_to_all x1, starting transfers between devices, shards(): gathered = lax.all_to_all(message, ('core',) + CUBE, 0, 0, tiled=True)  7.08 us
    unnamed x17, local copies, waits for them, and re-layouts  5.74 us
    pallas_call x1, Pallas kernels, shards(): pl.pallas_call(functools.partial(step_kernel, frames, chunk), out_shape=(...  5.35 us
    all_to_all x1, waiting for transfers between devices, shards(): gathered = lax.all_to_all(message, ('core',) + CUBE, 0, 0, tiled=True)  4.9 us
  transfers between devices with their start and end apart: 4, of which 3 were waited for; matrix products, arithmetic and copies ran while one was open for 2% of the time, Pallas kernels for 0%

profile of v2, /device:TPU:1, one launch (start us, length us, event | category | flops | bytes accessed | tf_op | source)
XLA Modules:
  0.0 109.1 jit_solution(5322375323829120925)
XLA Ops:
  1.3 0.7 reduce.1
  2.1 0.1 stack_tile.6
  2.2 0.1 stack_tile.7
  2.3 16.1 %collective-permute-start = (f32[2,30]{1,0:T(2,128)S(1)}, f32[2,30]{1,0:T(2,128)S(1)}, u32[]{:S(2)}, u32[]{:S(2)}) collective-permute-start(f32[2,30]{1,0:T(2,128)S(1)} %pad_maximum_fusion.5), channel_id=1, source_target_pairs={{1,0},{2,1},{3,2},{4,3},{5,4},{6,5},{7,6},{8,7},{9,8},{10,9},{11,1... | collective-permute-start | bytes 728 | tf_op jit(solution)/shard_map/ppermute | solution.py:218
  18.5 0.1 squeeze.22
  18.6 0.9 pad_maximum_fusion.1.w3_ref
  19.5 0.1 reshape.51
  19.8 0.1 maximum_maximum_fusion
  20.0 0.1 pad_add_fusion.meta_ref
  20.0 0.1 copy.15.x3_ref
  20.2 1.4 %copy-done = bf16[3,512,512]{2,1,0:T(8,128)(2,1)S(1)} copy-done((bf16[3,512,512]{2,1,0:T(8,128)(2,1)S(1)}, bf16[3,512,512]{2,1,0:T(8,128)(2,1)}, u32[]{:S(2)}) %copy-start) | copy-done | bytes 1572888
  21.6 0.9 copy-done.1
  22.5 0.7 copy-done.2
  23.2 0.7 copy-done.3
  23.9 0.7 copy-done.4
  24.6 0.7 copy-done.5
  25.2 0.7 copy-done.6
  25.9 5.3 %step.1 = (bf16[176,512]{1,0:T(8,128)(2,1)}, f32[8,200,256]{2,1,0:T(8,128)S(1)}, f32[8,200,256]{2,1,0:T(8,128)S(1)}) custom-call(s32[2]{0:T(128)S(1)} %pad_add_fusion.meta_ref, s32[1,384]{1,0:T(1,128)S(1)} %copy-done.6, f32[368,30]{1,0:T(8,128)S(1)} %copy.15.x3_ref, f32[2,30]{1,0:T(2,128)S(1)} %collective-permute-done.rim_ref, ...), custom_call_target="tpu_custom_call" | custom-call | tf_op jit(solution)/shard_map/step/pallas_call | solution.py:231
  31.3 1.9 %collective-permute-start.1 = (f32[8,200,256]{2,1,0:T(8,128)S(1)}, f32[8,200,256]{2,1,0:T(8,128)S(1)}, u32[]{:S(2)}, u32[]{:S(2)}) collective-permute-start(f32[8,200,256]{2,1,0:T(8,128)S(1)} %get-tuple-element.8), channel_id=1, source_target_pairs={{0,1},{1,0},{2,3},{3,2},{4,5},{5,4},{6,7},{7,6},{8,9},{9,8},{10,11... | collective-permute-start | bytes 4915208 | tf_op jit(solution)/shard_map/ppermute | solution.py:270
  33.2 3.5 %collective-permute-done.1 = f32[8,200,256]{2,1,0:T(8,128)S(1)} collective-permute-done((f32[8,200,256]{2,1,0:T(8,128)S(1)}, f32[8,200,256]{2,1,0:T(8,128)S(1)}, u32[]{:S(2)}, u32[]{:S(2)}) %collective-permute-start.1) | collective-permute-done | bytes 1638432 | tf_op jit(solution)/shard_map/ppermute | solution.py:270
  36.7 0.2 add.52
  36.9 24.1 %all_to_all.23 = f32[8,200,256]{2,1,0:T(8,128)S(1)} all-to-all(f32[8,200,256]{2,1,0:T(8,128)S(1)} %add.52), channel_id=1, replica_groups=mesh['zh'=2,'yh'=4,'y0'=2,'z1'=2,'z0'=2,'xh'=4,'x0'=2,'core'=2] {'y0','z..., dimensions={0} | all-to-all | bytes 3276800 | tf_op jit(solution)/shard_map/all_to_all | solution.py:271
  61.0 0.1 reduce_sum.18
  61.3 1.0 all_to_all.16
  62.2 15.2 %all-to-all-start.1 = ((f32[64,1,1280]{2,1,0:T(1,128)}), f32[64,1,1280]{2,1,0:T(1,128)S(1)}, u32[]{:S(2)}, u32[]{:S(2)}) async-start(f32[64,1,1280]{2,1,0:T(1,128)} %all_to_all.16), calls=%async_computation.1 | async-start | bytes 655360 | tf_op jit(solution)/shard_map/all_to_all | solution.py:274
  77.4 17.6 %all-to-all-done.1 = f32[64,1,1280]{2,1,0:T(1,128)S(1)} async-done(((f32[64,1,1280]{2,1,0:T(1,128)}), f32[64,1,1280]{2,1,0:T(1,128)S(1)}, u32[]{:S(2)}, u32[]{:S(2)}) %all-to-all-start.1) | async-done | bytes 327712 | tf_op jit(solution)/shard_map/all_to_all | solution.py:274
  95.0 0.2 reduce_sum.19
  95.2 0.6 broadcast_in_dim.31
  95.9 7.1 %all-to-all-start.2 = ((f32[16,1,768]{2,1,0:T(1,128)}), f32[16,1,768]{2,1,0:T(1,128)S(1)}, u32[]{:S(2)}, u32[]{:S(2)}) async-start(f32[16,1,768]{2,1,0:T(1,128)} %broadcast_in_dim.31), calls=%async_computation.2 | async-start | bytes 98304 | tf_op jit(solution)/shard_map/all_to_all | solution.py:278
  102.9 4.9 %all-to-all-done.2 = f32[16,1,768]{2,1,0:T(1,128)S(1)} async-done(((f32[16,1,768]{2,1,0:T(1,128)}), f32[16,1,768]{2,1,0:T(1,128)S(1)}, u32[]{:S(2)}, u32[]{:S(2)}) %all-to-all-start.2) | async-done | bytes 49184 | tf_op jit(solution)/shard_map/all_to_all | solution.py:278
  107.9 0.6 slice.60
  108.5 0.6 fusion.3
  (32 shorter events, 0.5 us)
Async XLA Ops:
  2.3 17.9 %collective-permute-start = (f32[2,30]{1,0:T(2,128)S(1)}, f32[2,30]{1,0:T(2,128)S(1)}, u32[]{:S(2)}, u32[]{:S(2)}) collective-permute-start(f32[2,30]{1,0:T(2,128)S(1)} %pad_maximum_fusion.5), channel_id=1, source_target_pairs={{1,0},{2,1},{3,2},{4,3},{5,4},{6,5},{7,6},{8,7},{9,8},{10,9},{11,1... | collective-permute-start | bytes 728 | tf_op jit(solution)/shard_map/ppermute | solution.py:218
  20.2 1.4 %copy-start = (bf16[3,512,512]{2,1,0:T(8,128)(2,1)S(1)}, bf16[3,512,512]{2,1,0:T(8,128)(2,1)}, u32[]{:S(2)}) copy-start(bf16[3,512,512]{2,1,0:T(8,128)(2,1)} %param.15) | copy-start | bytes 4718596
  21.6 0.9 copy-start.1
  22.5 0.7 copy-start.2
  23.2 0.7 copy-start.3
  23.9 0.7 copy-start.4
  24.6 0.7 copy-start.5
  25.2 0.7 copy-start.6
  31.3 5.4 %collective-permute-start.1 = (f32[8,200,256]{2,1,0:T(8,128)S(1)}, f32[8,200,256]{2,1,0:T(8,128)S(1)}, u32[]{:S(2)}, u32[]{:S(2)}) collective-permute-start(f32[8,200,256]{2,1,0:T(8,128)S(1)} %get-tuple-element.8), channel_id=1, source_target_pairs={{0,1},{1,0},{2,3},{3,2},{4,5},{5,4},{6,7},{7,6},{8,9},{9,8},{10,11... | collective-permute-start | bytes 4915208 | tf_op jit(solution)/shard_map/ppermute | solution.py:270
  62.2 32.8 %all-to-all-start.1 = ((f32[64,1,1280]{2,1,0:T(1,128)}), f32[64,1,1280]{2,1,0:T(1,128)S(1)}, u32[]{:S(2)}, u32[]{:S(2)}) async-start(f32[64,1,1280]{2,1,0:T(1,128)} %all_to_all.16), calls=%async_computation.1 | async-start | bytes 655360 | tf_op jit(solution)/shard_map/all_to_all | solution.py:274
  95.9 12.0 %all-to-all-start.2 = ((f32[16,1,768]{2,1,0:T(1,128)}), f32[16,1,768]{2,1,0:T(1,128)S(1)}, u32[]{:S(2)}, u32[]{:S(2)}) async-start(f32[16,1,768]{2,1,0:T(1,128)} %broadcast_in_dim.31), calls=%async_computation.2 | async-start | bytes 98304 | tf_op jit(solution)/shard_map/all_to_all | solution.py:278

commit v3 on v2

--- a/solution.py
+++ b/solution.py
@@ -18,9 +18,12 @@
 BF16, F32 = jnp.bfloat16, jnp.float32
 
 
-def row_order():
-    at = np.arange(GROUP).reshape(2, 2, 2, 2, 2, 2, 2, 3)
-    return at.transpose(1, 3, 6, 0, 2, 4, 5, 7).reshape(1, GROUP).astype(np.int32)
+def row_order(place):
+    chunk = (place * 171) >> 9
+    row = place - 3 * chunk
+    for source, target in ((6, 5), (5, 3), (4, 0), (3, 6), (2, 4), (1, 2), (0, 1)):
+        row = row + (((chunk >> source) & 1) << target) * 3
+    return row
 
 
 def normal_cdf(v):
@@ -45,16 +48,15 @@
     frames,
     chunk,
     meta_ref,
-    order_ref,
     x3_ref,
     rim_ref,
-    w3_ref,
-    gain0_ref,
-    shift0_ref,
-    w1_ref,
-    gain1_ref,
-    shift1_ref,
-    cot_ref,
+    w0_hbm,
+    gain0_hbm,
+    shift0_hbm,
+    w1_hbm,
+    gain1_hbm,
+    shift1_hbm,
+    cot_hbm,
     feat_ref,
     keep_ref,
     send_ref,
@@ -71,17 +73,37 @@
     dlow_ref,
     small_ref,
     grad_ref,
+    taps_ref,
+    w0_ref,
+    gain0_ref,
+    shift0_ref,
+    w1_ref,
+    gain1_ref,
+    shift1_ref,
+    cot_ref,
+    sems,
 ):
+    arriving = []
+    sources = (w0_hbm, gain0_hbm, shift0_hbm, w1_hbm, gain1_hbm, shift1_hbm, cot_hbm)
+    targets = (w0_ref, gain0_ref, shift0_ref, w1_ref, gain1_ref, shift1_ref, cot_ref)
+    for i, (source, target) in enumerate(zip(sources, targets)):
+        arriving.append(pltpu.make_async_copy(source, target, sems.at[i]))
+        arriving[-1].start()
     chans = w1_ref.shape[1]
     half = chans // 2
     rows = x3_ref.shape[0]
     xs = split_patches(x3_ref, rim_ref, frames, 2 * frames)
-    w3 = w3_ref[...]
-    w3 = w3 - jnp.mean(w3, -1, keepdims=True)
-    high = w3.astype(BF16).astype(F32)
-    tap = lax.broadcasted_iota(jnp.int32, w3.shape, 0)
-    ws = jnp.where((tap >= 10) & (tap < 20), w3 - high, high).astype(BF16)
+    arriving[0].wait()
+    w0 = w0_ref[...]
+    w0 = w0 - jnp.mean(w0, -1, keepdims=True)
+    high = w0.astype(BF16).astype(F32)
+    taps_ref[0:10] = high
+    taps_ref[10:20] = w0 - high
+    taps_ref[20:30] = high
+    ws = taps_ref[0:30].astype(BF16)
     pre0_ref[...] = jnp.dot(xs, ws, preferred_element_type=F32)
+    arriving[1].wait()
+    arriving[2].wait()
     gain0 = jnp.broadcast_to(gain0_ref[...], (chunk, chans))
     shift0 = jnp.broadcast_to(shift0_ref[...], (chunk, chans))
     for at in range(0, rows, chunk):
@@ -101,7 +123,10 @@
     for at in range(0, frames, chunk):
         patch_ref[at : at + chunk, :chans] = even_ref[at : at + chunk].astype(BF16)
         patch_ref[at : at + chunk, 2 * chans :] = even_ref[at + 1 : at + 1 + chunk].astype(BF16)
+    arriving[3].wait()
     pre1_ref[...] = jnp.dot(patch_ref[...], w1_ref[...], preferred_element_type=F32)
+    for copy in arriving[4:]:
+        copy.wait()
     gain1 = jnp.broadcast_to(gain1_ref[...], (chunk, chans))
     shift1 = jnp.broadcast_to(shift1_ref[...], (chunk, chans))
     sum_gain = jnp.zeros((chunk, chans), F32)
@@ -129,7 +154,8 @@
     small_ref[14:16] = jnp.zeros((2, chans), F32)
 
     source = lax.broadcasted_iota(jnp.int32, (GROUP, GROUP), 0)
-    place = (source == order_ref[...]).astype(F32).astype(BF16)
+    order = row_order(lax.broadcasted_iota(jnp.int32, (1, GROUP), 1))
+    place = (source == order).astype(F32).astype(BF16)
     over_rows = (((0,), (0,)), ((), ()))
     part = GROUP // 8
     for group in range(3 * chans // GROUP):
@@ -184,6 +210,7 @@
     send_ref[...] = grad_ref[1 - core]
 
 
+HBM = pl.BlockSpec(memory_space=pltpu.HBM)
 VMEM = pl.BlockSpec(memory_space=pltpu.VMEM)
 SMEM = pl.BlockSpec(memory_space=pltpu.SMEM)
 
@@ -205,25 +232,25 @@
     frames = samples_dev // 10
     chans = conv1_weight.shape[2]
     length = lengths[0]
-    sample_pos = position * samples_dev + jnp.arange(samples_dev, dtype=jnp.int32)
-    cleaned = jnp.where(sample_pos < length, waveform[0], 0.0)
-
-    first = cleaned[:10]
-    rim_odd = jnp.concatenate([jnp.zeros((5,), F32), first[:5]])
-    rim = jnp.stack([jnp.tile(rim_odd, 3), jnp.tile(first, 3)])
+    start = position * samples_dev
+    sample_pos = start + lax.broadcasted_iota(jnp.int32, (1, samples_dev), 1)
+
+    lane = lax.broadcasted_iota(jnp.int32, (1, 10), 1)
+    first = jnp.where(start + lane < length, waveform[:, :10], 0.0)
+    rim_odd = jnp.pad(first[:, :5], ((0, 0), (5, 0)))
+    rim = jnp.concatenate([jnp.tile(rim_odd, (1, 3)), jnp.tile(first, (1, 3))], 0)
     back = []
     for i in range(int(np.prod(SHAPE))):
         if i % 64:
             back.append((i, i - 1))
     rim = lax.ppermute(rim, AXES, back)
 
+    cleaned = jnp.where(sample_pos < length, waveform, 0.0)[0]
     odd = jnp.concatenate([cleaned[5:], jnp.zeros((5,), F32)]).reshape(frames, 10)
     even = cleaned.reshape(frames, 10)
     rows = 2 * frames + 16
     patches = jnp.concatenate([odd, even, jnp.zeros((16, 10), F32)], 0)
     x3 = jnp.concatenate([patches, patches, patches], 1)
-    w3 = jnp.concatenate([conv0_weight, conv0_weight, conv0_weight], 0)
-
     meta = jnp.stack([length // 10 - position * frames, core]).astype(jnp.int32)
     half = chans // 2
     chunk = 16
@@ -235,7 +262,7 @@
             shape((8, 200, half), F32),
             shape((8, 200, half), F32),
         ),
-        in_specs=[SMEM] + [VMEM] * 10,
+        in_specs=[SMEM] + [VMEM] * 2 + [HBM] * 7,
         out_specs=(VMEM,) * 3,
         scratch_shapes=[
             pltpu.VMEM((rows, chans), F32),
@@ -251,36 +278,50 @@
             pltpu.VMEM((rows, chans), BF16),
             pltpu.VMEM((16, chans), F32),
             pltpu.VMEM((2, 8, 200, half), F32),
+            pltpu.VMEM((32, chans), F32),
+            pltpu.VMEM((10, chans), F32),
+            pltpu.VMEM((1, chans), F32),
+            pltpu.VMEM((1, chans), F32),
+            pltpu.VMEM((3 * chans, chans), BF16),
+            pltpu.VMEM((1, chans), F32),
+            pltpu.VMEM((1, chans), F32),
+            pltpu.VMEM((frames, chans), BF16),
+            pltpu.SemaphoreType.DMA((7,)),
         ],
         compiler_params=pltpu.CompilerParams(vmem_limit_bytes=32 << 20),
         name="step",
     )(
         meta,
-        row_order(),
         x3,
         rim,
-        w3,
-        norm0_gain.reshape(1, chans),
-        norm0_shift.reshape(1, chans),
-        conv1_weight.reshape(3 * chans, chans),
-        norm1_gain.reshape(1, chans),
-        norm1_shift.reshape(1, chans),
-        cotangent[0],
+        *(
+            pltpu.with_memory_space_constraint(operand, pltpu.HBM)
+            for operand in (
+                conv0_weight,
+                norm0_gain.reshape(1, chans),
+                norm0_shift.reshape(1, chans),
+                conv1_weight.reshape(3 * chans, chans),
+                norm1_gain.reshape(1, chans),
+                norm1_shift.reshape(1, chans),
+                cotangent[0],
+            )
+        ),
     )
+    send, first_core = lax.optimization_barrier((send, core == 0))
     mine = keep + lax.ppermute(send, "core", [(0, 1), (1, 0)])
     mine = jnp.sum(lax.all_to_all(mine, CUBE, 0, 0, tiled=True), 0)
     line = mine[192:194].reshape(1, chans)
     message = jnp.concatenate([mine[:192].reshape(64, 3 * half), jnp.broadcast_to(line, (64, chans))], 1)
     mine = jnp.sum(lax.all_to_all(message, CUBES, 0, 0, tiled=True), 0)
     part, line = mine[: 3 * half].reshape(3, half), mine[3 * half :]
-    out = jnp.where(core == 0, part[2], part[0])
+    out = jnp.where(first_core, part[2], part[0])
     message = jnp.broadcast_to(jnp.concatenate([line, out])[None], (16, chans + half))
     gathered = lax.all_to_all(message, ("core",) + CUBE, 0, 0, tiled=True)
     small_grads = gathered[:14, :chans]
     peer = (1 - core) * 8 + lax.axis_index(CUBE)
     got = lax.dynamic_slice(gathered, (peer, chans), (1, half))[0]
     conv1_grad = jnp.where(
-        core == 0,
+        first_core,
         jnp.concatenate([part[0], got, part[1]]),
         jnp.concatenate([part[1], got, part[2]]),
     )

time: 110 us -> 105 us (0.955)
  blocking collectives: 24.1 us -> 57 us
  waiting for transfers between devices: 26 us -> 8.38 us
  starting transfers between devices: 40.2 us -> 25.2 us
  local copies, waits for them, and re-layouts: 8.92 us -> 2.49 us
  Pallas kernels: 5.35 us -> 6.57 us
    all_to_all x0 -> x1, blocking collectives: none -> 32.9 us  [shards(): mine = jnp.sum(lax.all_to_all(message, CUBES, 0, 0, tiled=True), 0)]
    all_to_all x1 -> x0, waiting for transfers between devices: 17.6 us -> none  [shards(): mine = jnp.sum(lax.all_to_all(message, CUBES, 0, 0, tiled=True), 0)]
    all_to_all x1 -> x0, starting transfers between devices: 15.2 us -> none  [shards(): mine = jnp.sum(lax.all_to_all(message, CUBES, 0, 0, tiled=True), 0)]
    unnamed x17 -> x3, local copies, waits for them, and re-layouts: 5.74 us -> 0.01 us
    select_n x3, other arithmetic: 0.64 us -> 1.99 us  [the longest x1 0.73 us: shards(): cleaned = jnp.where(sample_pos < length, waveform, 0.0)[0]]
    pallas_call x1, Pallas kernels: 5.35 us -> 6.57 us  [shards(): pl.pallas_call(functools.partial(step_kernel, frames, chunk), out_shape=(...]
  transfers between devices with their start and end apart: 4 -> 3, of which waited for: 3 -> 2; matrix products, arithmetic and copies ran while one was open for 2% -> 1% of each run, Pallas kernels for 0% -> 0%
where the time goes in v3:
time: 105 us; the launch traced here: 104 us
  blocking collectives  57 us (54%)
  starting transfers between devices  25.2 us (24%)
  waiting for transfers between devices  8.38 us (8%)
  Pallas kernels  6.57 us (6%)
  other arithmetic  3.42 us (3%)
  local copies, waits for them, and re-layouts  2.49 us (2%)
  between operations  1.48 us (1%)
    all_to_all x1, blocking collectives, shards(): mine = jnp.sum(lax.all_to_all(message, CUBES, 0, 0, tiled=True), 0)  32.9 us
    all_to_all x1, blocking collectives, shards(): mine = jnp.sum(lax.all_to_all(mine, CUBE, 0, 0, tiled=True), 0)  24.1 us
    ppermute x1, starting transfers between devices, shards(): rim = lax.ppermute(rim, AXES, back)  16.1 us
    all_to_all x1, starting transfers between devices, shards(): gathered = lax.all_to_all(message, ('core',) + CUBE, 0, 0, tiled=True)  7.17 us
    pallas_call x1, Pallas kernels, shards(): pl.pallas_call(functools.partial(step_kernel, frames, chunk), out_shape=(...  6.57 us
    all_to_all x1, waiting for transfers between devices, shards(): gathered = lax.all_to_all(message, ('core',) + CUBE, 0, 0, tiled=True)  4.9 us
    ppermute x1, waiting for transfers between devices, shards(): mine = keep + lax.ppermute(send, 'core', [(0, 1), (1, 0)])  3.47 us
  transfers between devices with their start and end apart: 3, of which 2 were waited for; matrix products, arithmetic and copies ran while one was open for 1% of the time, Pallas kernels for 0%

profile of v3, /device:TPU:1, one launch (start us, length us, event | category | flops | bytes accessed | tf_op | source)
XLA Modules:
  0.0 104.5 jit_solution(13985335498925795937)
XLA Ops:
  1.3 0.7 fusion.5
  2.0 0.7 compare_select_fusion.1
  2.6 0.1 pad_bitcast_fusion
  2.7 0.1 tile.24
  2.8 0.1 tile.27
  2.9 16.1 %collective-permute-start = (f32[2,30]{1,0:T(2,128)S(1)}, f32[2,30]{1,0:T(2,128)S(1)}, u32[]{:S(2)}, u32[]{:S(2)}) collective-permute-start(f32[2,30]{1,0:T(2,128)S(1)} %pad_maximum_fusion.4), channel_id=1, source_target_pairs={{1,0},{2,1},{3,2},{4,3},{5,4},{6,5},{7,6},{8,7},{9,8},{10,9},{11,1... | collective-permute-start | bytes 728 | tf_op jit(solution)/shard_map/ppermute | solution.py:246
  19.0 0.7 fusion.3
  19.7 0.1 slice_reduce_fusion
  19.8 0.1 reshape.83
  20.0 0.1 copy.12
  20.0 0.1 reshape_squeeze.3
  20.2 0.1 copy.13
  20.3 0.1 maximum_maximum_fusion
  20.4 0.1 pad_add_fusion.meta_ref
  20.4 0.1 copy.14.x3_ref
  20.6 0.0 collective-permute-done.rim_ref
  20.6 6.6 %step.1 = (bf16[176,512]{1,0:T(8,128)(2,1)}, f32[8,200,256]{2,1,0:T(8,128)S(1)}, f32[8,200,256]{2,1,0:T(8,128)S(1)}) custom-call(s32[2]{0:T(128)S(1)} %pad_add_fusion.meta_ref, f32[368,30]{1,0:T(8,128)S(1)} %copy.14.x3_ref, f32[2,30]{1,0:T(2,128)S(1)} %collective-permute-done.rim_ref, f32[10,512]{1,0:T(8,128)} %w0_hbm.1, f32[1,512]{1,0:T(1,128)} %bitcast.33, ...), custom_call_target="tpu_custom_call" | custom-call | tf_op jit(solution)/shard_map/step/pallas_call | solution.py:258
  27.2 1.9 %collective-permute-start.1 = (f32[8,200,256]{2,1,0:T(8,128)S(1)}, f32[8,200,256]{2,1,0:T(8,128)S(1)}, u32[]{:S(2)}, u32[]{:S(2)}) collective-permute-start(f32[8,200,256]{2,1,0:T(8,128)S(1)} %get-tuple-element.12), channel_id=1, source_target_pairs={{0,1},{1,0},{2,3},{3,2},{4,5},{5,4},{6,7},{7,6},{8,9},{9,8},{10,11... | collective-permute-start | bytes 4915208 | tf_op jit(solution)/shard_map/ppermute | solution.py:311
  29.1 3.5 %collective-permute-done.1 = f32[8,200,256]{2,1,0:T(8,128)S(1)} collective-permute-done((f32[8,200,256]{2,1,0:T(8,128)S(1)}, f32[8,200,256]{2,1,0:T(8,128)S(1)}, u32[]{:S(2)}, u32[]{:S(2)}) %collective-permute-start.1) | collective-permute-done | bytes 1638432 | tf_op jit(solution)/shard_map/ppermute | solution.py:311
  32.6 0.2 add.68
  32.8 24.1 %all_to_all.23 = f32[8,200,256]{2,1,0:T(8,128)S(1)} all-to-all(f32[8,200,256]{2,1,0:T(8,128)S(1)} %add.68), channel_id=1, replica_groups=mesh['zh'=2,'yh'=4,'y0'=2,'z1'=2,'z0'=2,'xh'=4,'x0'=2,'core'=2] {'y0','z..., dimensions={0} | all-to-all | bytes 3276800 | tf_op jit(solution)/shard_map/all_to_all | solution.py:312
  56.9 0.1 reduce_sum.18
  57.0 0.1 reshape.89
  57.2 0.2 all_to_all.16
  57.4 32.9 %all_to_all.24 = f32[64,1,1280]{2,1,0:T(1,128)S(1)} all-to-all(f32[64,1,1280]{2,1,0:T(1,128)S(1)} %all_to_all.16), channel_id=1, replica_groups=mesh['zh'=2,'yh'=4,'y0'=2,'z1'=2,'z0'=2,'xh'=4,'x0'=2,'core'=2] {'zh','y..., dimensions={0} | all-to-all | bytes 655360 | tf_op jit(solution)/shard_map/all_to_all | solution.py:315
  90.3 0.2 reduce_sum.19
  90.5 0.6 broadcast_in_dim.33
  91.2 7.2 %all-to-all-start.2 = ((f32[16,1,768]{2,1,0:T(1,128)}), f32[16,1,768]{2,1,0:T(1,128)S(1)}, u32[]{:S(2)}, u32[]{:S(2)}) async-start(f32[16,1,768]{2,1,0:T(1,128)} %broadcast_in_dim.33), calls=%async_computation.2 | async-start | bytes 98304 | tf_op jit(solution)/shard_map/all_to_all | solution.py:319
  98.3 4.9 %all-to-all-done.2 = f32[16,1,768]{2,1,0:T(1,128)S(1)} async-done(((f32[16,1,768]{2,1,0:T(1,128)}), f32[16,1,768]{2,1,0:T(1,128)S(1)}, u32[]{:S(2)}, u32[]{:S(2)}) %all-to-all-start.2) | async-done | bytes 49184 | tf_op jit(solution)/shard_map/all_to_all | solution.py:319
  103.3 0.6 slice.61
  103.9 0.6 fusion.1
  (15 shorter events, 0.1 us)
Async XLA Ops:
  2.9 17.7 %collective-permute-start = (f32[2,30]{1,0:T(2,128)S(1)}, f32[2,30]{1,0:T(2,128)S(1)}, u32[]{:S(2)}, u32[]{:S(2)}) collective-permute-start(f32[2,30]{1,0:T(2,128)S(1)} %pad_maximum_fusion.4), channel_id=1, source_target_pairs={{1,0},{2,1},{3,2},{4,3},{5,4},{6,5},{7,6},{8,7},{9,8},{10,9},{11,1... | collective-permute-start | bytes 728 | tf_op jit(solution)/shard_map/ppermute | solution.py:246
  27.2 5.4 %collective-permute-start.1 = (f32[8,200,256]{2,1,0:T(8,128)S(1)}, f32[8,200,256]{2,1,0:T(8,128)S(1)}, u32[]{:S(2)}, u32[]{:S(2)}) collective-permute-start(f32[8,200,256]{2,1,0:T(8,128)S(1)} %get-tuple-element.12), channel_id=1, source_target_pairs={{0,1},{1,0},{2,3},{3,2},{4,5},{5,4},{6,7},{7,6},{8,9},{9,8},{10,11... | collective-permute-start | bytes 4915208 | tf_op jit(solution)/shard_map/ppermute | solution.py:311
  91.2 12.1 %all-to-all-start.2 = ((f32[16,1,768]{2,1,0:T(1,128)}), f32[16,1,768]{2,1,0:T(1,128)S(1)}, u32[]{:S(2)}, u32[]{:S(2)}) async-start(f32[16,1,768]{2,1,0:T(1,128)} %broadcast_in_dim.33), calls=%async_computation.2 | async-start | bytes 98304 | tf_op jit(solution)/shard_map/all_to_all | solution.py:319

commit v4 on v3

--- a/solution.py
+++ b/solution.py
@@ -18,6 +18,16 @@
 BF16, F32 = jnp.bfloat16, jnp.float32
 
 
+def cubes():
+    groups = {}
+    for i in range(int(np.prod(SHAPE))):
+        zh, yh, y0, z1, z0, xh, x0, core = (int(v) for v in np.unravel_index(i, SHAPE))
+        z, y, x = zh * 4 + z1 * 2 + z0, yh * 2 + y0, xh * 2 + x0
+        cube = tuple(((v - core) % 8) // 2 for v in (z, y, x)) + (core,)
+        groups.setdefault(cube, [0] * 8)[(y0 * 2 + z0) * 2 + x0] = i
+    return list(groups.values())
+
+
 def row_order(place):
     chunk = (place * 171) >> 9
     row = place - 3 * chunk
@@ -34,12 +44,17 @@
     return jnp.exp(v * v * np.float32(-0.5)) * np.float32((2 * np.pi) ** -0.5)
 
 
-def split_patches(x3_ref, rim_ref, odd_rows, even_last):
+def split_patches(x3_ref, rim_ref, odd_last, even_last):
     value = x3_ref[...]
+    width = value.shape[1]
+    rim = jnp.broadcast_to(rim_ref[...], (8, 128))
+    five = jnp.where(lax.broadcasted_iota(jnp.int32, rim.shape, 1) < 5, rim, 0.0)
+    even = rim + pltpu.roll(rim, 10, 1) + pltpu.roll(rim, 20, 1)
+    odd = pltpu.roll(five, 5, 1) + pltpu.roll(five, 15, 1) + pltpu.roll(five, 25, 1)
     row = lax.broadcasted_iota(jnp.int32, value.shape, 0)
     lane = lax.broadcasted_iota(jnp.int32, value.shape, 1)
-    value = jnp.where(row == odd_rows - 1, value + rim_ref[0:1, :], value)
-    value = jnp.where(row == even_last, value + rim_ref[1:2, :], value)
+    value = jnp.where(row == odd_last, value + odd[0:1, :width], value)
+    value = jnp.where(row == even_last, value + even[0:1, :width], value)
     high = value.astype(BF16).astype(F32)
     return jnp.where(lane < 20, high, value - high).astype(BF16)
 
@@ -72,7 +87,7 @@
     dhigh_ref,
     dlow_ref,
     small_ref,
-    grad_ref,
+    sides_ref,
     taps_ref,
     w0_ref,
     gain0_ref,
@@ -92,7 +107,8 @@
     chans = w1_ref.shape[1]
     half = chans // 2
     rows = x3_ref.shape[0]
-    xs = split_patches(x3_ref, rim_ref, frames, 2 * frames)
+    core = meta_ref[1]
+    xs = split_patches(x3_ref, rim_ref, frames - 1, 2 * frames)
     arriving[0].wait()
     w0 = w0_ref[...]
     w0 = w0 - jnp.mean(w0, -1, keepdims=True)
@@ -148,7 +164,11 @@
         dx = dv * gain1
         first = jnp.mean(dx, -1, keepdims=True)
         second = jnp.mean(dx * xhat, -1, keepdims=True)
-        d_ref[at : at + chunk] = (rstd * (dx - first - xhat * second)).astype(BF16)
+        d = rstd * (dx - first - xhat * second)
+        d_ref[at : at + chunk] = d.astype(BF16)
+        left, right = d[:, :half], d[:, half:]
+        sides_ref[at : at + chunk, :half] = jnp.where(core == 0, right, left).astype(BF16)
+        sides_ref[at : at + chunk, half:] = jnp.where(core == 0, left, right).astype(BF16)
     small_ref[12:13] = jnp.sum(sum_gain, 0, keepdims=True)
     small_ref[13:14] = jnp.sum(sum_shift, 0, keepdims=True)
     small_ref[14:16] = jnp.zeros((2, chans), F32)
@@ -160,12 +180,11 @@
     part = GROUP // 8
     for group in range(3 * chans // GROUP):
         lanes = jnp.dot(patch_ref[:, group * GROUP : (group + 1) * GROUP], place, preferred_element_type=F32).astype(BF16)
-        grad = lax.dot_general(lanes, d_ref[...], over_rows, preferred_element_type=F32)
+        grad = lax.dot_general(lanes, sides_ref[...], over_rows, preferred_element_type=F32)
         for cube in range(8):
-            for side in range(2):
-                grad_ref[side, cube, group * part : (group + 1) * part] = grad[
-                    cube * part : (cube + 1) * part, side * half : (side + 1) * half
-                ]
+            block = grad[cube * part : (cube + 1) * part]
+            send_ref[cube, group * part : (group + 1) * part] = block[:, :half]
+            keep_ref[cube, group * part : (group + 1) * part] = block[:, half:]
 
     def spread(tap):
         return lax.dot_general(
@@ -198,16 +217,13 @@
     small_ref[0:10] = by_high[0:10] + by_high[20:30] + by_low[0:10]
     small_ref[10:11] = jnp.sum(sum_gain, 0, keepdims=True)
     small_ref[11:12] = jnp.sum(sum_shift, 0, keepdims=True)
-    last = grad_ref.shape[2]
-    for side in range(2):
+    last = keep_ref.shape[1] - 8
+    for out_ref, owner in ((keep_ref, core), (send_ref, 1 - core)):
         for cube in range(8):
-            row = small_ref[8 * side + cube : 8 * side + cube + 1]
-            grad_ref[side, cube, last - 8 : last - 7] = row[:, :half]
-            grad_ref[side, cube, last - 7 : last - 6] = row[:, half:]
-            grad_ref[side, cube, last - 6 :] = jnp.zeros((6, half), F32)
-    core = meta_ref[1]
-    keep_ref[...] = grad_ref[core]
-    send_ref[...] = grad_ref[1 - core]
+            row = small_ref[pl.ds(8 * owner + cube, 1)]
+            out_ref[cube, last : last + 1] = row[:, :half]
+            out_ref[cube, last + 1 : last + 2] = row[:, half:]
+            out_ref[cube, last + 2 :] = jnp.zeros((6, half), F32)
 
 
 HBM = pl.BlockSpec(memory_space=pltpu.HBM)
@@ -235,10 +251,8 @@
     start = position * samples_dev
     sample_pos = start + lax.broadcasted_iota(jnp.int32, (1, samples_dev), 1)
 
-    lane = lax.broadcasted_iota(jnp.int32, (1, 10), 1)
-    first = jnp.where(start + lane < length, waveform[:, :10], 0.0)
-    rim_odd = jnp.pad(first[:, :5], ((0, 0), (5, 0)))
-    rim = jnp.concatenate([jnp.tile(rim_odd, (1, 3)), jnp.tile(first, (1, 3))], 0)
+    lane = lax.broadcasted_iota(jnp.int32, (1, 128), 1)
+    rim = jnp.where((lane < 10) & (start + lane < length), waveform[:, :128], 0.0)
     back = []
     for i in range(int(np.prod(SHAPE))):
         if i % 64:
@@ -277,7 +291,7 @@
             pltpu.VMEM((rows, chans), BF16),
             pltpu.VMEM((rows, chans), BF16),
             pltpu.VMEM((16, chans), F32),
-            pltpu.VMEM((2, 8, 200, half), F32),
+            pltpu.VMEM((frames, chans), BF16),
             pltpu.VMEM((32, chans), F32),
             pltpu.VMEM((10, chans), F32),
             pltpu.VMEM((1, chans), F32),
@@ -309,7 +323,7 @@
     )
     send, first_core = lax.optimization_barrier((send, core == 0))
     mine = keep + lax.ppermute(send, "core", [(0, 1), (1, 0)])
-    mine = jnp.sum(lax.all_to_all(mine, CUBE, 0, 0, tiled=True), 0)
+    mine = jnp.sum(lax.all_to_all(mine, AXES, 0, 0, axis_index_groups=cubes(), tiled=True), 0)
     line = mine[192:194].reshape(1, chans)
     message = jnp.concatenate([mine[:192].reshape(64, 3 * half), jnp.broadcast_to(line, (64, chans))], 1)
     mine = jnp.sum(lax.all_to_all(message, CUBES, 0, 0, tiled=True), 0)

time: 105 us -> 95.7 us (0.911)
  starting transfers between devices: 25.2 us -> 21.4 us
  blocking collectives: 57 us -> 54 us
    all_to_all x1, blocking collectives: 32.9 us -> 27.1 us  [shards(): mine = jnp.sum(lax.all_to_all(message, CUBES, 0, 0, tiled=True), 0)]
    all_to_all x1, starting transfers between devices: 7.17 us -> 3.38 us  [shards(): gathered = lax.all_to_all(message, ('core',) + CUBE, 0, 0, tiled=True)]
    all_to_all x1, blocking collectives: 24.1 us -> 26.9 us  [shards(): lax.all_to_all(mine, AXES, 0, 0, axis_index_groups=cubes(), tiled=True)]
  transfers between devices with their start and end apart: 3 -> 3, of which waited for: 2 -> 2; matrix products, arithmetic and copies ran while one was open for 1% -> 2% of each run, Pallas kernels for 0% -> 0%
where the time goes in v4:
time: 95.7 us; the launch traced here: 95.3 us
  blocking collectives  54 us (56%)
  starting transfers between devices  21.4 us (22%)
  waiting for transfers between devices  7.73 us (8%)
  Pallas kernels  5.72 us (6%)
  other arithmetic  2.75 us (3%)
  local copies, waits for them, and re-layouts  2.23 us (2%)
  between operations  1.5 us (2%)
    all_to_all x1, blocking collectives, shards(): mine = jnp.sum(lax.all_to_all(message, CUBES, 0, 0, tiled=True), 0)  27.1 us
    all_to_all x1, blocking collectives, shards(): lax.all_to_all(mine, AXES, 0, 0, axis_index_groups=cubes(), tiled=True)  26.9 us
    ppermute x1, starting transfers between devices, shards(): rim = lax.ppermute(rim, AXES, back)  16.1 us
    pallas_call x1, Pallas kernels, shards(): pl.pallas_call(functools.partial(step_kernel, frames, chunk), out_shape=(...  5.72 us
    all_to_all x1, waiting for transfers between devices, shards(): gathered = lax.all_to_all(message, ('core',) + CUBE, 0, 0, tiled=True)  4.25 us
    ppermute x1, waiting for transfers between devices, shards(): mine = keep + lax.ppermute(send, 'core', [(0, 1), (1, 0)])  3.47 us
    all_to_all x1, starting transfers between devices, shards(): gathered = lax.all_to_all(message, ('core',) + CUBE, 0, 0, tiled=True)  3.38 us
    ppermute x1, starting transfers between devices, shards(): mine = keep + lax.ppermute(send, 'core', [(0, 1), (1, 0)])  1.92 us
  transfers between devices with their start and end apart: 3, of which 2 were waited for; matrix products, arithmetic and copies ran while one was open for 2% of the time, Pallas kernels for 0%

profile of v4, /device:TPU:1, one launch (start us, length us, event | category | flops | bytes accessed | tf_op | source)
XLA Modules:
  0.0 95.3 jit_solution(18320718792179658731)
XLA Ops:
  1.3 0.7 and_select_fusion
  2.0 16.1 %collective-permute-start = (f32[1,128]{1,0:T(1,128)S(1)}, f32[1,128]{1,0:T(1,128)S(1)}, u32[]{:S(2)}, u32[]{:S(2)}) collective-permute-start(f32[1,128]{1,0:T(1,128)S(1)} %and_select_fusion), channel_id=1, source_target_pairs={{1,0},{2,1},{3,2},{4,3},{5,4},{6,5},{7,6},{8,7},{9,8},{10,9},{11,1... | collective-permute-start | bytes 1544 | tf_op jit(solution)/shard_map/ppermute | solution.py:260
  18.0 0.7 fusion.3
  18.8 0.1 slice_reduce_fusion
  18.9 0.1 reshape.83
  19.0 0.1 copy.12
  19.1 0.1 reshape_squeeze.3
  19.2 0.1 copy.13
  19.3 0.1 maximum_maximum_fusion
  19.4 0.1 pad_add_fusion.meta_ref
  19.5 0.1 copy.14.x3_ref
  19.6 0.0 collective-permute-done.rim_ref
  19.7 5.7 %step.1 = (bf16[176,512]{1,0:T(8,128)(2,1)}, f32[8,200,256]{2,1,0:T(8,128)S(1)}, f32[8,200,256]{2,1,0:T(8,128)S(1)}) custom-call(s32[2]{0:T(128)S(1)} %pad_add_fusion.meta_ref, f32[368,30]{1,0:T(8,128)S(1)} %copy.14.x3_ref, f32[1,128]{1,0:T(1,128)S(1)} %collective-permute-done.rim_ref, f32[10,512]{1,0:T(8,128)} %w0_hbm.1, f32[1,512]{1,0:T(1,128)} %bitcast.27, ...), custom_call_target="tpu_custom_call" | custom-call | tf_op jit(solution)/shard_map/step/pallas_call | solution.py:272
  25.4 1.9 %collective-permute-start.1 = (f32[8,200,256]{2,1,0:T(8,128)S(1)}, f32[8,200,256]{2,1,0:T(8,128)S(1)}, u32[]{:S(2)}, u32[]{:S(2)}) collective-permute-start(f32[8,200,256]{2,1,0:T(8,128)S(1)} %get-tuple-element.12), channel_id=1, source_target_pairs={{0,1},{1,0},{2,3},{3,2},{4,5},{5,4},{6,7},{7,6},{8,9},{9,8},{10,11... | collective-permute-start | bytes 4915208 | tf_op jit(solution)/shard_map/ppermute | solution.py:325
  27.3 3.5 %collective-permute-done.1 = f32[8,200,256]{2,1,0:T(8,128)S(1)} collective-permute-done((f32[8,200,256]{2,1,0:T(8,128)S(1)}, f32[8,200,256]{2,1,0:T(8,128)S(1)}, u32[]{:S(2)}, u32[]{:S(2)}) %collective-permute-start.1) | collective-permute-done | bytes 1638432 | tf_op jit(solution)/shard_map/ppermute | solution.py:325
  30.8 0.2 add.66
  31.0 26.9 %all_to_all.23 = f32[8,200,256]{2,1,0:T(8,128)S(1)} all-to-all(f32[8,200,256]{2,1,0:T(8,128)S(1)} %add.66), channel_id=1, replica_groups={{0,2,16,18,64,66,80,82},{1,15,561,575,449,463,1009,1023},{5,3,565,563,4..., dimensions={0} | all-to-all | bytes 3276800 | tf_op jit(solution)/shard_map/all_to_all | solution.py:326
  57.9 0.1 reduce_sum.18
  58.0 0.1 reshape.89
  58.2 0.2 all_to_all.16
  58.4 27.1 %all_to_all.24 = f32[64,1,1280]{2,1,0:T(1,128)S(1)} all-to-all(f32[64,1,1280]{2,1,0:T(1,128)S(1)} %all_to_all.16), channel_id=1, replica_groups=mesh['zh'=2,'yh'=4,'y0'=2,'z1'=2,'z0'=2,'xh'=4,'x0'=2,'core'=2] {'zh','y..., dimensions={0} | all-to-all | bytes 655360 | tf_op jit(solution)/shard_map/all_to_all | solution.py:329
  85.5 0.2 reduce_sum.19
  85.8 0.6 broadcast_in_dim.33
  86.4 3.4 %all-to-all-start.2 = ((f32[16,1,768]{2,1,0:T(1,128)}), f32[16,1,768]{2,1,0:T(1,128)S(1)}, u32[]{:S(2)}, u32[]{:S(2)}) async-start(f32[16,1,768]{2,1,0:T(1,128)} %broadcast_in_dim.33), calls=%async_computation.2 | async-start | bytes 98304 | tf_op jit(solution)/shard_map/all_to_all | solution.py:333
  89.8 4.3 %all-to-all-done.2 = f32[16,1,768]{2,1,0:T(1,128)S(1)} async-done(((f32[16,1,768]{2,1,0:T(1,128)}), f32[16,1,768]{2,1,0:T(1,128)S(1)}, u32[]{:S(2)}, u32[]{:S(2)}) %all-to-all-start.2) | async-done | bytes 49184 | tf_op jit(solution)/shard_map/all_to_all | solution.py:333
  94.1 0.6 slice.57
  94.7 0.6 fusion.1
  (12 shorter events, 0.1 us)
Async XLA Ops:
  2.0 17.7 %collective-permute-start = (f32[1,128]{1,0:T(1,128)S(1)}, f32[1,128]{1,0:T(1,128)S(1)}, u32[]{:S(2)}, u32[]{:S(2)}) collective-permute-start(f32[1,128]{1,0:T(1,128)S(1)} %and_select_fusion), channel_id=1, source_target_pairs={{1,0},{2,1},{3,2},{4,3},{5,4},{6,5},{7,6},{8,7},{9,8},{10,9},{11,1... | collective-permute-start | bytes 1544 | tf_op jit(solution)/shard_map/ppermute | solution.py:260
  25.4 5.4 %collective-permute-start.1 = (f32[8,200,256]{2,1,0:T(8,128)S(1)}, f32[8,200,256]{2,1,0:T(8,128)S(1)}, u32[]{:S(2)}, u32[]{:S(2)}) collective-permute-start(f32[8,200,256]{2,1,0:T(8,128)S(1)} %get-tuple-element.12), channel_id=1, source_target_pairs={{0,1},{1,0},{2,3},{3,2},{4,5},{5,4},{6,7},{7,6},{8,9},{9,8},{10,11... | collective-permute-start | bytes 4915208 | tf_op jit(solution)/shard_map/ppermute | solution.py:325
  86.4 7.7 %all-to-all-start.2 = ((f32[16,1,768]{2,1,0:T(1,128)}), f32[16,1,768]{2,1,0:T(1,128)S(1)}, u32[]{:S(2)}, u32[]{:S(2)}) async-start(f32[16,1,768]{2,1,0:T(1,128)} %broadcast_in_dim.33), calls=%async_computation.2 | async-start | bytes 98304 | tf_op jit(solution)/shard_map/all_to_all | solution.py:333

commit v5 on v4

--- a/solution.py
+++ b/solution.py
@@ -9,29 +9,34 @@
 from jax.sharding import Mesh
 from jax.sharding import PartitionSpec as P
 
-SHAPE = (2, 4, 2, 2, 2, 4, 2, 2)
-AXES = ("zh", "yh", "y0", "z1", "z0", "xh", "x0", "core")
+SHAPE = (2,) * 10
+AXES = ("z2", "y2", "y1", "y0", "z1", "z0", "x2", "x1", "x0", "core")
+DP, AUDIO = AXES[:4], AXES[4:]
 CUBE = ("y0", "z0", "x0")
-CUBES = ("zh", "yh", "z1", "xh")
+FAR = ("z2", "y2", "x2")
 GROUP = 384
 EPS = 1e-05
 BF16, F32 = jnp.bfloat16, jnp.float32
 
 
-def cubes():
+def cubes(bit):
     groups = {}
-    for i in range(int(np.prod(SHAPE))):
-        zh, yh, y0, z1, z0, xh, x0, core = (int(v) for v in np.unravel_index(i, SHAPE))
-        z, y, x = zh * 4 + z1 * 2 + z0, yh * 2 + y0, xh * 2 + x0
-        cube = tuple(((v - core) % 8) // 2 for v in (z, y, x)) + (core,)
-        groups.setdefault(cube, [0] * 8)[(y0 * 2 + z0) * 2 + x0] = i
+    for i in range(2 ** len(AXES)):
+        at = dict(zip(AXES, (int(v) for v in np.unravel_index(i, SHAPE))))
+        group, member = [at["core"]], 0
+        for axis in "yzx":
+            place = sum(at[f"{axis}{n}"] << n for n in range(3))
+            moved = (place - (at["core"] << bit)) % 8
+            group.append(moved & ~(1 << bit))
+            member = member * 2 + ((place >> bit) & 1)
+        groups.setdefault(tuple(group), [0] * 8)[member] = i
     return list(groups.values())
 
 
 def row_order(place):
     chunk = (place * 171) >> 9
     row = place - 3 * chunk
-    for source, target in ((6, 5), (5, 3), (4, 0), (3, 6), (2, 4), (1, 2), (0, 1)):
+    for source, target in ((6, 5), (5, 3), (4, 0), (3, 6), (2, 4), (1, 1), (0, 2)):
         row = row + (((chunk >> source) & 1) << target) * 3
     return row
 
@@ -44,26 +49,31 @@
     return jnp.exp(v * v * np.float32(-0.5)) * np.float32((2 * np.pi) ** -0.5)
 
 
-def split_patches(x3_ref, rim_ref, odd_last, even_last):
-    value = x3_ref[...]
-    width = value.shape[1]
-    rim = jnp.broadcast_to(rim_ref[...], (8, 128))
-    five = jnp.where(lax.broadcasted_iota(jnp.int32, rim.shape, 1) < 5, rim, 0.0)
-    even = rim + pltpu.roll(rim, 10, 1) + pltpu.roll(rim, 20, 1)
-    odd = pltpu.roll(five, 5, 1) + pltpu.roll(five, 15, 1) + pltpu.roll(five, 25, 1)
-    row = lax.broadcasted_iota(jnp.int32, value.shape, 0)
-    lane = lax.broadcasted_iota(jnp.int32, value.shape, 1)
-    value = jnp.where(row == odd_last, value + odd[0:1, :width], value)
-    value = jnp.where(row == even_last, value + even[0:1, :width], value)
-    high = value.astype(BF16).astype(F32)
-    return jnp.where(lane < 20, high, value - high).astype(BF16)
+def fill_patches(block_ref, rim_ref, ext_ref, xs_ref, start, length):
+    frames = block_ref.shape[0]
+    row = lax.broadcasted_iota(jnp.int32, (frames, 10), 0)
+    lane = lax.broadcasted_iota(jnp.int32, (frames, 10), 1)
+    ext_ref[...] = jnp.zeros_like(ext_ref)
+    ext_ref[0:frames, 0:10] = jnp.where(start + row * 10 + lane < length, block_ref[...], 0.0)
+    lane = lax.broadcasted_iota(jnp.int32, (1, 128), 1)
+    rim = jnp.where((lane < 10) & (start + frames * 10 + lane < length), rim_ref[:, :128], 0.0)
+    ext_ref[frames : frames + 1] = rim
+    here, after = ext_ref[...], ext_ref[1 : frames + 1]
+    lane = lax.broadcasted_iota(jnp.int32, (frames, 128), 1)
+    later = jnp.where(lane < 5, after, 0.0)
+    odd = pltpu.roll(jnp.where(lane >= 5, here[:frames], 0.0), 123, 1) + pltpu.roll(later, 5, 1)
+    for at, value in ((0, odd), (frames, here)):
+        value = value + pltpu.roll(value, 10, 1) + pltpu.roll(value, 20, 1)
+        high = value.astype(BF16).astype(F32)
+        lane = lax.broadcasted_iota(jnp.int32, value.shape, 1)
+        xs_ref[at : at + value.shape[0]] = jnp.where(lane < 20, high, value - high).astype(BF16)
 
 
 def step_kernel(
     frames,
     chunk,
-    meta_ref,
-    x3_ref,
+    length_ref,
+    block_ref,
     rim_ref,
     w0_hbm,
     gain0_hbm,
@@ -88,6 +98,8 @@
     dlow_ref,
     small_ref,
     sides_ref,
+    ext_ref,
+    xs_ref,
     taps_ref,
     w0_ref,
     gain0_ref,
@@ -106,9 +118,12 @@
         arriving[-1].start()
     chans = w1_ref.shape[1]
     half = chans // 2
-    rows = x3_ref.shape[0]
-    core = meta_ref[1]
-    xs = split_patches(x3_ref, rim_ref, frames - 1, 2 * frames)
+    rows = pre0_ref.shape[0]
+    core = lax.axis_index("core")
+    position = lax.axis_index(AUDIO)
+    length = length_ref[0]
+    fill_patches(block_ref, rim_ref, ext_ref, xs_ref, position * (frames * 10), length)
+    xs = xs_ref[:, :30]
     arriving[0].wait()
     w0 = w0_ref[...]
     w0 = w0 - jnp.mean(w0, -1, keepdims=True)
@@ -155,7 +170,7 @@
         v = xhat * gain1 + shift1
         cdf = normal_cdf(v)
         frame = at + lax.broadcasted_iota(jnp.int32, (chunk, chans), 0)
-        valid = frame < meta_ref[0]
+        valid = (position * frames + frame) * 10 + 10 <= length
         feat_ref[at : at + chunk] = jnp.where(valid, v * cdf, 0.0).astype(BF16)
         dv = cot_ref[at : at + chunk].astype(F32) * (cdf + v * normal_pdf(v))
         dv = jnp.where(valid, dv, 0.0)
@@ -226,6 +241,43 @@
             out_ref[cube, last + 2 :] = jnp.zeros((6, half), F32)
 
 
+def near_kernel(cube_ref, out_ref, sum_ref):
+    sum_ref[...] = jnp.sum(cube_ref[...], 0)
+    for target in range(8):
+        for group in range(4):
+            at = group * 48 + target * 6
+            out_ref[target, group * 6 : group * 6 + 6] = sum_ref[at : at + 6]
+        out_ref[target, 24:26] = sum_ref[192:194]
+
+
+def far_kernel(near_ref, out_ref, sum_ref):
+    sum_ref[...] = jnp.sum(near_ref[...], 0)
+    for target in range(8):
+        out_ref[target, 0:3] = sum_ref[target * 3 : target * 3 + 3]
+        out_ref[target, 3:5] = sum_ref[24:26]
+
+
+def share_kernel(far_ref, out_ref, kept_ref, sum_ref):
+    sum_ref[...] = jnp.sum(far_ref[...], 0)
+    first = lax.axis_index("core") == 0
+    out_ref[:, 0:2] = jnp.broadcast_to(sum_ref[3:5][None], (16, 2, out_ref.shape[2]))
+    other = jnp.where(first, sum_ref[2:3], sum_ref[0:1])
+    out_ref[:, 2:3] = jnp.broadcast_to(other[None], (16, 1, out_ref.shape[2]))
+    kept_ref[0:1] = jnp.where(first, sum_ref[0:1], sum_ref[1:2])
+    kept_ref[1:2] = jnp.where(first, sum_ref[1:2], sum_ref[2:3])
+
+
+def final_kernel(peer_ref, all_ref, kept_ref, grad_ref, small_ref):
+    half = all_ref.shape[2]
+    got = all_ref[peer_ref[0]][2:3]
+    grad_ref[0:1] = kept_ref[0:1]
+    grad_ref[1:2] = got
+    grad_ref[2:3] = kept_ref[1:2]
+    for row in range(14):
+        small_ref[row : row + 1, :half] = all_ref[row, 0:1]
+        small_ref[row : row + 1, half:] = all_ref[row, 1:2]
+
+
 HBM = pl.BlockSpec(memory_space=pltpu.HBM)
 VMEM = pl.BlockSpec(memory_space=pltpu.VMEM)
 SMEM = pl.BlockSpec(memory_space=pltpu.SMEM)
@@ -242,30 +294,14 @@
     norm1_shift,
     cotangent,
 ):
-    position = lax.axis_index(("z1", "z0", "xh", "x0", "core"))
-    core = lax.axis_index("core")
-    samples_dev = waveform.shape[1]
-    frames = samples_dev // 10
+    frames = waveform.shape[1] // 10
     chans = conv1_weight.shape[2]
-    length = lengths[0]
-    start = position * samples_dev
-    sample_pos = start + lax.broadcasted_iota(jnp.int32, (1, samples_dev), 1)
-
-    lane = lax.broadcasted_iota(jnp.int32, (1, 128), 1)
-    rim = jnp.where((lane < 10) & (start + lane < length), waveform[:, :128], 0.0)
+    rows = 2 * frames + 16
     back = []
-    for i in range(int(np.prod(SHAPE))):
-        if i % 64:
+    for i in range(2 ** len(AXES)):
+        if i % 2 ** len(AUDIO):
             back.append((i, i - 1))
-    rim = lax.ppermute(rim, AXES, back)
-
-    cleaned = jnp.where(sample_pos < length, waveform, 0.0)[0]
-    odd = jnp.concatenate([cleaned[5:], jnp.zeros((5,), F32)]).reshape(frames, 10)
-    even = cleaned.reshape(frames, 10)
-    rows = 2 * frames + 16
-    patches = jnp.concatenate([odd, even, jnp.zeros((16, 10), F32)], 0)
-    x3 = jnp.concatenate([patches, patches, patches], 1)
-    meta = jnp.stack([length // 10 - position * frames, core]).astype(jnp.int32)
+    rim = lax.ppermute(waveform, AXES, back)
     half = chans // 2
     chunk = 16
     shape = jax.ShapeDtypeStruct
@@ -292,6 +328,8 @@
             pltpu.VMEM((rows, chans), BF16),
             pltpu.VMEM((16, chans), F32),
             pltpu.VMEM((frames, chans), BF16),
+            pltpu.VMEM((frames + 16, 128), F32),
+            pltpu.VMEM((rows, 128), BF16),
             pltpu.VMEM((32, chans), F32),
             pltpu.VMEM((10, chans), F32),
             pltpu.VMEM((1, chans), F32),
@@ -305,8 +343,8 @@
         compiler_params=pltpu.CompilerParams(vmem_limit_bytes=32 << 20),
         name="step",
     )(
-        meta,
-        x3,
+        lengths,
+        waveform.reshape(frames, 10),
         rim,
         *(
             pltpu.with_memory_space_constraint(operand, pltpu.HBM)
@@ -321,30 +359,39 @@
             )
         ),
     )
-    send, first_core = lax.optimization_barrier((send, core == 0))
     mine = keep + lax.ppermute(send, "core", [(0, 1), (1, 0)])
-    mine = jnp.sum(lax.all_to_all(mine, AXES, 0, 0, axis_index_groups=cubes(), tiled=True), 0)
-    line = mine[192:194].reshape(1, chans)
-    message = jnp.concatenate([mine[:192].reshape(64, 3 * half), jnp.broadcast_to(line, (64, chans))], 1)
-    mine = jnp.sum(lax.all_to_all(message, CUBES, 0, 0, tiled=True), 0)
-    part, line = mine[: 3 * half].reshape(3, half), mine[3 * half :]
-    out = jnp.where(first_core, part[2], part[0])
-    message = jnp.broadcast_to(jnp.concatenate([line, out])[None], (16, chans + half))
+    small_call = functools.partial(pl.pallas_call, compiler_params=pltpu.CompilerParams(vmem_limit_bytes=8 << 20))
+
+    def stage(kernel, value, shapes, sums, operands=()):
+        return small_call(
+            kernel,
+            out_shape=[shape(s, F32) for s in shapes],
+            in_specs=[VMEM] * (1 + len(operands)),
+            out_specs=[VMEM] * len(shapes),
+            scratch_shapes=[pltpu.VMEM(sums, F32)],
+            name=kernel.__name__,
+        )(value, *operands)
+
+    mine = lax.all_to_all(mine, AXES, 0, 0, axis_index_groups=cubes(0), tiled=True)
+    (mine,) = stage(near_kernel, mine, [(8, 26, half)], (200, half))
+    mine = lax.all_to_all(mine, AXES, 0, 0, axis_index_groups=cubes(1), tiled=True)
+    (mine,) = stage(far_kernel, mine, [(8, 5, half)], (26, half))
+    mine = lax.all_to_all(mine, FAR, 0, 0, tiled=True)
+    message, kept = stage(share_kernel, mine, [(16, 3, half), (2, half)], (5, half))
     gathered = lax.all_to_all(message, ("core",) + CUBE, 0, 0, tiled=True)
-    small_grads = gathered[:14, :chans]
-    peer = (1 - core) * 8 + lax.axis_index(CUBE)
-    got = lax.dynamic_slice(gathered, (peer, chans), (1, half))[0]
-    conv1_grad = jnp.where(
-        first_core,
-        jnp.concatenate([part[0], got, part[1]]),
-        jnp.concatenate([part[1], got, part[2]]),
-    )
-    return (features[None], conv1_grad, small_grads)
+    peer = (1 - lax.axis_index("core")) * 8 + lax.axis_index(CUBE)
+    conv1_grad, small_grads = small_call(
+        final_kernel,
+        out_shape=[shape((3, half), F32), shape((14, chans), F32)],
+        in_specs=[SMEM, VMEM, VMEM],
+        out_specs=[VMEM, VMEM],
+        name="final_kernel",
+    )(peer.astype(jnp.int32).reshape(1), gathered, kept)
+    return (features[None], conv1_grad.reshape(-1), small_grads)
 
 
 def solution(mesh):
     torus = Mesh(mesh.devices.reshape(SHAPE), AXES)
-    dp, audio = AXES[:3], AXES[3:]
-    in_specs = (P(dp, audio), P(dp), P(), P(), P(), P(), P(), P(), P(dp, audio, None))
-    out_specs = (P(dp, audio, None), P(dp + audio), P())
+    in_specs = (P(DP, AUDIO), P(DP), P(), P(), P(), P(), P(), P(), P(DP, AUDIO, None))
+    out_specs = (P(DP, AUDIO, None), P(DP + AUDIO), P())
     return jax.shard_map(shards, mesh=torus, in_specs=in_specs, out_specs=out_specs, check_vma=False)

time: 95.7 us -> 108 us (1.13)
  blocking collectives: 54 us -> 65.9 us
  other arithmetic: 2.75 us -> 0.93 us
  starting transfers between devices: 21.4 us -> 23.2 us
  local copies, waits for them, and re-layouts: 2.23 us -> 0.73 us
    all_to_all x2 -> x3, blocking collectives: 54 us -> 65.9 us  [the longest x1 26.9 us: shards(): lax.all_to_all(mine, AXES, 0, 0, axis_index_groups=cubes(0), tiled=True)]
    select_n x3 -> x0, other arithmetic: 1.99 us -> none  [the longest x1 0.73 us: shards(): cleaned = jnp.where(sample_pos < length, waveform, 0.0)[0]]
    all_to_all x1, starting transfers between devices: 3.38 us -> 5.25 us  [shards(): gathered = lax.all_to_all(message, ('core',) + CUBE, 0, 0, tiled=True)]
    pallas_call x0 -> x4, Pallas kernels: none -> 1.44 us  [the longest x3 0.81 us: stage(): small_call(kernel, out_shape=[shape(s, F32) for s in shapes], in_specs=[V...]
  transfers between devices with their start and end apart: 3 -> 3, of which waited for: 2 -> 2; matrix products, arithmetic and copies ran while one was open for 2% -> 1% of each run, Pallas kernels for 0% -> 0%
where the time goes in v5:
time: 108 us; the launch traced here: 107 us
  blocking collectives  65.9 us (61%)
  starting transfers between devices  23.2 us (21%)
  waiting for transfers between devices  8.39 us (8%)
  Pallas kernels  6.67 us (6%)
  between operations  1.33 us (1%)
    all_to_all x1, blocking collectives, shards(): lax.all_to_all(mine, AXES, 0, 0, axis_index_groups=cubes(0), tiled=True)  26.9 us
    all_to_all x1, blocking collectives, shards(): mine = lax.all_to_all(mine, FAR, 0, 0, tiled=True)  23.9 us
    ppermute x1, starting transfers between devices, shards(): rim = lax.ppermute(waveform, AXES, back)  16.1 us
    all_to_all x1, blocking collectives, shards(): lax.all_to_all(mine, AXES, 0, 0, axis_index_groups=cubes(1), tiled=True)  15.1 us
    all_to_all x1, starting transfers between devices, shards(): gathered = lax.all_to_all(message, ('core',) + CUBE, 0, 0, tiled=True)  5.25 us
    pallas_call x1, Pallas kernels, shards(): pl.pallas_call(functools.partial(step_kernel, frames, chunk), out_shape=(...  5.23 us
    all_to_all x1, waiting for transfers between devices, shards(): gathered = lax.all_to_all(message, ('core',) + CUBE, 0, 0, tiled=True)  4.92 us
    ppermute x1, waiting for transfers between devices, shards(): mine = keep + lax.ppermute(send, 'core', [(0, 1), (1, 0)])  3.47 us
  transfers between devices with their start and end apart: 3, of which 2 were waited for; matrix products, arithmetic and copies ran while one was open for 1% of the time, Pallas kernels for 0%

profile of v5, /device:TPU:1, one launch (start us, length us, event | category | flops | bytes accessed | tf_op | source)
XLA Modules:
  0.0 107.1 jit_solution(4549993420137380648)
XLA Ops:
  0.6 16.1 %collective-permute-start = (f32[1,1760]{1,0:T(1,128)}, f32[1,1760]{1,0:T(1,128)S(1)}, u32[]{:S(2)}, u32[]{:S(2)}) collective-permute-start(f32[1,1760]{1,0:T(1,128)} %param.9), channel_id=1, source_target_pairs={{1,0},{2,1},{3,2},{4,3},{5,4},{6,5},{7,6},{8,7},{9,8},{10,9},{11,1... | collective-permute-start | bytes 21128 | tf_op jit(solution)/shard_map/ppermute | solution.py:304
  17.3 0.7 reduce
  18.1 0.1 reshape.30.block_ref
  18.2 0.0 collective-permute-done.rim_ref
  18.2 5.2 %step.1 = (bf16[176,512]{1,0:T(8,128)(2,1)}, f32[8,200,256]{2,1,0:T(8,128)S(1)}, f32[8,200,256]{2,1,0:T(8,128)S(1)}) custom-call(s32[1]{0:T(128)S(6)} %copy.12.length_ref, f32[176,10]{1,0:T(8,128)S(1)} %reshape.30.block_ref, f32[1,1760]{1,0:T(1,128)S(1)} %collective-permute-done.rim_ref, f32[10,512]{1,0:T(8,128)} %w0_hbm.1, f32[1,512]{1,0:T(1,128)} %bitcast.10, ...), custom_call_target="tpu_custom_call" | custom-call | tf_op jit(solution)/shard_map/step/pallas_call | solution.py:308
  23.5 1.9 %collective-permute-start.1 = (f32[8,200,256]{2,1,0:T(8,128)S(1)}, f32[8,200,256]{2,1,0:T(8,128)S(1)}, u32[]{:S(2)}, u32[]{:S(2)}) collective-permute-start(f32[8,200,256]{2,1,0:T(8,128)S(1)} %get-tuple-element.12), channel_id=1, source_target_pairs={{0,1},{1,0},{2,3},{3,2},{4,5},{5,4},{6,7},{7,6},{8,9},{9,8},{10,11... | collective-permute-start | bytes 4915208 | tf_op jit(solution)/shard_map/ppermute | solution.py:362
  25.4 3.5 %collective-permute-done.1 = f32[8,200,256]{2,1,0:T(8,128)S(1)} collective-permute-done((f32[8,200,256]{2,1,0:T(8,128)S(1)}, f32[8,200,256]{2,1,0:T(8,128)S(1)}, u32[]{:S(2)}, u32[]{:S(2)}) %collective-permute-start.1) | collective-permute-done | bytes 1638432 | tf_op jit(solution)/shard_map/ppermute | solution.py:362
  28.9 0.2 add.15
  29.1 26.9 %all_to_all.20.cube_ref = f32[8,200,256]{2,1,0:T(8,128)S(1)} all-to-all(f32[8,200,256]{2,1,0:T(8,128)S(1)} %add.15), channel_id=1, replica_groups={{0,2,16,18,64,66,80,82},{1,15,561,575,449,463,1009,1023},{5,3,565,563,4..., dimensions={0} | all-to-all | bytes 3276800 | tf_op jit(solution)/shard_map/all_to_all | solution.py:375
  56.0 0.1 near_kernel.1
  56.1 15.1 %all_to_all.21.near_ref = f32[8,26,256]{2,1,0:T(8,128)S(1)} all-to-all(f32[8,26,256]{2,1,0:T(8,128)S(1)} %near_kernel.1), channel_id=1, replica_groups={{0,4,32,36,128,132,160,164},{1,13,545,557,385,397,929,941},{2,6,34,38,1..., dimensions={0} | all-to-all | bytes 425984 | tf_op jit(solution)/shard_map/all_to_all | solution.py:377
  71.2 23.9 %all_to_all.22.far_ref = f32[8,5,256]{2,1,0:T(8,128)S(1)} all-to-all(f32[8,5,256]{2,1,0:T(8,128)S(1)} %far_kernel.1), channel_id=1, replica_groups=mesh['z2'=2,'y2'=2,'y1'=2,'y0'=2,'z1'=2,'z0'=2,'x2'=2,'x1'=2,'x0'=2,'cor..., dimensions={0} | all-to-all | bytes 81920 | tf_op jit(solution)/shard_map/all_to_all | solution.py:379
  95.1 0.6 share_kernel.1
  95.7 5.2 %all-to-all-start.3 = ((f32[16,3,256]{2,1,0:T(4,128)}), f32[16,3,256]{2,1,0:T(4,128)S(1)}, u32[]{:S(2)}, u32[]{:S(2)}) async-start(f32[16,3,256]{2,1,0:T(4,128)} %get-tuple-element.13), calls=%async_computation.3 | async-start | bytes 131072 | tf_op jit(solution)/shard_map/all_to_all | solution.py:381
  101.0 4.9 %all-to-all-done.3.all_ref = f32[16,3,256]{2,1,0:T(4,128)S(1)} async-done(((f32[16,3,256]{2,1,0:T(4,128)}), f32[16,3,256]{2,1,0:T(4,128)S(1)}, u32[]{:S(2)}, u32[]{:S(2)}) %all-to-all-start.3) | async-done | bytes 49184 | tf_op jit(solution)/shard_map/all_to_all | solution.py:381
  105.9 0.6 final_kernel.1
  106.5 0.6 reshape.37
  (1 shorter events, 0.0 us)
Async XLA Ops:
  0.6 17.6 %collective-permute-start = (f32[1,1760]{1,0:T(1,128)}, f32[1,1760]{1,0:T(1,128)S(1)}, u32[]{:S(2)}, u32[]{:S(2)}) collective-permute-start(f32[1,1760]{1,0:T(1,128)} %param.9), channel_id=1, source_target_pairs={{1,0},{2,1},{3,2},{4,3},{5,4},{6,5},{7,6},{8,7},{9,8},{10,9},{11,1... | collective-permute-start | bytes 21128 | tf_op jit(solution)/shard_map/ppermute | solution.py:304
  23.5 5.4 %collective-permute-start.1 = (f32[8,200,256]{2,1,0:T(8,128)S(1)}, f32[8,200,256]{2,1,0:T(8,128)S(1)}, u32[]{:S(2)}, u32[]{:S(2)}) collective-permute-start(f32[8,200,256]{2,1,0:T(8,128)S(1)} %get-tuple-element.12), channel_id=1, source_target_pairs={{0,1},{1,0},{2,3},{3,2},{4,5},{5,4},{6,7},{7,6},{8,9},{9,8},{10,11... | collective-permute-start | bytes 4915208 | tf_op jit(solution)/shard_map/ppermute | solution.py:362
  95.7 10.2 %all-to-all-start.3 = ((f32[16,3,256]{2,1,0:T(4,128)}), f32[16,3,256]{2,1,0:T(4,128)S(1)}, u32[]{:S(2)}, u32[]{:S(2)}) async-start(f32[16,3,256]{2,1,0:T(4,128)} %get-tuple-element.13), calls=%async_computation.3 | async-start | bytes 131072 | tf_op jit(solution)/shard_map/all_to_all | solution.py:381

commit v6 on v5

--- a/solution.py
+++ b/solution.py
@@ -13,22 +13,21 @@
 AXES = ("z2", "y2", "y1", "y0", "z1", "z0", "x2", "x1", "x0", "core")
 DP, AUDIO = AXES[:4], AXES[4:]
 CUBE = ("y0", "z0", "x0")
-FAR = ("z2", "y2", "x2")
+FAR = ("z2", "y2", "y1", "z1", "x2", "x1")
 GROUP = 384
 EPS = 1e-05
 BF16, F32 = jnp.bfloat16, jnp.float32
 
 
-def cubes(bit):
+def cubes():
     groups = {}
     for i in range(2 ** len(AXES)):
         at = dict(zip(AXES, (int(v) for v in np.unravel_index(i, SHAPE))))
         group, member = [at["core"]], 0
         for axis in "yzx":
             place = sum(at[f"{axis}{n}"] << n for n in range(3))
-            moved = (place - (at["core"] << bit)) % 8
-            group.append(moved & ~(1 << bit))
-            member = member * 2 + ((place >> bit) & 1)
+            group.append((place - at["core"]) % 8 // 2)
+            member = member * 2 + place % 2
         groups.setdefault(tuple(group), [0] * 8)[member] = i
     return list(groups.values())
 
@@ -36,7 +35,7 @@
 def row_order(place):
     chunk = (place * 171) >> 9
     row = place - 3 * chunk
-    for source, target in ((6, 5), (5, 3), (4, 0), (3, 6), (2, 4), (1, 1), (0, 2)):
+    for source, target in ((6, 5), (5, 3), (4, 0), (3, 6), (2, 4), (1, 2), (0, 1)):
         row = row + (((chunk >> source) & 1) << target) * 3
     return row
 
@@ -241,41 +240,36 @@
             out_ref[cube, last + 2 :] = jnp.zeros((6, half), F32)
 
 
-def near_kernel(cube_ref, out_ref, sum_ref):
+def cube_kernel(cube_ref, out_ref, sum_ref):
     sum_ref[...] = jnp.sum(cube_ref[...], 0)
-    for target in range(8):
-        for group in range(4):
-            at = group * 48 + target * 6
-            out_ref[target, group * 6 : group * 6 + 6] = sum_ref[at : at + 6]
-        out_ref[target, 24:26] = sum_ref[192:194]
-
-
-def far_kernel(near_ref, out_ref, sum_ref):
-    sum_ref[...] = jnp.sum(near_ref[...], 0)
-    for target in range(8):
-        out_ref[target, 0:3] = sum_ref[target * 3 : target * 3 + 3]
-        out_ref[target, 3:5] = sum_ref[24:26]
-
-
-def share_kernel(far_ref, out_ref, kept_ref, sum_ref):
-    sum_ref[...] = jnp.sum(far_ref[...], 0)
+    half = sum_ref.shape[1]
+    for target in range(64):
+        for row in range(3):
+            out_ref[target, :, row * half : (row + 1) * half] = sum_ref[3 * target + row : 3 * target + row + 1]
+    for row in range(2):
+        line = jnp.broadcast_to(sum_ref[192 + row : 193 + row][None], (64, 1, half))
+        out_ref[:, :, (3 + row) * half : (4 + row) * half] = line
+
+
+def share_kernel(far_ref, out_ref, kept_ref):
+    total = jnp.sum(far_ref[...], 0)
+    half = kept_ref.shape[1] // 2
     first = lax.axis_index("core") == 0
-    out_ref[:, 0:2] = jnp.broadcast_to(sum_ref[3:5][None], (16, 2, out_ref.shape[2]))
-    other = jnp.where(first, sum_ref[2:3], sum_ref[0:1])
-    out_ref[:, 2:3] = jnp.broadcast_to(other[None], (16, 1, out_ref.shape[2]))
-    kept_ref[0:1] = jnp.where(first, sum_ref[0:1], sum_ref[1:2])
-    kept_ref[1:2] = jnp.where(first, sum_ref[1:2], sum_ref[2:3])
+    a, b, c = (total[:, row * half : (row + 1) * half] for row in range(3))
+    message = jnp.concatenate([total[:, 3 * half :], jnp.where(first, c, a)], 1)
+    out_ref[...] = jnp.broadcast_to(message[None], out_ref.shape)
+    kept_ref[:, :half] = jnp.where(first, a, b)
+    kept_ref[:, half:] = jnp.where(first, b, c)
 
 
 def final_kernel(peer_ref, all_ref, kept_ref, grad_ref, small_ref):
-    half = all_ref.shape[2]
-    got = all_ref[peer_ref[0]][2:3]
-    grad_ref[0:1] = kept_ref[0:1]
-    grad_ref[1:2] = got
-    grad_ref[2:3] = kept_ref[1:2]
+    half = kept_ref.shape[1] // 2
+    got = all_ref[peer_ref[0]]
+    grad_ref[:, :half] = kept_ref[:, :half]
+    grad_ref[:, half : 2 * half] = got[:, 2 * half :]
+    grad_ref[:, 2 * half :] = kept_ref[:, half:]
     for row in range(14):
-        small_ref[row : row + 1, :half] = all_ref[row, 0:1]
-        small_ref[row : row + 1, half:] = all_ref[row, 1:2]
+        small_ref[row : row + 1] = all_ref[row, :, : 2 * half]
 
 
 HBM = pl.BlockSpec(memory_space=pltpu.HBM)
@@ -362,30 +356,31 @@
     mine = keep + lax.ppermute(send, "core", [(0, 1), (1, 0)])
     small_call = functools.partial(pl.pallas_call, compiler_params=pltpu.CompilerParams(vmem_limit_bytes=8 << 20))
 
-    def stage(kernel, value, shapes, sums, operands=()):
-        return small_call(
-            kernel,
-            out_shape=[shape(s, F32) for s in shapes],
-            in_specs=[VMEM] * (1 + len(operands)),
-            out_specs=[VMEM] * len(shapes),
-            scratch_shapes=[pltpu.VMEM(sums, F32)],
-            name=kernel.__name__,
-        )(value, *operands)
-
-    mine = lax.all_to_all(mine, AXES, 0, 0, axis_index_groups=cubes(0), tiled=True)
-    (mine,) = stage(near_kernel, mine, [(8, 26, half)], (200, half))
-    mine = lax.all_to_all(mine, AXES, 0, 0, axis_index_groups=cubes(1), tiled=True)
-    (mine,) = stage(far_kernel, mine, [(8, 5, half)], (26, half))
-    mine = lax.all_to_all(mine, FAR, 0, 0, tiled=True)
-    message, kept = stage(share_kernel, mine, [(16, 3, half), (2, half)], (5, half))
+    mine = lax.all_to_all(mine, AXES, 0, 0, axis_index_groups=cubes(), tiled=True)
+    message = small_call(
+        cube_kernel,
+        out_shape=shape((64, 1, 5 * half), F32),
+        in_specs=[VMEM],
+        out_specs=VMEM,
+        scratch_shapes=[pltpu.VMEM((200, half), F32)],
+        name="cube_sum",
+    )(mine)
+    mine = lax.all_to_all(message, FAR, 0, 0, tiled=True)
+    message, kept = small_call(
+        share_kernel,
+        out_shape=[shape((16, 1, 3 * half), F32), shape((1, 2 * half), F32)],
+        in_specs=[VMEM],
+        out_specs=[VMEM, VMEM],
+        name="far_sum",
+    )(mine)
     gathered = lax.all_to_all(message, ("core",) + CUBE, 0, 0, tiled=True)
     peer = (1 - lax.axis_index("core")) * 8 + lax.axis_index(CUBE)
     conv1_grad, small_grads = small_call(
         final_kernel,
-        out_shape=[shape((3, half), F32), shape((14, chans), F32)],
+        out_shape=[shape((1, 3 * half), F32), shape((14, chans), F32)],
         in_specs=[SMEM, VMEM, VMEM],
         out_specs=[VMEM, VMEM],
-        name="final_kernel",
+        name="outputs",
     )(peer.astype(jnp.int32).reshape(1), gathered, kept)
     return (features[None], conv1_grad.reshape(-1), small_grads)
 

time: 108 us -> 93.7 us (0.87)
  blocking collectives: 65.9 us -> 54.3 us
  starting transfers between devices: 23.2 us -> 21.4 us
    all_to_all x3 -> x2, blocking collectives: 65.9 us -> 54.3 us  [the longest x1 27.4 us: shards(): mine = lax.all_to_all(message, FAR, 0, 0, tiled=True)]
    all_to_all x1, starting transfers between devices: 5.25 us -> 3.39 us  [shards(): gathered = lax.all_to_all(message, ('core',) + CUBE, 0, 0, tiled=True)]
where the time goes in v6:
time: 93.7 us; the launch traced here: 93.3 us
  blocking collectives  54.3 us (58%)
  starting transfers between devices  21.4 us (23%)
  waiting for transfers between devices  7.77 us (8%)
  Pallas kernels  6.88 us (7%)
  other arithmetic  1.53 us (2%)
  between operations  1.35 us (1%)
    all_to_all x1, blocking collectives, shards(): mine = lax.all_to_all(message, FAR, 0, 0, tiled=True)  27.4 us
    all_to_all x1, blocking collectives, shards(): lax.all_to_all(mine, AXES, 0, 0, axis_index_groups=cubes(), tiled=True)  26.9 us
    ppermute x1, starting transfers between devices, shards(): rim = lax.ppermute(waveform, AXES, back)  16.1 us
    pallas_call x1, Pallas kernels, shards(): pl.pallas_call(functools.partial(step_kernel, frames, chunk), out_shape=(...  5.23 us
    all_to_all x1, waiting for transfers between devices, shards(): gathered = lax.all_to_all(message, ('core',) + CUBE, 0, 0, tiled=True)  4.3 us
    ppermute x1, waiting for transfers between devices, shards(): mine = keep + lax.ppermute(send, 'core', [(0, 1), (1, 0)])  3.47 us
    all_to_all x1, starting transfers between devices, shards(): gathered = lax.all_to_all(message, ('core',) + CUBE, 0, 0, tiled=True)  3.39 us
    ppermute x1, starting transfers between devices, shards(): mine = keep + lax.ppermute(send, 'core', [(0, 1), (1, 0)])  1.92 us
  transfers between devices with their start and end apart: 3, of which 2 were waited for; matrix products, arithmetic and copies ran while one was open for 1% of the time, Pallas kernels for 0%

profile of v6, /device:TPU:1, one launch (start us, length us, event | category | flops | bytes accessed | tf_op | source)
XLA Modules:
  0.0 93.3 jit_solution(420978860466802375)
XLA Ops:
  0.6 16.1 %collective-permute-start = (f32[1,1760]{1,0:T(1,128)}, f32[1,1760]{1,0:T(1,128)S(1)}, u32[]{:S(2)}, u32[]{:S(2)}) collective-permute-start(f32[1,1760]{1,0:T(1,128)} %param.9), channel_id=1, source_target_pairs={{1,0},{2,1},{3,2},{4,3},{5,4},{6,5},{7,6},{8,7},{9,8},{10,9},{11,1... | collective-permute-start | bytes 21128 | tf_op jit(solution)/shard_map/ppermute | solution.py:298
  17.3 0.7 reduce
  18.1 0.1 reshape.30.block_ref
  18.2 0.0 collective-permute-done.rim_ref
  18.2 5.2 %step.1 = (bf16[176,512]{1,0:T(8,128)(2,1)}, f32[8,200,256]{2,1,0:T(8,128)S(1)}, f32[8,200,256]{2,1,0:T(8,128)S(1)}) custom-call(s32[1]{0:T(128)S(6)} %copy.12.length_ref, f32[176,10]{1,0:T(8,128)S(1)} %reshape.30.block_ref, f32[1,1760]{1,0:T(1,128)S(1)} %collective-permute-done.rim_ref, f32[10,512]{1,0:T(8,128)} %w0_hbm.1, f32[1,512]{1,0:T(1,128)} %bitcast.10, ...), custom_call_target="tpu_custom_call" | custom-call | tf_op jit(solution)/shard_map/step/pallas_call | solution.py:302
  23.5 1.9 %collective-permute-start.1 = (f32[8,200,256]{2,1,0:T(8,128)S(1)}, f32[8,200,256]{2,1,0:T(8,128)S(1)}, u32[]{:S(2)}, u32[]{:S(2)}) collective-permute-start(f32[8,200,256]{2,1,0:T(8,128)S(1)} %get-tuple-element.12), channel_id=1, source_target_pairs={{0,1},{1,0},{2,3},{3,2},{4,5},{5,4},{6,7},{7,6},{8,9},{9,8},{10,11... | collective-permute-start | bytes 4915208 | tf_op jit(solution)/shard_map/ppermute | solution.py:356
  25.4 3.5 %collective-permute-done.1 = f32[8,200,256]{2,1,0:T(8,128)S(1)} collective-permute-done((f32[8,200,256]{2,1,0:T(8,128)S(1)}, f32[8,200,256]{2,1,0:T(8,128)S(1)}, u32[]{:S(2)}, u32[]{:S(2)}) %collective-permute-start.1) | collective-permute-done | bytes 1638432 | tf_op jit(solution)/shard_map/ppermute | solution.py:356
  28.9 0.2 add.15
  29.1 26.9 %all_to_all.15.cube_ref = f32[8,200,256]{2,1,0:T(8,128)S(1)} all-to-all(f32[8,200,256]{2,1,0:T(8,128)S(1)} %add.15), channel_id=1, replica_groups={{0,2,16,18,64,66,80,82},{1,15,561,575,449,463,1009,1023},{5,3,565,563,4..., dimensions={0} | all-to-all | bytes 3276800 | tf_op jit(solution)/shard_map/all_to_all | solution.py:359
  56.0 0.2 cube_sum.1
  56.2 27.4 %all_to_all.16.far_ref = f32[64,1,1280]{2,1,0:T(1,128)S(1)} all-to-all(f32[64,1,1280]{2,1,0:T(1,128)S(1)} %cube_sum.1), channel_id=1, replica_groups=mesh['z2'=2,'y2'=2,'y1'=2,'y0'=2,'z1'=2,'z0'=2,'x2'=2,'x1'=2,'x0'=2,'cor..., dimensions={0} | all-to-all | bytes 655360 | tf_op jit(solution)/shard_map/all_to_all | solution.py:368
  83.6 0.8 far_sum.1
  84.4 3.4 %all-to-all-start.2 = ((f32[16,1,768]{2,1,0:T(1,128)}), f32[16,1,768]{2,1,0:T(1,128)S(1)}, u32[]{:S(2)}, u32[]{:S(2)}) async-start(f32[16,1,768]{2,1,0:T(1,128)} %get-tuple-element.13), calls=%async_computation.2 | async-start | bytes 98304 | tf_op jit(solution)/shard_map/all_to_all | solution.py:376
  87.8 4.3 %all-to-all-done.2.all_ref = f32[16,1,768]{2,1,0:T(1,128)S(1)} async-done(((f32[16,1,768]{2,1,0:T(1,128)}), f32[16,1,768]{2,1,0:T(1,128)S(1)}, u32[]{:S(2)}, u32[]{:S(2)}) %all-to-all-start.2) | async-done | bytes 49184 | tf_op jit(solution)/shard_map/all_to_all | solution.py:376
  92.1 0.6 outputs.1
  92.7 0.6 reduce.1
Async XLA Ops:
  0.6 17.6 %collective-permute-start = (f32[1,1760]{1,0:T(1,128)}, f32[1,1760]{1,0:T(1,128)S(1)}, u32[]{:S(2)}, u32[]{:S(2)}) collective-permute-start(f32[1,1760]{1,0:T(1,128)} %param.9), channel_id=1, source_target_pairs={{1,0},{2,1},{3,2},{4,3},{5,4},{6,5},{7,6},{8,7},{9,8},{10,9},{11,1... | collective-permute-start | bytes 21128 | tf_op jit(solution)/shard_map/ppermute | solution.py:298
  23.5 5.4 %collective-permute-start.1 = (f32[8,200,256]{2,1,0:T(8,128)S(1)}, f32[8,200,256]{2,1,0:T(8,128)S(1)}, u32[]{:S(2)}, u32[]{:S(2)}) collective-permute-start(f32[8,200,256]{2,1,0:T(8,128)S(1)} %get-tuple-element.12), channel_id=1, source_target_pairs={{0,1},{1,0},{2,3},{3,2},{4,5},{5,4},{6,7},{7,6},{8,9},{9,8},{10,11... | collective-permute-start | bytes 4915208 | tf_op jit(solution)/shard_map/ppermute | solution.py:356
  84.4 7.7 %all-to-all-start.2 = ((f32[16,1,768]{2,1,0:T(1,128)}), f32[16,1,768]{2,1,0:T(1,128)S(1)}, u32[]{:S(2)}, u32[]{:S(2)}) async-start(f32[16,1,768]{2,1,0:T(1,128)} %get-tuple-element.13), calls=%async_computation.2 | async-start | bytes 98304 | tf_op jit(solution)/shard_map/all_to_all | solution.py:376

commit v7 on v5

--- a/solution.py
+++ b/solution.py
@@ -13,22 +13,22 @@
 AXES = ("z2", "y2", "y1", "y0", "z1", "z0", "x2", "x1", "x0", "core")
 DP, AUDIO = AXES[:4], AXES[4:]
 CUBE = ("y0", "z0", "x0")
-FAR = ("z2", "y2", "x2")
+FAR = ("z2", "y2", "y1", "z1")
+LAST = ("core", "y0", "z0", "x0", "x2", "x1")
 GROUP = 384
 EPS = 1e-05
 BF16, F32 = jnp.bfloat16, jnp.float32
 
 
-def cubes(bit):
+def cubes():
     groups = {}
     for i in range(2 ** len(AXES)):
         at = dict(zip(AXES, (int(v) for v in np.unravel_index(i, SHAPE))))
         group, member = [at["core"]], 0
         for axis in "yzx":
             place = sum(at[f"{axis}{n}"] << n for n in range(3))
-            moved = (place - (at["core"] << bit)) % 8
-            group.append(moved & ~(1 << bit))
-            member = member * 2 + ((place >> bit) & 1)
+            group.append((place - at["core"]) % 8 // 2)
+            member = member * 2 + place % 2
         groups.setdefault(tuple(group), [0] * 8)[member] = i
     return list(groups.values())
 
@@ -36,7 +36,7 @@
 def row_order(place):
     chunk = (place * 171) >> 9
     row = place - 3 * chunk
-    for source, target in ((6, 5), (5, 3), (4, 0), (3, 6), (2, 4), (1, 1), (0, 2)):
+    for source, target in ((6, 5), (5, 3), (4, 0), (3, 6), (2, 4), (1, 2), (0, 1)):
         row = row + (((chunk >> source) & 1) << target) * 3
     return row
 
@@ -241,41 +241,37 @@
             out_ref[cube, last + 2 :] = jnp.zeros((6, half), F32)
 
 
-def near_kernel(cube_ref, out_ref, sum_ref):
+def cube_kernel(cube_ref, out_ref, sum_ref):
     sum_ref[...] = jnp.sum(cube_ref[...], 0)
-    for target in range(8):
-        for group in range(4):
-            at = group * 48 + target * 6
-            out_ref[target, group * 6 : group * 6 + 6] = sum_ref[at : at + 6]
-        out_ref[target, 24:26] = sum_ref[192:194]
-
-
-def far_kernel(near_ref, out_ref, sum_ref):
-    sum_ref[...] = jnp.sum(near_ref[...], 0)
-    for target in range(8):
-        out_ref[target, 0:3] = sum_ref[target * 3 : target * 3 + 3]
-        out_ref[target, 3:5] = sum_ref[24:26]
-
-
-def share_kernel(far_ref, out_ref, kept_ref, sum_ref):
+    small = jnp.concatenate([sum_ref[192:194], jnp.zeros((2, sum_ref.shape[1]), F32)], 0)
+    for target in range(16):
+        out_ref[target, 0:12] = sum_ref[12 * target : 12 * target + 12]
+        out_ref[target, 12:16] = small
+
+
+def far_kernel(far_ref, out_ref, sum_ref):
     sum_ref[...] = jnp.sum(far_ref[...], 0)
-    first = lax.axis_index("core") == 0
-    out_ref[:, 0:2] = jnp.broadcast_to(sum_ref[3:5][None], (16, 2, out_ref.shape[2]))
-    other = jnp.where(first, sum_ref[2:3], sum_ref[0:1])
-    out_ref[:, 2:3] = jnp.broadcast_to(other[None], (16, 1, out_ref.shape[2]))
-    kept_ref[0:1] = jnp.where(first, sum_ref[0:1], sum_ref[1:2])
-    kept_ref[1:2] = jnp.where(first, sum_ref[1:2], sum_ref[2:3])
-
-
-def final_kernel(peer_ref, all_ref, kept_ref, grad_ref, small_ref):
+    small = sum_ref[12:14]
+    for core in range(2):
+        for place in range(4):
+            at = 3 * place + core
+            message = jnp.concatenate([small, sum_ref[at : at + 2]], 0)
+            for cube in range(8):
+                out_ref[core * 32 + cube * 4 + place] = message
+
+
+def last_kernel(all_ref, grad_ref, small_ref, sum_ref):
     half = all_ref.shape[2]
-    got = all_ref[peer_ref[0]][2:3]
-    grad_ref[0:1] = kept_ref[0:1]
-    grad_ref[1:2] = got
-    grad_ref[2:3] = kept_ref[1:2]
+    sum_ref[...] = jnp.sum(all_ref[...].reshape(16, 4, 4, half), 1)
+    core, cube = lax.axis_index("core"), lax.axis_index(CUBE)
+    own = sum_ref[core * 8 + cube]
+    other = sum_ref[(1 - core) * 8 + cube]
+    grad_ref[0:half] = own[2]
+    grad_ref[half : 2 * half] = jnp.where(core == 0, other[2], other[3])
+    grad_ref[2 * half :] = own[3]
     for row in range(14):
-        small_ref[row : row + 1, :half] = all_ref[row, 0:1]
-        small_ref[row : row + 1, half:] = all_ref[row, 1:2]
+        small_ref[row : row + 1, :half] = sum_ref[row, 0:1]
+        small_ref[row : row + 1, half:] = sum_ref[row, 1:2]
 
 
 HBM = pl.BlockSpec(memory_space=pltpu.HBM)
@@ -362,32 +358,23 @@
     mine = keep + lax.ppermute(send, "core", [(0, 1), (1, 0)])
     small_call = functools.partial(pl.pallas_call, compiler_params=pltpu.CompilerParams(vmem_limit_bytes=8 << 20))
 
-    def stage(kernel, value, shapes, sums, operands=()):
+    def stage(kernel, value, shapes, sums):
         return small_call(
             kernel,
             out_shape=[shape(s, F32) for s in shapes],
-            in_specs=[VMEM] * (1 + len(operands)),
+            in_specs=[VMEM],
             out_specs=[VMEM] * len(shapes),
             scratch_shapes=[pltpu.VMEM(sums, F32)],
             name=kernel.__name__,
-        )(value, *operands)
-
-    mine = lax.all_to_all(mine, AXES, 0, 0, axis_index_groups=cubes(0), tiled=True)
-    (mine,) = stage(near_kernel, mine, [(8, 26, half)], (200, half))
-    mine = lax.all_to_all(mine, AXES, 0, 0, axis_index_groups=cubes(1), tiled=True)
-    (mine,) = stage(far_kernel, mine, [(8, 5, half)], (26, half))
+        )(value)
+
+    mine = lax.all_to_all(mine, AXES, 0, 0, axis_index_groups=cubes(), tiled=True)
+    (mine,) = stage(cube_kernel, mine, [(16, 16, half)], (200, half))
     mine = lax.all_to_all(mine, FAR, 0, 0, tiled=True)
-    message, kept = stage(share_kernel, mine, [(16, 3, half), (2, half)], (5, half))
-    gathered = lax.all_to_all(message, ("core",) + CUBE, 0, 0, tiled=True)
-    peer = (1 - lax.axis_index("core")) * 8 + lax.axis_index(CUBE)
-    conv1_grad, small_grads = small_call(
-        final_kernel,
-        out_shape=[shape((3, half), F32), shape((14, chans), F32)],
-        in_specs=[SMEM, VMEM, VMEM],
-        out_specs=[VMEM, VMEM],
-        name="final_kernel",
-    )(peer.astype(jnp.int32).reshape(1), gathered, kept)
-    return (features[None], conv1_grad.reshape(-1), small_grads)
+    (mine,) = stage(far_kernel, mine, [(64, 4, half)], (16, half))
+    mine = lax.all_to_all(mine, LAST, 0, 0, tiled=True)
+    conv1_grad, small_grads = stage(last_kernel, mine, [(3 * half,), (14, chans)], (16, 4, half))
+    return (features[None], conv1_grad, small_grads)
 
 
 def solution(mesh):

time: 108 us -> 94.1 us (0.87)
  starting transfers between devices: 23.2 us -> 18 us
  waiting for transfers between devices: 8.39 us -> 3.47 us
  blocking collectives: 65.9 us -> 63.9 us
    all_to_all x1, blocking collectives: 23.9 us -> 17.2 us  [shards(): mine = lax.all_to_all(mine, FAR, 0, 0, tiled=True)]
    all_to_all x1 -> x0, starting transfers between devices: 5.25 us -> none  [shards(): gathered = lax.all_to_all(message, ('core',) + CUBE, 0, 0, tiled=True)]
    all_to_all x1 -> x0, waiting for transfers between devices: 4.92 us -> none  [shards(): gathered = lax.all_to_all(message, ('core',) + CUBE, 0, 0, tiled=True)]
    all_to_all x2, blocking collectives: 42 us -> 46.7 us  [the longest x1 26.9 us: shards(): lax.all_to_all(mine, AXES, 0, 0, axis_index_groups=cubes(), tiled=True)]
  transfers between devices with their start and end apart: 3 -> 2, of which waited for: 2 -> 1; matrix products, arithmetic and copies ran while one was open for 1% -> 1% of each run, Pallas kernels for 0% -> 0%
where the time goes in v7:
time: 94.1 us; the launch traced here: 93.8 us
  blocking collectives  63.9 us (68%)
  starting transfers between devices  18 us (19%)
  Pallas kernels  6.07 us (6%)
  waiting for transfers between devices  3.47 us (4%)
  between operations  1.33 us (1%)
    all_to_all x1, blocking collectives, shards(): lax.all_to_all(mine, AXES, 0, 0, axis_index_groups=cubes(), tiled=True)  26.9 us
    all_to_all x1, blocking collectives, shards(): mine = lax.all_to_all(mine, LAST, 0, 0, tiled=True)  19.8 us
    all_to_all x1, blocking collectives, shards(): mine = lax.all_to_all(mine, FAR, 0, 0, tiled=True)  17.2 us
    ppermute x1, starting transfers between devices, shards(): rim = lax.ppermute(waveform, AXES, back)  16.1 us
    pallas_call x1, Pallas kernels, shards(): pl.pallas_call(functools.partial(step_kernel, frames, chunk), out_shape=(...  5.23 us
    ppermute x1, waiting for transfers between devices, shards(): mine = keep + lax.ppermute(send, 'core', [(0, 1), (1, 0)])  3.47 us
    ppermute x1, starting transfers between devices, shards(): mine = keep + lax.ppermute(send, 'core', [(0, 1), (1, 0)])  1.92 us
  transfers between devices with their start and end apart: 2, of which 1 were waited for; matrix products, arithmetic and copies ran while one was open for 1% of the time, Pallas kernels for 0%

profile of v7, /device:TPU:1, one launch (start us, length us, event | category | flops | bytes accessed | tf_op | source)
XLA Modules:
  0.0 93.8 jit_solution(2679358595323960701)
XLA Ops:
  0.6 16.1 %collective-permute-start = (f32[1,1760]{1,0:T(1,128)}, f32[1,1760]{1,0:T(1,128)S(1)}, u32[]{:S(2)}, u32[]{:S(2)}) collective-permute-start(f32[1,1760]{1,0:T(1,128)} %param.9), channel_id=1, source_target_pairs={{1,0},{2,1},{3,2},{4,3},{5,4},{6,5},{7,6},{8,7},{9,8},{10,9},{11,1... | collective-permute-start | bytes 21128 | tf_op jit(solution)/shard_map/ppermute | solution.py:300
  17.3 0.7 reduce
  18.1 0.1 reshape.24.block_ref
  18.2 0.0 collective-permute-done.rim_ref
  18.2 5.2 %step.1 = (bf16[176,512]{1,0:T(8,128)(2,1)}, f32[8,200,256]{2,1,0:T(8,128)S(1)}, f32[8,200,256]{2,1,0:T(8,128)S(1)}) custom-call(s32[1]{0:T(128)S(6)} %copy.12.length_ref, f32[176,10]{1,0:T(8,128)S(1)} %reshape.24.block_ref, f32[1,1760]{1,0:T(1,128)S(1)} %collective-permute-done.rim_ref, f32[10,512]{1,0:T(8,128)} %w0_hbm.1, f32[1,512]{1,0:T(1,128)} %bitcast.9, ...), custom_call_target="tpu_custom_call" | custom-call | tf_op jit(solution)/shard_map/step/pallas_call | solution.py:304
  23.5 1.9 %collective-permute-start.1 = (f32[8,200,256]{2,1,0:T(8,128)S(1)}, f32[8,200,256]{2,1,0:T(8,128)S(1)}, u32[]{:S(2)}, u32[]{:S(2)}) collective-permute-start(f32[8,200,256]{2,1,0:T(8,128)S(1)} %get-tuple-element.10), channel_id=1, source_target_pairs={{0,1},{1,0},{2,3},{3,2},{4,5},{5,4},{6,7},{7,6},{8,9},{9,8},{10,11... | collective-permute-start | bytes 4915208 | tf_op jit(solution)/shard_map/ppermute | solution.py:358
  25.4 3.5 %collective-permute-done.1 = f32[8,200,256]{2,1,0:T(8,128)S(1)} collective-permute-done((f32[8,200,256]{2,1,0:T(8,128)S(1)}, f32[8,200,256]{2,1,0:T(8,128)S(1)}, u32[]{:S(2)}, u32[]{:S(2)}) %collective-permute-start.1) | collective-permute-done | bytes 1638432 | tf_op jit(solution)/shard_map/ppermute | solution.py:358
  28.9 0.2 add.3
  29.1 26.9 %all_to_all.15.cube_ref = f32[8,200,256]{2,1,0:T(8,128)S(1)} all-to-all(f32[8,200,256]{2,1,0:T(8,128)S(1)} %add.3), channel_id=1, replica_groups={{0,2,16,18,64,66,80,82},{1,15,561,575,449,463,1009,1023},{5,3,565,563,4..., dimensions={0} | all-to-all | bytes 3276800 | tf_op jit(solution)/shard_map/all_to_all | solution.py:371
  56.0 0.1 cube_kernel.1
  56.1 17.2 %all_to_all.16.far_ref = f32[16,16,256]{2,1,0:T(8,128)S(1)} all-to-all(f32[16,16,256]{2,1,0:T(8,128)S(1)} %cube_kernel.1), channel_id=1, replica_groups=mesh['z2'=2,'y2'=2,'y1'=2,'y0'=2,'z1'=2,'z0'=2,'x2'=2,'x1'=2,'x0'=2,'cor..., dimensions={0} | all-to-all | bytes 524288 | tf_op jit(solution)/shard_map/all_to_all | solution.py:373
  73.3 19.8 %all_to_all.17.all_ref = f32[64,4,256]{2,1,0:T(4,128)S(1)} all-to-all(f32[64,4,256]{2,1,0:T(4,128)S(1)} %far_kernel.1), channel_id=1, replica_groups=mesh['z2'=2,'y2'=2,'y1'=2,'y0'=2,'z1'=2,'z0'=2,'x2'=2,'x1'=2,'x0'=2,'cor..., dimensions={0} | all-to-all | bytes 524288 | tf_op jit(solution)/shard_map/all_to_all | solution.py:375
  93.1 0.7 last_kernel.1
  (1 shorter events, 0.0 us)
Async XLA Ops:
  0.6 17.6 %collective-permute-start = (f32[1,1760]{1,0:T(1,128)}, f32[1,1760]{1,0:T(1,128)S(1)}, u32[]{:S(2)}, u32[]{:S(2)}) collective-permute-start(f32[1,1760]{1,0:T(1,128)} %param.9), channel_id=1, source_target_pairs={{1,0},{2,1},{3,2},{4,3},{5,4},{6,5},{7,6},{8,7},{9,8},{10,9},{11,1... | collective-permute-start | bytes 21128 | tf_op jit(solution)/shard_map/ppermute | solution.py:300
  23.5 5.4 %collective-permute-start.1 = (f32[8,200,256]{2,1,0:T(8,128)S(1)}, f32[8,200,256]{2,1,0:T(8,128)S(1)}, u32[]{:S(2)}, u32[]{:S(2)}) collective-permute-start(f32[8,200,256]{2,1,0:T(8,128)S(1)} %get-tuple-element.10), channel_id=1, source_target_pairs={{0,1},{1,0},{2,3},{3,2},{4,5},{5,4},{6,7},{7,6},{8,9},{9,8},{10,11... | collective-permute-start | bytes 4915208 | tf_op jit(solution)/shard_map/ppermute | solution.py:358

commit v8 on v7

--- a/solution.py
+++ b/solution.py
@@ -13,8 +13,8 @@
 AXES = ("z2", "y2", "y1", "y0", "z1", "z0", "x2", "x1", "x0", "core")
 DP, AUDIO = AXES[:4], AXES[4:]
 CUBE = ("y0", "z0", "x0")
-FAR = ("z2", "y2", "y1", "z1")
-LAST = ("core", "y0", "z0", "x0", "x2", "x1")
+FAR = ("z2", "y2", "y1", "z1", "x1")
+LAST = ("core", "y0", "z0", "x0", "x2")
 GROUP = 384
 EPS = 1e-05
 BF16, F32 = jnp.bfloat16, jnp.float32
@@ -36,7 +36,7 @@
 def row_order(place):
     chunk = (place * 171) >> 9
     row = place - 3 * chunk
-    for source, target in ((6, 5), (5, 3), (4, 0), (3, 6), (2, 4), (1, 2), (0, 1)):
+    for source, target in ((6, 5), (5, 3), (4, 0), (3, 6), (2, 4), (1, 1), (0, 2)):
         row = row + (((chunk >> source) & 1) << target) * 3
     return row
 
@@ -82,7 +82,7 @@
     gain1_hbm,
     shift1_hbm,
     cot_hbm,
-    feat_ref,
+    feat_hbm,
     keep_ref,
     send_ref,
     pre0_ref,
@@ -108,6 +108,7 @@
     gain1_ref,
     shift1_ref,
     cot_ref,
+    feat_ref,
     sems,
 ):
     arriving = []
@@ -184,6 +185,8 @@
         left, right = d[:, :half], d[:, half:]
         sides_ref[at : at + chunk, :half] = jnp.where(core == 0, right, left).astype(BF16)
         sides_ref[at : at + chunk, half:] = jnp.where(core == 0, left, right).astype(BF16)
+    leaving = pltpu.make_async_copy(feat_ref, feat_hbm, sems.at[7])
+    leaving.start()
     small_ref[12:13] = jnp.sum(sum_gain, 0, keepdims=True)
     small_ref[13:14] = jnp.sum(sum_shift, 0, keepdims=True)
     small_ref[14:16] = jnp.zeros((2, chans), F32)
@@ -239,30 +242,30 @@
             out_ref[cube, last : last + 1] = row[:, :half]
             out_ref[cube, last + 1 : last + 2] = row[:, half:]
             out_ref[cube, last + 2 :] = jnp.zeros((6, half), F32)
+    leaving.wait()
 
 
 def cube_kernel(cube_ref, out_ref, sum_ref):
     sum_ref[...] = jnp.sum(cube_ref[...], 0)
-    small = jnp.concatenate([sum_ref[192:194], jnp.zeros((2, sum_ref.shape[1]), F32)], 0)
-    for target in range(16):
-        out_ref[target, 0:12] = sum_ref[12 * target : 12 * target + 12]
-        out_ref[target, 12:16] = small
+    for target in range(32):
+        out_ref[target, 0:6] = sum_ref[6 * target : 6 * target + 6]
+        out_ref[target, 6:8] = sum_ref[192:194]
 
 
 def far_kernel(far_ref, out_ref, sum_ref):
     sum_ref[...] = jnp.sum(far_ref[...], 0)
-    small = sum_ref[12:14]
+    small = sum_ref[6:8]
     for core in range(2):
-        for place in range(4):
+        for place in range(2):
             at = 3 * place + core
             message = jnp.concatenate([small, sum_ref[at : at + 2]], 0)
             for cube in range(8):
-                out_ref[core * 32 + cube * 4 + place] = message
+                out_ref[core * 16 + cube * 2 + place] = message
 
 
 def last_kernel(all_ref, grad_ref, small_ref, sum_ref):
     half = all_ref.shape[2]
-    sum_ref[...] = jnp.sum(all_ref[...].reshape(16, 4, 4, half), 1)
+    sum_ref[...] = jnp.sum(all_ref[...].reshape(16, 2, 4, half), 1)
     core, cube = lax.axis_index("core"), lax.axis_index(CUBE)
     own = sum_ref[core * 8 + cube]
     other = sum_ref[(1 - core) * 8 + cube]
@@ -309,7 +312,7 @@
             shape((8, 200, half), F32),
         ),
         in_specs=[SMEM] + [VMEM] * 2 + [HBM] * 7,
-        out_specs=(VMEM,) * 3,
+        out_specs=(HBM, VMEM, VMEM),
         scratch_shapes=[
             pltpu.VMEM((rows, chans), F32),
             pltpu.VMEM((rows, chans), F32),
@@ -334,7 +337,8 @@
             pltpu.VMEM((1, chans), F32),
             pltpu.VMEM((1, chans), F32),
             pltpu.VMEM((frames, chans), BF16),
-            pltpu.SemaphoreType.DMA((7,)),
+            pltpu.VMEM((frames, chans), BF16),
+            pltpu.SemaphoreType.DMA((8,)),
         ],
         compiler_params=pltpu.CompilerParams(vmem_limit_bytes=32 << 20),
         name="step",
@@ -369,9 +373,9 @@
         )(value)
 
     mine = lax.all_to_all(mine, AXES, 0, 0, axis_index_groups=cubes(), tiled=True)
-    (mine,) = stage(cube_kernel, mine, [(16, 16, half)], (200, half))
+    (mine,) = stage(cube_kernel, mine, [(32, 8, half)], (200, half))
     mine = lax.all_to_all(mine, FAR, 0, 0, tiled=True)
-    (mine,) = stage(far_kernel, mine, [(64, 4, half)], (16, half))
+    (mine,) = stage(far_kernel, mine, [(32, 4, half)], (8, half))
     mine = lax.all_to_all(mine, LAST, 0, 0, tiled=True)
     conv1_grad, small_grads = stage(last_kernel, mine, [(3 * half,), (14, chans)], (16, 4, half))
     return (features[None], conv1_grad, small_grads)

time: 94.1 us -> 93.8 us (level)
    all_to_all x1, blocking collectives: 19.8 us -> 18.6 us  [shards(): mine = lax.all_to_all(mine, LAST, 0, 0, tiled=True)]
where the time goes in v8:
time: 93.8 us; the launch traced here: 93.5 us
  blocking collectives  63.5 us (68%)
  starting transfers between devices  18 us (19%)
  Pallas kernels  6.09 us (6%)
  waiting for transfers between devices  3.47 us (4%)
  between operations  1.33 us (1%)
    all_to_all x1, blocking collectives, shards(): lax.all_to_all(mine, AXES, 0, 0, axis_index_groups=cubes(), tiled=True)  26.9 us
    all_to_all x1, blocking collectives, shards(): mine = lax.all_to_all(mine, LAST, 0, 0, tiled=True)  18.6 us
    all_to_all x1, blocking collectives, shards(): mine = lax.all_to_all(mine, FAR, 0, 0, tiled=True)  18.1 us
    ppermute x1, starting transfers between devices, shards(): rim = lax.ppermute(waveform, AXES, back)  16.1 us
    pallas_call x1, Pallas kernels, shards(): pl.pallas_call(functools.partial(step_kernel, frames, chunk), out_shape=(...  5.24 us
    ppermute x1, waiting for transfers between devices, shards(): mine = keep + lax.ppermute(send, 'core', [(0, 1), (1, 0)])  3.47 us
    ppermute x1, starting transfers between devices, shards(): mine = keep + lax.ppermute(send, 'core', [(0, 1), (1, 0)])  1.92 us
  transfers between devices with their start and end apart: 2, of which 1 were waited for; matrix products, arithmetic and copies ran while one was open for 1% of the time, Pallas kernels for 0%

profile of v8, /device:TPU:1, one launch (start us, length us, event | category | flops | bytes accessed | tf_op | source)
XLA Modules:
  0.0 93.5 jit_solution(11867786885743124061)
XLA Ops:
  0.6 16.1 %collective-permute-start = (f32[1,1760]{1,0:T(1,128)}, f32[1,1760]{1,0:T(1,128)S(1)}, u32[]{:S(2)}, u32[]{:S(2)}) collective-permute-start(f32[1,1760]{1,0:T(1,128)} %param.9), channel_id=1, source_target_pairs={{1,0},{2,1},{3,2},{4,3},{5,4},{6,5},{7,6},{8,7},{9,8},{10,9},{11,1... | collective-permute-start | bytes 21128 | tf_op jit(solution)/shard_map/ppermute | solution.py:303
  17.3 0.7 reduce
  18.1 0.1 reshape.24.block_ref
  18.2 0.0 collective-permute-done.rim_ref
  18.2 5.2 %step.1 = (bf16[176,512]{1,0:T(8,128)(2,1)}, f32[8,200,256]{2,1,0:T(8,128)S(1)}, f32[8,200,256]{2,1,0:T(8,128)S(1)}) custom-call(s32[1]{0:T(128)S(6)} %copy.12.length_ref, f32[176,10]{1,0:T(8,128)S(1)} %reshape.24.block_ref, f32[1,1760]{1,0:T(1,128)S(1)} %collective-permute-done.rim_ref, f32[10,512]{1,0:T(8,128)} %w0_hbm.1, f32[1,512]{1,0:T(1,128)} %bitcast.9, ...), custom_call_target="tpu_custom_call" | custom-call | tf_op jit(solution)/shard_map/step/pallas_call | solution.py:307
  23.5 1.9 %collective-permute-start.1 = (f32[8,200,256]{2,1,0:T(8,128)S(1)}, f32[8,200,256]{2,1,0:T(8,128)S(1)}, u32[]{:S(2)}, u32[]{:S(2)}) collective-permute-start(f32[8,200,256]{2,1,0:T(8,128)S(1)} %get-tuple-element.10), channel_id=1, source_target_pairs={{0,1},{1,0},{2,3},{3,2},{4,5},{5,4},{6,7},{7,6},{8,9},{9,8},{10,11... | collective-permute-start | bytes 4915208 | tf_op jit(solution)/shard_map/ppermute | solution.py:362
  25.4 3.5 %collective-permute-done.1 = f32[8,200,256]{2,1,0:T(8,128)S(1)} collective-permute-done((f32[8,200,256]{2,1,0:T(8,128)S(1)}, f32[8,200,256]{2,1,0:T(8,128)S(1)}, u32[]{:S(2)}, u32[]{:S(2)}) %collective-permute-start.1) | collective-permute-done | bytes 1638432 | tf_op jit(solution)/shard_map/ppermute | solution.py:362
  28.9 0.2 add.3
  29.1 26.9 %all_to_all.15.cube_ref = f32[8,200,256]{2,1,0:T(8,128)S(1)} all-to-all(f32[8,200,256]{2,1,0:T(8,128)S(1)} %add.3), channel_id=1, replica_groups={{0,2,16,18,64,66,80,82},{1,15,561,575,449,463,1009,1023},{5,3,565,563,4..., dimensions={0} | all-to-all | bytes 3276800 | tf_op jit(solution)/shard_map/all_to_all | solution.py:375
  56.0 0.1 cube_kernel.1
  56.1 18.1 %all_to_all.16.far_ref = f32[32,8,256]{2,1,0:T(8,128)S(1)} all-to-all(f32[32,8,256]{2,1,0:T(8,128)S(1)} %cube_kernel.1), channel_id=1, replica_groups=mesh['z2'=2,'y2'=2,'y1'=2,'y0'=2,'z1'=2,'z0'=2,'x2'=2,'x1'=2,'x0'=2,'cor..., dimensions={0} | all-to-all | bytes 524288 | tf_op jit(solution)/shard_map/all_to_all | solution.py:377
  74.2 0.1 far_kernel.1
  74.3 18.6 %all_to_all.17.all_ref = f32[32,4,256]{2,1,0:T(4,128)S(1)} all-to-all(f32[32,4,256]{2,1,0:T(4,128)S(1)} %far_kernel.1), channel_id=1, replica_groups=mesh['z2'=2,'y2'=2,'y1'=2,'y0'=2,'z1'=2,'z0'=2,'x2'=2,'x1'=2,'x0'=2,'cor..., dimensions={0} | all-to-all | bytes 262144 | tf_op jit(solution)/shard_map/all_to_all | solution.py:379
  92.8 0.7 last_kernel.1
Async XLA Ops:
  0.6 17.6 %collective-permute-start = (f32[1,1760]{1,0:T(1,128)}, f32[1,1760]{1,0:T(1,128)S(1)}, u32[]{:S(2)}, u32[]{:S(2)}) collective-permute-start(f32[1,1760]{1,0:T(1,128)} %param.9), channel_id=1, source_target_pairs={{1,0},{2,1},{3,2},{4,3},{5,4},{6,5},{7,6},{8,7},{9,8},{10,9},{11,1... | collective-permute-start | bytes 21128 | tf_op jit(solution)/shard_map/ppermute | solution.py:303
  23.5 5.4 %collective-permute-start.1 = (f32[8,200,256]{2,1,0:T(8,128)S(1)}, f32[8,200,256]{2,1,0:T(8,128)S(1)}, u32[]{:S(2)}, u32[]{:S(2)}) collective-permute-start(f32[8,200,256]{2,1,0:T(8,128)S(1)} %get-tuple-element.10), channel_id=1, source_target_pairs={{0,1},{1,0},{2,3},{3,2},{4,5},{5,4},{6,7},{7,6},{8,9},{9,8},{10,11... | collective-permute-start | bytes 4915208 | tf_op jit(solution)/shard_map/ppermute | solution.py:362

commit v9 on v8

--- a/solution.py
+++ b/solution.py
@@ -159,6 +159,14 @@
     pre1_ref[...] = jnp.dot(patch_ref[...], w1_ref[...], preferred_element_type=F32)
     for copy in arriving[4:]:
         copy.wait()
+    source = lax.broadcasted_iota(jnp.int32, (GROUP, GROUP), 1)
+    order = row_order(lax.broadcasted_iota(jnp.int32, (GROUP, 1), 0))
+    place = (source == order).astype(F32).astype(BF16)
+    columns = []
+    for group in range(3 * chans // GROUP):
+        lanes = patch_ref[:, group * GROUP : (group + 1) * GROUP]
+        turned = lax.dot_general(place, lanes, (((1,), (1,)), ((), ())), preferred_element_type=F32)
+        columns.append(turned.astype(BF16))
     gain1 = jnp.broadcast_to(gain1_ref[...], (chunk, chans))
     shift1 = jnp.broadcast_to(shift1_ref[...], (chunk, chans))
     sum_gain = jnp.zeros((chunk, chans), F32)
@@ -191,18 +199,16 @@
     small_ref[13:14] = jnp.sum(sum_shift, 0, keepdims=True)
     small_ref[14:16] = jnp.zeros((2, chans), F32)
 
-    source = lax.broadcasted_iota(jnp.int32, (GROUP, GROUP), 0)
-    order = row_order(lax.broadcasted_iota(jnp.int32, (1, GROUP), 1))
-    place = (source == order).astype(F32).astype(BF16)
-    over_rows = (((0,), (0,)), ((), ()))
     part = GROUP // 8
-    for group in range(3 * chans // GROUP):
-        lanes = jnp.dot(patch_ref[:, group * GROUP : (group + 1) * GROUP], place, preferred_element_type=F32).astype(BF16)
-        grad = lax.dot_general(lanes, sides_ref[...], over_rows, preferred_element_type=F32)
+
+    def second_gradient(group):
+        grad = jnp.dot(columns[group], sides_ref[...], preferred_element_type=F32)
         for cube in range(8):
             block = grad[cube * part : (cube + 1) * part]
             send_ref[cube, group * part : (group + 1) * part] = block[:, :half]
             keep_ref[cube, group * part : (group + 1) * part] = block[:, half:]
+
+    over_rows = (((0,), (0,)), ((), ()))
 
     def spread(tap):
         return lax.dot_general(
@@ -219,6 +225,8 @@
     sum_gain = jnp.zeros((chunk, chans), F32)
     sum_shift = jnp.zeros((chunk, chans), F32)
     for at in range(0, rows, chunk):
+        if at % (5 * chunk) == 0 and at // (5 * chunk) < len(columns):
+            second_gradient(at // (5 * chunk))
         xhat = xhat_ref[at : at + chunk]
         dv = dact_ref[at : at + chunk] * slope_ref[at : at + chunk]
         sum_gain = sum_gain + dv * xhat

time: 93.8 us -> 93 us (level)
  no operation moved by 1% of the time
where the time goes in v9:
time: 93 us; the launch traced here: 92.6 us
  blocking collectives  63.5 us (68%)
  starting transfers between devices  18 us (19%)
  Pallas kernels  5.25 us (6%)
  waiting for transfers between devices  3.47 us (4%)
  between operations  1.33 us (1%)
  other arithmetic  0.93 us (1%)
    all_to_all x1, blocking collectives, shards(): lax.all_to_all(mine, AXES, 0, 0, axis_index_groups=cubes(), tiled=True)  26.9 us
    all_to_all x1, blocking collectives, shards(): mine = lax.all_to_all(mine, LAST, 0, 0, tiled=True)  18.6 us
    all_to_all x1, blocking collectives, shards(): mine = lax.all_to_all(mine, FAR, 0, 0, tiled=True)  18.1 us
    ppermute x1, starting transfers between devices, shards(): rim = lax.ppermute(waveform, AXES, back)  16.1 us
    pallas_call x1, Pallas kernels, shards(): pl.pallas_call(functools.partial(step_kernel, frames, chunk), out_shape=(...  4.4 us
    ppermute x1, waiting for transfers between devices, shards(): mine = keep + lax.ppermute(send, 'core', [(0, 1), (1, 0)])  3.47 us
    ppermute x1, starting transfers between devices, shards(): mine = keep + lax.ppermute(send, 'core', [(0, 1), (1, 0)])  1.92 us
  transfers between devices with their start and end apart: 2, of which 1 were waited for; matrix products, arithmetic and copies ran while one was open for 1% of the time, Pallas kernels for 0%

profile of v9, /device:TPU:1, one launch (start us, length us, event | category | flops | bytes accessed | tf_op | source)
XLA Modules:
  0.0 92.6 jit_solution(1549035118908948371)
XLA Ops:
  0.6 16.1 %collective-permute-start = (f32[1,1760]{1,0:T(1,128)}, f32[1,1760]{1,0:T(1,128)S(1)}, u32[]{:S(2)}, u32[]{:S(2)}) collective-permute-start(f32[1,1760]{1,0:T(1,128)} %param.9), channel_id=1, source_target_pairs={{1,0},{2,1},{3,2},{4,3},{5,4},{6,5},{7,6},{8,7},{9,8},{10,9},{11,1... | collective-permute-start | bytes 21128 | tf_op jit(solution)/shard_map/ppermute | solution.py:311
  17.3 0.7 reduce
  18.1 0.1 reshape.24.block_ref
  18.2 0.0 collective-permute-done.rim_ref
  18.2 4.4 %step.1 = (bf16[176,512]{1,0:T(8,128)(2,1)}, f32[8,200,256]{2,1,0:T(8,128)S(1)}, f32[8,200,256]{2,1,0:T(8,128)S(1)}) custom-call(s32[1]{0:T(128)S(6)} %copy.12.length_ref, f32[176,10]{1,0:T(8,128)S(1)} %reshape.24.block_ref, f32[1,1760]{1,0:T(1,128)S(1)} %collective-permute-done.rim_ref, f32[10,512]{1,0:T(8,128)} %w0_hbm.1, f32[1,512]{1,0:T(1,128)} %bitcast.9, ...), custom_call_target="tpu_custom_call" | custom-call | tf_op jit(solution)/shard_map/step/pallas_call | solution.py:315
  22.6 1.9 %collective-permute-start.1 = (f32[8,200,256]{2,1,0:T(8,128)S(1)}, f32[8,200,256]{2,1,0:T(8,128)S(1)}, u32[]{:S(2)}, u32[]{:S(2)}) collective-permute-start(f32[8,200,256]{2,1,0:T(8,128)S(1)} %get-tuple-element.10), channel_id=1, source_target_pairs={{0,1},{1,0},{2,3},{3,2},{4,5},{5,4},{6,7},{7,6},{8,9},{9,8},{10,11... | collective-permute-start | bytes 4915208 | tf_op jit(solution)/shard_map/ppermute | solution.py:370
  24.6 3.5 %collective-permute-done.1 = f32[8,200,256]{2,1,0:T(8,128)S(1)} collective-permute-done((f32[8,200,256]{2,1,0:T(8,128)S(1)}, f32[8,200,256]{2,1,0:T(8,128)S(1)}, u32[]{:S(2)}, u32[]{:S(2)}) %collective-permute-start.1) | collective-permute-done | bytes 1638432 | tf_op jit(solution)/shard_map/ppermute | solution.py:370
  28.0 0.2 add.3
  28.2 26.9 %all_to_all.15.cube_ref = f32[8,200,256]{2,1,0:T(8,128)S(1)} all-to-all(f32[8,200,256]{2,1,0:T(8,128)S(1)} %add.3), channel_id=1, replica_groups={{0,2,16,18,64,66,80,82},{1,15,561,575,449,463,1009,1023},{5,3,565,563,4..., dimensions={0} | all-to-all | bytes 3276800 | tf_op jit(solution)/shard_map/all_to_all | solution.py:383
  55.1 0.1 cube_kernel.1
  55.3 18.1 %all_to_all.16.far_ref = f32[32,8,256]{2,1,0:T(8,128)S(1)} all-to-all(f32[32,8,256]{2,1,0:T(8,128)S(1)} %cube_kernel.1), channel_id=1, replica_groups=mesh['z2'=2,'y2'=2,'y1'=2,'y0'=2,'z1'=2,'z0'=2,'x2'=2,'x1'=2,'x0'=2,'cor..., dimensions={0} | all-to-all | bytes 524288 | tf_op jit(solution)/shard_map/all_to_all | solution.py:385
  73.4 0.1 far_kernel.1
  73.4 18.6 %all_to_all.17.all_ref = f32[32,4,256]{2,1,0:T(4,128)S(1)} all-to-all(f32[32,4,256]{2,1,0:T(4,128)S(1)} %far_kernel.1), channel_id=1, replica_groups=mesh['z2'=2,'y2'=2,'y1'=2,'y0'=2,'z1'=2,'z0'=2,'x2'=2,'x1'=2,'x0'=2,'cor..., dimensions={0} | all-to-all | bytes 262144 | tf_op jit(solution)/shard_map/all_to_all | solution.py:387
  92.0 0.7 last_kernel.1
Async XLA Ops:
  0.6 17.6 %collective-permute-start = (f32[1,1760]{1,0:T(1,128)}, f32[1,1760]{1,0:T(1,128)S(1)}, u32[]{:S(2)}, u32[]{:S(2)}) collective-permute-start(f32[1,1760]{1,0:T(1,128)} %param.9), channel_id=1, source_target_pairs={{1,0},{2,1},{3,2},{4,3},{5,4},{6,5},{7,6},{8,7},{9,8},{10,9},{11,1... | collective-permute-start | bytes 21128 | tf_op jit(solution)/shard_map/ppermute | solution.py:311
  22.6 5.4 %collective-permute-start.1 = (f32[8,200,256]{2,1,0:T(8,128)S(1)}, f32[8,200,256]{2,1,0:T(8,128)S(1)}, u32[]{:S(2)}, u32[]{:S(2)}) collective-permute-start(f32[8,200,256]{2,1,0:T(8,128)S(1)} %get-tuple-element.10), channel_id=1, source_target_pairs={{0,1},{1,0},{2,3},{3,2},{4,5},{5,4},{6,7},{7,6},{8,9},{9,8},{10,11... | collective-permute-start | bytes 4915208 | tf_op jit(solution)/shard_map/ppermute | solution.py:370

commit v10 on v9

--- a/solution.py
+++ b/solution.py
@@ -13,8 +13,8 @@
 AXES = ("z2", "y2", "y1", "y0", "z1", "z0", "x2", "x1", "x0", "core")
 DP, AUDIO = AXES[:4], AXES[4:]
 CUBE = ("y0", "z0", "x0")
-FAR = ("z2", "y2", "y1", "z1", "x1")
-LAST = ("core", "y0", "z0", "x0", "x2")
+FAR = ("y2", "y1", "z1", "x2", "x1")
+LAST = ("core", "y0", "z0", "x0", "z2")
 GROUP = 384
 EPS = 1e-05
 BF16, F32 = jnp.bfloat16, jnp.float32
@@ -36,7 +36,7 @@
 def row_order(place):
     chunk = (place * 171) >> 9
     row = place - 3 * chunk
-    for source, target in ((6, 5), (5, 3), (4, 0), (3, 6), (2, 4), (1, 1), (0, 2)):
+    for source, target in ((6, 5), (5, 3), (4, 0), (3, 6), (2, 4), (1, 2), (0, 1)):
         row = row + (((chunk >> source) & 1) << target) * 3
     return row
 
@@ -256,7 +256,9 @@
 def cube_kernel(cube_ref, out_ref, sum_ref):
     sum_ref[...] = jnp.sum(cube_ref[...], 0)
     for target in range(32):
-        out_ref[target, 0:6] = sum_ref[6 * target : 6 * target + 6]
+        for place in range(2):
+            at = place * 96 + 3 * target
+            out_ref[target, 3 * place : 3 * place + 3] = sum_ref[at : at + 3]
         out_ref[target, 6:8] = sum_ref[192:194]
 
 

time: 93 us -> 92.8 us (level)
    all_to_all x1, blocking collectives: 18.6 us -> 13.9 us  [shards(): mine = lax.all_to_all(mine, LAST, 0, 0, tiled=True)]
    all_to_all x1, blocking collectives: 18.1 us -> 22.5 us  [shards(): mine = lax.all_to_all(mine, FAR, 0, 0, tiled=True)]
where the time goes in v10:
time: 92.8 us; the launch traced here: 92.5 us
  blocking collectives  63.4 us (68%)
  starting transfers between devices  18 us (19%)
  Pallas kernels  5.28 us (6%)
  waiting for transfers between devices  3.47 us (4%)
  between operations  1.33 us (1%)
  other arithmetic  0.93 us (1%)
    all_to_all x1, blocking collectives, shards(): lax.all_to_all(mine, AXES, 0, 0, axis_index_groups=cubes(), tiled=True)  26.9 us
    all_to_all x1, blocking collectives, shards(): mine = lax.all_to_all(mine, FAR, 0, 0, tiled=True)  22.5 us
    ppermute x1, starting transfers between devices, shards(): rim = lax.ppermute(waveform, AXES, back)  16.1 us
    all_to_all x1, blocking collectives, shards(): mine = lax.all_to_all(mine, LAST, 0, 0, tiled=True)  13.9 us
    pallas_call x1, Pallas kernels, shards(): pl.pallas_call(functools.partial(step_kernel, frames, chunk), out_shape=(...  4.4 us
    ppermute x1, waiting for transfers between devices, shards(): mine = keep + lax.ppermute(send, 'core', [(0, 1), (1, 0)])  3.47 us
    ppermute x1, starting transfers between devices, shards(): mine = keep + lax.ppermute(send, 'core', [(0, 1), (1, 0)])  1.92 us
  transfers between devices with their start and end apart: 2, of which 1 were waited for; matrix products, arithmetic and copies ran while one was open for 1% of the time, Pallas kernels for 0%

profile of v10, /device:TPU:1, one launch (start us, length us, event | category | flops | bytes accessed | tf_op | source)
XLA Modules:
  0.0 92.5 jit_solution(4531269746198954318)
XLA Ops:
  0.6 16.1 %collective-permute-start = (f32[1,1760]{1,0:T(1,128)}, f32[1,1760]{1,0:T(1,128)S(1)}, u32[]{:S(2)}, u32[]{:S(2)}) collective-permute-start(f32[1,1760]{1,0:T(1,128)} %param.9), channel_id=1, source_target_pairs={{1,0},{2,1},{3,2},{4,3},{5,4},{6,5},{7,6},{8,7},{9,8},{10,9},{11,1... | collective-permute-start | bytes 21128 | tf_op jit(solution)/shard_map/ppermute | solution.py:313
  17.3 0.7 reduce
  18.1 0.1 reshape.24.block_ref
  18.2 0.0 collective-permute-done.rim_ref
  18.2 4.4 %step.1 = (bf16[176,512]{1,0:T(8,128)(2,1)}, f32[8,200,256]{2,1,0:T(8,128)S(1)}, f32[8,200,256]{2,1,0:T(8,128)S(1)}) custom-call(s32[1]{0:T(128)S(6)} %copy.12.length_ref, f32[176,10]{1,0:T(8,128)S(1)} %reshape.24.block_ref, f32[1,1760]{1,0:T(1,128)S(1)} %collective-permute-done.rim_ref, f32[10,512]{1,0:T(8,128)} %w0_hbm.1, f32[1,512]{1,0:T(1,128)} %bitcast.9, ...), custom_call_target="tpu_custom_call" | custom-call | tf_op jit(solution)/shard_map/step/pallas_call | solution.py:317
  22.6 1.9 %collective-permute-start.1 = (f32[8,200,256]{2,1,0:T(8,128)S(1)}, f32[8,200,256]{2,1,0:T(8,128)S(1)}, u32[]{:S(2)}, u32[]{:S(2)}) collective-permute-start(f32[8,200,256]{2,1,0:T(8,128)S(1)} %get-tuple-element.10), channel_id=1, source_target_pairs={{0,1},{1,0},{2,3},{3,2},{4,5},{5,4},{6,7},{7,6},{8,9},{9,8},{10,11... | collective-permute-start | bytes 4915208 | tf_op jit(solution)/shard_map/ppermute | solution.py:372
  24.6 3.5 %collective-permute-done.1 = f32[8,200,256]{2,1,0:T(8,128)S(1)} collective-permute-done((f32[8,200,256]{2,1,0:T(8,128)S(1)}, f32[8,200,256]{2,1,0:T(8,128)S(1)}, u32[]{:S(2)}, u32[]{:S(2)}) %collective-permute-start.1) | collective-permute-done | bytes 1638432 | tf_op jit(solution)/shard_map/ppermute | solution.py:372
  28.0 0.2 add.3
  28.2 26.9 %all_to_all.15.cube_ref = f32[8,200,256]{2,1,0:T(8,128)S(1)} all-to-all(f32[8,200,256]{2,1,0:T(8,128)S(1)} %add.3), channel_id=1, replica_groups={{0,2,16,18,64,66,80,82},{1,15,561,575,449,463,1009,1023},{5,3,565,563,4..., dimensions={0} | all-to-all | bytes 3276800 | tf_op jit(solution)/shard_map/all_to_all | solution.py:385
  55.1 0.2 cube_kernel.1
  55.3 22.5 %all_to_all.16.far_ref = f32[32,8,256]{2,1,0:T(8,128)S(1)} all-to-all(f32[32,8,256]{2,1,0:T(8,128)S(1)} %cube_kernel.1), channel_id=1, replica_groups=mesh['z2'=2,'y2'=2,'y1'=2,'y0'=2,'z1'=2,'z0'=2,'x2'=2,'x1'=2,'x0'=2,'cor..., dimensions={0} | all-to-all | bytes 524288 | tf_op jit(solution)/shard_map/all_to_all | solution.py:387
  77.8 0.1 far_kernel.1
  77.9 13.9 %all_to_all.17.all_ref = f32[32,4,256]{2,1,0:T(4,128)S(1)} all-to-all(f32[32,4,256]{2,1,0:T(4,128)S(1)} %far_kernel.1), channel_id=1, replica_groups=mesh['z2'=2,'y2'=2,'y1'=2,'y0'=2,'z1'=2,'z0'=2,'x2'=2,'x1'=2,'x0'=2,'cor..., dimensions={0} | all-to-all | bytes 262144 | tf_op jit(solution)/shard_map/all_to_all | solution.py:389
  91.8 0.7 last_kernel.1
Async XLA Ops:
  0.6 17.6 %collective-permute-start = (f32[1,1760]{1,0:T(1,128)}, f32[1,1760]{1,0:T(1,128)S(1)}, u32[]{:S(2)}, u32[]{:S(2)}) collective-permute-start(f32[1,1760]{1,0:T(1,128)} %param.9), channel_id=1, source_target_pairs={{1,0},{2,1},{3,2},{4,3},{5,4},{6,5},{7,6},{8,7},{9,8},{10,9},{11,1... | collective-permute-start | bytes 21128 | tf_op jit(solution)/shard_map/ppermute | solution.py:313
  22.6 5.4 %collective-permute-start.1 = (f32[8,200,256]{2,1,0:T(8,128)S(1)}, f32[8,200,256]{2,1,0:T(8,128)S(1)}, u32[]{:S(2)}, u32[]{:S(2)}) collective-permute-start(f32[8,200,256]{2,1,0:T(8,128)S(1)} %get-tuple-element.10), channel_id=1, source_target_pairs={{0,1},{1,0},{2,3},{3,2},{4,5},{5,4},{6,7},{7,6},{8,9},{9,8},{10,11... | collective-permute-start | bytes 4915208 | tf_op jit(solution)/shard_map/ppermute | solution.py:372

commit v11 on v10

--- a/solution.py
+++ b/solution.py
@@ -163,15 +163,19 @@
     order = row_order(lax.broadcasted_iota(jnp.int32, (GROUP, 1), 0))
     place = (source == order).astype(F32).astype(BF16)
     columns = []
-    for group in range(3 * chans // GROUP):
-        lanes = patch_ref[:, group * GROUP : (group + 1) * GROUP]
+
+    def turn():
+        lanes = patch_ref[:, len(columns) * GROUP : (len(columns) + 1) * GROUP]
         turned = lax.dot_general(place, lanes, (((1,), (1,)), ((), ())), preferred_element_type=F32)
         columns.append(turned.astype(BF16))
+
     gain1 = jnp.broadcast_to(gain1_ref[...], (chunk, chans))
     shift1 = jnp.broadcast_to(shift1_ref[...], (chunk, chans))
     sum_gain = jnp.zeros((chunk, chans), F32)
     sum_shift = jnp.zeros((chunk, chans), F32)
     for at in range(0, frames, chunk):
+        if at % (3 * chunk) == 0:
+            turn()
         pre = pre1_ref[at : at + chunk]
         centred = pre - jnp.mean(pre, -1, keepdims=True)
         rstd = lax.rsqrt(jnp.mean(centred * centred, -1, keepdims=True) + EPS)

time: 92.8 us -> 92.8 us (level)
  no operation moved by 1% of the time
where the time goes in v11:
time: 92.8 us; the launch traced here: 92.5 us
  blocking collectives  63.4 us (68%)
  starting transfers between devices  18 us (19%)
  Pallas kernels  5.28 us (6%)
  waiting for transfers between devices  3.47 us (4%)
  between operations  1.33 us (1%)
  other arithmetic  0.93 us (1%)
    all_to_all x1, blocking collectives, shards(): lax.all_to_all(mine, AXES, 0, 0, axis_index_groups=cubes(), tiled=True)  26.9 us
    all_to_all x1, blocking collectives, shards(): mine = lax.all_to_all(mine, FAR, 0, 0, tiled=True)  22.5 us
    ppermute x1, starting transfers between devices, shards(): rim = lax.ppermute(waveform, AXES, back)  16.1 us
    all_to_all x1, blocking collectives, shards(): mine = lax.all_to_all(mine, LAST, 0, 0, tiled=True)  13.9 us
    pallas_call x1, Pallas kernels, shards(): pl.pallas_call(functools.partial(step_kernel, frames, chunk), out_shape=(...  4.4 us
    ppermute x1, waiting for transfers between devices, shards(): mine = keep + lax.ppermute(send, 'core', [(0, 1), (1, 0)])  3.47 us
    ppermute x1, starting transfers between devices, shards(): mine = keep + lax.ppermute(send, 'core', [(0, 1), (1, 0)])  1.92 us
  transfers between devices with their start and end apart: 2, of which 1 were waited for; matrix products, arithmetic and copies ran while one was open for 1% of the time, Pallas kernels for 0%

profile of v11, /device:TPU:1, one launch (start us, length us, event | category | flops | bytes accessed | tf_op | source)
XLA Modules:
  0.0 92.5 jit_solution(6968558984316224114)
XLA Ops:
  0.6 16.1 %collective-permute-start = (f32[1,1760]{1,0:T(1,128)}, f32[1,1760]{1,0:T(1,128)S(1)}, u32[]{:S(2)}, u32[]{:S(2)}) collective-permute-start(f32[1,1760]{1,0:T(1,128)} %param.9), channel_id=1, source_target_pairs={{1,0},{2,1},{3,2},{4,3},{5,4},{6,5},{7,6},{8,7},{9,8},{10,9},{11,1... | collective-permute-start | bytes 21128 | tf_op jit(solution)/shard_map/ppermute | solution.py:317
  17.3 0.7 reduce
  18.1 0.1 reshape.24.block_ref
  18.2 0.0 collective-permute-done.rim_ref
  18.2 4.4 %step.1 = (bf16[176,512]{1,0:T(8,128)(2,1)}, f32[8,200,256]{2,1,0:T(8,128)S(1)}, f32[8,200,256]{2,1,0:T(8,128)S(1)}) custom-call(s32[1]{0:T(128)S(6)} %copy.12.length_ref, f32[176,10]{1,0:T(8,128)S(1)} %reshape.24.block_ref, f32[1,1760]{1,0:T(1,128)S(1)} %collective-permute-done.rim_ref, f32[10,512]{1,0:T(8,128)} %w0_hbm.1, f32[1,512]{1,0:T(1,128)} %bitcast.9, ...), custom_call_target="tpu_custom_call" | custom-call | tf_op jit(solution)/shard_map/step/pallas_call | solution.py:321
  22.6 1.9 %collective-permute-start.1 = (f32[8,200,256]{2,1,0:T(8,128)S(1)}, f32[8,200,256]{2,1,0:T(8,128)S(1)}, u32[]{:S(2)}, u32[]{:S(2)}) collective-permute-start(f32[8,200,256]{2,1,0:T(8,128)S(1)} %get-tuple-element.10), channel_id=1, source_target_pairs={{0,1},{1,0},{2,3},{3,2},{4,5},{5,4},{6,7},{7,6},{8,9},{9,8},{10,11... | collective-permute-start | bytes 4915208 | tf_op jit(solution)/shard_map/ppermute | solution.py:376
  24.6 3.5 %collective-permute-done.1 = f32[8,200,256]{2,1,0:T(8,128)S(1)} collective-permute-done((f32[8,200,256]{2,1,0:T(8,128)S(1)}, f32[8,200,256]{2,1,0:T(8,128)S(1)}, u32[]{:S(2)}, u32[]{:S(2)}) %collective-permute-start.1) | collective-permute-done | bytes 1638432 | tf_op jit(solution)/shard_map/ppermute | solution.py:376
  28.0 0.2 add.3
  28.2 26.9 %all_to_all.15.cube_ref = f32[8,200,256]{2,1,0:T(8,128)S(1)} all-to-all(f32[8,200,256]{2,1,0:T(8,128)S(1)} %add.3), channel_id=1, replica_groups={{0,2,16,18,64,66,80,82},{1,15,561,575,449,463,1009,1023},{5,3,565,563,4..., dimensions={0} | all-to-all | bytes 3276800 | tf_op jit(solution)/shard_map/all_to_all | solution.py:389
  55.1 0.2 cube_kernel.1
  55.3 22.5 %all_to_all.16.far_ref = f32[32,8,256]{2,1,0:T(8,128)S(1)} all-to-all(f32[32,8,256]{2,1,0:T(8,128)S(1)} %cube_kernel.1), channel_id=1, replica_groups=mesh['z2'=2,'y2'=2,'y1'=2,'y0'=2,'z1'=2,'z0'=2,'x2'=2,'x1'=2,'x0'=2,'cor..., dimensions={0} | all-to-all | bytes 524288 | tf_op jit(solution)/shard_map/all_to_all | solution.py:391
  77.8 0.1 far_kernel.1
  77.9 13.9 %all_to_all.17.all_ref = f32[32,4,256]{2,1,0:T(4,128)S(1)} all-to-all(f32[32,4,256]{2,1,0:T(4,128)S(1)} %far_kernel.1), channel_id=1, replica_groups=mesh['z2'=2,'y2'=2,'y1'=2,'y0'=2,'z1'=2,'z0'=2,'x2'=2,'x1'=2,'x0'=2,'cor..., dimensions={0} | all-to-all | bytes 262144 | tf_op jit(solution)/shard_map/all_to_all | solution.py:393
  91.8 0.7 last_kernel.1
Async XLA Ops:
  0.6 17.6 %collective-permute-start = (f32[1,1760]{1,0:T(1,128)}, f32[1,1760]{1,0:T(1,128)S(1)}, u32[]{:S(2)}, u32[]{:S(2)}) collective-permute-start(f32[1,1760]{1,0:T(1,128)} %param.9), channel_id=1, source_target_pairs={{1,0},{2,1},{3,2},{4,3},{5,4},{6,5},{7,6},{8,7},{9,8},{10,9},{11,1... | collective-permute-start | bytes 21128 | tf_op jit(solution)/shard_map/ppermute | solution.py:317
  22.6 5.4 %collective-permute-start.1 = (f32[8,200,256]{2,1,0:T(8,128)S(1)}, f32[8,200,256]{2,1,0:T(8,128)S(1)}, u32[]{:S(2)}, u32[]{:S(2)}) collective-permute-start(f32[8,200,256]{2,1,0:T(8,128)S(1)} %get-tuple-element.10), channel_id=1, source_target_pairs={{0,1},{1,0},{2,3},{3,2},{4,5},{5,4},{6,7},{7,6},{8,9},{9,8},{10,11... | collective-permute-start | bytes 4915208 | tf_op jit(solution)/shard_map/ppermute | solution.py:376
